TPU v7x, 32 devices: a whole 2x2x4 slice. The times are simulated.
32 devices in a mesh: grp: 4 (over y, x), en: 8 (over z, core).
Axes of the slice: x: 2, y: 2, z: 4, core: 2. Of those that a mesh axis runs over, the one named last changes fastest.
Arguments:
- lesser: float32 [2, 512, 4096], P(None, 'grp', 'en'), may hold values from -6 to 6
- greater: float32 [2, 512, 4096], P(None, 'grp', 'en'), may hold values from -6 to 6
- mirror: int32 [512], P('grp'), may hold values from 0 to 511, as said below
Outputs:
- polar: float32 [2, 512, 4096], P(None, 'grp', 'en')
Inputs may be any that keep to these rules, and one draw needn't show every extreme that they name: mirror is an involution without fixed points; for every entry p, mirror[p] // 16 = (p // 16 + 512 // 32) mod (32), so the mirrored entry lies in the aligned block of 16 entries 512 / 2 entries away.
All inputs are finite; a program needn't handle non-finite values.
Results may differ from a plain program's by a relative error of at most 0.000098.
Values sent between devices are 32-bit elements; how exact they have to be, the bound alone decides.
No kernel may reach another device: no remote copies, remote signals or barrier semaphores. Data moves between devices by JAX's collectives and lax.ppermute only.
A program may use at most 64 MiB of HBM per device.

v0:
```python
import functools
import math

import jax
import jax.numpy as jnp
import numpy as np
from jax import lax
from jax.experimental import pallas as pl
from jax.experimental.pallas import tpu as pltpu
from jax.sharding import Mesh
from jax.sharding import PartitionSpec as P

LANES = 128
SUBLANES = 8


def dft_block(scale):
    turn = 2.0 * math.pi / LANES * (np.outer(np.arange(LANES), np.arange(LANES)) % LANES)
    cos, sin = np.cos(turn), np.sin(turn)
    full = (np.block([[cos, -sin], [sin, cos]]) * scale).astype(np.float32)
    high = full.astype(jnp.bfloat16)
    low = (full - high.astype(np.float32)).astype(jnp.bfloat16)
    return np.stack([high, low])


def twiddles(points):
    length = points * LANES
    turn = 2.0 * math.pi / length * (np.outer(np.arange(points), np.arange(LANES)) % length)
    return np.stack([np.cos(turn), -np.sin(turn)]).astype(np.float32)


def times_root(value, numerator, denominator):
    re, im = value
    eighths = 8 * numerator / denominator % 8
    if eighths == 0:
        return re, im
    if eighths == 2:
        return im, -re
    if eighths == 4:
        return -re, -im
    if eighths == 6:
        return -im, re
    half = math.sqrt(0.5)
    if eighths == 1:
        return (re + im) * half, (im - re) * half
    if eighths == 3:
        return (im - re) * half, -(re + im) * half
    turn = 2.0 * math.pi * numerator / denominator
    cos, sin = math.cos(turn), math.sin(turn)
    return re * cos + im * sin, im * cos - re * sin


def add(a, b):
    return a[0] + b[0], a[1] + b[1]


def sub(a, b):
    return a[0] - b[0], a[1] - b[1]


def small_dft(values):
    count = len(values)
    if count == 1:
        return values
    even, odd = small_dft(values[0::2]), small_dft(values[1::2])
    odd = [times_root(v, k, count) for k, v in enumerate(odd)]
    return [add(e, o) for e, o in zip(even, odd)] + [sub(e, o) for e, o in zip(even, odd)]


def long_dft(load, keep, points):
    first = min(8, points)
    second = points // first
    for s in range(second):
        for k, value in enumerate(small_dft([load(e * second + s) for e in range(first)])):
            keep[k * second + s, 0], keep[k * second + s, 1] = times_root(value, s * k, points)
    for k in range(first):
        group = [(keep[k * second + s, 0], keep[k * second + s, 1]) for s in range(second)]
        for j, value in enumerate(small_dft(group)):
            yield k + first * j, value


def split_store(ref, row, rows, re, im):
    for place, part in enumerate((re, im)):
        high = part.astype(jnp.bfloat16)
        low = (part - high.astype(jnp.float32)).astype(jnp.bfloat16)
        ref[0, pl.ds(row, rows), place * LANES : (place + 1) * LANES] = high
        ref[1, pl.ds(row, rows), place * LANES : (place + 1) * LANES] = low


def dot(left, right):
    return jnp.dot(left, right, preferred_element_type=jnp.float32)


def lane_dft(halves, table):
    high, low = halves[0], halves[1]
    return dot(high, table[0]) + dot(low, table[0]) + dot(high, table[1])


def times_twist(twist, k, value):
    re, im = value
    cos, sin = twist[0, pl.ds(k, 1), :], twist[1, pl.ds(k, 1), :]
    return re * cos - im * sin, re * sin + im * cos


def pack_kernel(units, alone, mirror, lesser, greater, mine, give, *refs):
    *single, places, held, moved_rows, sems, block_sems = refs
    _, count, tiles, sub, local_len = lesser.shape
    rows = tiles * sub
    me = lax.axis_index("en")
    loads = [pltpu.make_async_copy(mirror, places, sems.at[0])]
    loads += [pltpu.make_async_copy(greater.at[p], held.at[p], sems.at[1 + p]) for p in range(2)]
    offers = [(mine.at[i], *unit, 0) for i, unit in enumerate(units)]
    offers += [(give.at[i], *unit, 1) for i, unit in enumerate(units)]
    offers += [(ref, *one) for ref, one in zip(single, alone)]
    blocks = [
        pltpu.make_async_copy(lesser.at[:, me ^ (2 * chip + core), chunk], ref, block_sems.at[i])
        for i, (ref, chunk, (half, chip), core) in enumerate(offers)
        if not half
    ]
    for copy in loads + blocks:
        copy.start()
    loads[0].wait()
    lane = lax.broadcasted_iota(jnp.int32, (rows, count * rows), 1)
    line = lax.broadcasted_iota(jnp.int32, (rows, count * rows), 0)
    goal = jnp.broadcast_to(places[...], (rows, count * rows)) % rows
    source = jnp.where(goal == line, (lane % rows).astype(jnp.float32), 0.0)
    orders = [
        jnp.sum(jnp.where(lane // rows == to, source, 0.0), axis=1, keepdims=True).astype(jnp.int32)
        for to in range(count)
    ]
    for part in range(2):
        loads[1 + part].wait()
        for to in range(count):
            order = jnp.broadcast_to(orders[to], (rows, LANES))
            for start in range(0, local_len, LANES):
                span = slice(start, start + LANES)
                tiles_in = [held[part, to, u, :, span] for u in range(tiles)]
                for t in range(tiles):
                    wanted = order[t * sub : (t + 1) * sub]
                    moved = jnp.zeros((sub, LANES), jnp.float32)
                    for u, tile in enumerate(tiles_in):
                        picked = jnp.take_along_axis(tile, wanted % sub, axis=0)
                        moved = jnp.where(wanted // sub == u, picked, moved)
                    moved_rows[t, to, part, :, span] = moved
    for ref, chunk, (half, chip), core in offers:
        if half:
            ref[...] = moved_rows[chunk, me ^ (2 * chip + core)]
    for copy in blocks:
        copy.wait()


def join_kernel(groups, *refs):
    outs = refs[-len(groups) :]
    for group, out in zip(groups, outs):
        for i, (which, index) in enumerate(group):
            out[2 * i] = refs[2 * which][index]
            out[2 * i + 1] = refs[2 * which + 1][index]


def correlate(got, forward, backward, twist, out, keep, halves, left, right):
    count = got.shape[0] // 2
    rows = got.shape[2]
    steps = got.shape[3] // LANES
    points = count * steps
    own = lax.axis_index("half")

    def read(start, swap):
        def load(t):
            where = slice(t % steps * LANES, (t % steps + 1) * LANES)
            re = got[start + t // steps, 0, :, where]
            im = got[start + t // steps, 1, :, where]
            return (im, re) if swap else (re, im)

        return load

    for which, target in enumerate((left, right)):
        start = jnp.where(own == which, 0, count)
        for k, value in long_dft(read(start, which == 1), keep, points):
            split_store(halves, k * rows, rows, *times_twist(twist, k, value))
        target[...] = lane_dft(halves, forward)

    for k in range(points):
        span = pl.ds(k * rows, rows)
        a_re, a_im = left[span, :LANES], left[span, LANES:]
        b_im, b_re = right[span, :LANES], right[span, LANES:]
        split_store(halves, k * rows, rows, a_re * b_im + a_im * b_re, a_re * b_re - a_im * b_im)
    left[...] = lane_dft(halves, backward)

    def spectrum(k):
        span = pl.ds(k * rows, rows)
        return times_twist(twist, k, (left[span, :LANES], left[span, LANES:]))

    for t, (c_im, c_re) in long_dft(spectrum, keep, points):
        where = slice(t % steps * LANES, (t % steps + 1) * LANES)
        out[t // steps, 0, :, where] = c_im
        out[t // steps, 1, :, where] = -c_re


def pieces_of(refs, held):
    for ref, blocks in zip(refs, held):
        for i, block in enumerate(blocks):
            yield (ref.at[i] if len(blocks) > 1 else ref), *block


def correlate_kernel(chunk, held, bundled, direct, *refs):
    count = len(held)
    pieces, (forward, backward, twist) = refs[:count], refs[count : count + 3]
    mine, give, *rest = refs[count + 3 :]
    far, (got, out, *scratch) = rest[: 2 * len(direct)], rest[2 * len(direct) :]
    own = lax.axis_index("half")
    me = lax.axis_index("en")
    for ref, of, (half, chip), core in pieces_of(pieces, held):
        if of == chunk:
            side = 1 - own if half else own
            got[side * out.shape[0] + (me ^ (2 * chip + core))] = ref[...]
    correlate(got, forward, backward, twist, out, *scratch)
    for i, chip in enumerate(bundled):
        mine[i] = out[me ^ (2 * chip)]
        give[i] = out[me ^ (2 * chip + 1)]
    for i, ref in enumerate(far):
        ref[...] = out[me ^ (2 * direct[i // 2] + i % 2)]


def keep_kernel(held, *refs):
    out, sems = refs[-2:]
    me = lax.axis_index("en")
    copies = [
        pltpu.make_async_copy(ref, out.at[:, me ^ (2 * chip + core), chunk], sems.at[i])
        for i, (ref, chunk, chip, core) in enumerate(pieces_of(refs, held))
    ]
    for copy in copies:
        copy.start()
    for copy in copies:
        copy.wait()


def call(kernel, out_shape, in_specs, out_specs, scratch=(), mib=4, **settings):
    return pl.pallas_call(
        kernel,
        out_shape=out_shape,
        in_specs=in_specs,
        out_specs=out_specs,
        scratch_shapes=scratch,
        compiler_params=pltpu.CompilerParams(vmem_limit_bytes=mib << 20),
        **settings,
    )


def plan(chips):
    arrive = [(half, chip) for chip in range(chips - 1, -1, -1) for half in (1, 0)]
    back = list(range(chips - 1, -1, -1))
    cut = chips // 2
    return arrive[: 2 * cut], arrive[2 * cut :], back[:cut], back[cut:]


def body(lesser, greater, mirror):
    _, group_rows, local_len = lesser.shape
    count = lax.axis_size("en")
    chips = count // 2
    rows = group_rows // count
    tiles = rows // SUBLANES
    length = local_len * count
    points = length // LANES
    f32 = jnp.float32
    block = jax.ShapeDtypeStruct((2, SUBLANES, local_len), f32)
    tiled = jax.ShapeDtypeStruct((2, count, tiles, SUBLANES, local_len), f32)
    in_vmem = pl.BlockSpec(memory_space=pltpu.VMEM)
    in_hbm = pl.BlockSpec(memory_space=pltpu.HBM)
    dma = pltpu.SemaphoreType.DMA
    far, near, far_back, near_back = plan(chips)

    def stack(pieces):
        return jax.ShapeDtypeStruct((pieces, *block.shape), f32)

    def vmem(shape):
        return pltpu.VMEM(shape.shape, shape.dtype)

    def swap(give):
        return lax.ppermute(give, "en", [(e, e ^ 1) for e in range(count)])

    def join(pairs, groups):
        shapes = [stack(2 * len(group)) for group in groups]
        return call(
            functools.partial(join_kernel, groups),
            shapes,
            [in_vmem] * 2 * len(pairs),
            [in_vmem] * len(groups),
        )(*sum(pairs, ()))

    def send(value, half, chip, core=0):
        distance = half * count + 2 * chip + core
        route = [(d, d ^ distance) for d in range(2 * count)]
        return lax.ppermute(value, ("half", "en"), route) if distance else value

    mirror, lesser, greater = (
        pltpu.with_memory_space_constraint(x, pltpu.HBM)
        for x in (mirror[None], lesser.reshape(tiled.shape), greater.reshape(tiled.shape))
    )
    tables = (
        jnp.asarray(dft_block(1.0)),
        jnp.asarray(dft_block(length**-1.5)),
        jnp.asarray(twiddles(points)),
    )

    last = tiles - 1
    chunks = range(tiles)
    alone = [(0, t, core) for t in far[:1] for core in range(2)]
    groups = [[(0, t)] for t in far[1:]]
    groups += [[(chunk, t) for chunk in chunks] for t in near]
    groups += [[(chunk, t)] for chunk in chunks[1:] for t in far]
    units = sum(groups, [])
    mine, give, *single = call(
        functools.partial(pack_kernel, units, alone),
        [stack(len(units))] * 2 + [block] * len(alone),
        [in_hbm] * 3,
        [in_vmem] * (2 + len(alone)),
        [
            pltpu.VMEM((1, group_rows), jnp.int32),
            vmem(tiled),
            pltpu.VMEM((tiles, count, *block.shape), f32),
            dma((3,)),
            dma((2 * len(units) + len(alone),)),
        ],
        mib=8,
    )(mirror, lesser, greater)
    given = swap(give)
    arrived = [send(value, *t, core) for value, (_, t, core) in zip(single, alone)]
    held = [(one,) for one in alone]
    places = iter(range(len(units)))
    joined = join([(mine, given)], [[(0, next(places)) for _ in group] for group in groups])
    for value, group in zip(joined, groups):
        chunk, t = group[0]
        arrived.append(send(value, *t))
        held.append(tuple((*unit, core) for unit in group for core in range(2)))

    kept, pairs, out = [], [], []
    for chunk in chunks:
        direct = far_back[:1] if chunk == last else []
        bundled = far_back[len(direct) :] + near_back
        used = [i for i, blocks in enumerate(held) if any(b[0] == chunk for b in blocks)]
        mine, give, *single = call(
            functools.partial(
                correlate_kernel, chunk, tuple(held[i] for i in used), bundled, direct
            ),
            [stack(len(bundled))] * 2 + [block] * 2 * len(direct),
            [in_vmem] * (len(used) + 3),
            [in_vmem] * (2 + 2 * len(direct)),
            [
                vmem(stack(2 * count)),
                vmem(stack(count)),
                pltpu.VMEM((points, 2, SUBLANES, LANES), f32),
                pltpu.VMEM((2, points * SUBLANES, 2 * LANES), jnp.bfloat16),
                pltpu.VMEM((points * SUBLANES, 2 * LANES), f32),
                pltpu.VMEM((points * SUBLANES, 2 * LANES), f32),
            ],
            mib=16,
            cost_estimate=pl.CostEstimate(
                flops=3 * 2 * 3 * points * SUBLANES * 4 * LANES * LANES,
                bytes_accessed=4 << 20,
                transcendentals=0,
            ),
        )(*(arrived[i] for i in used), *tables)
        returned = [
            (
                send(value, 0, direct[i // 2], i % 2),
                ((chunk, direct[i // 2], i % 2),),
            )
            for i, value in enumerate(single)
        ]
        pairs.append((mine, swap(give)))
        kept.append(bundled)
        groups = [[(chunk, z)] for z in far_back[len(direct) :]]
        if chunk == last:
            groups += [[(c, z) for c in chunks] for z in near_back]
        joined = join(
            pairs if chunk == last else pairs[-1:],
            [[(c if chunk == last else 0, kept[c].index(z)) for c, z in group] for group in groups],
        )
        for value, group in zip(joined, groups):
            z = group[0][1]
            blocks = tuple((*unit, core) for unit in group for core in range(2))
            returned.append((send(value, 0, z), blocks))
        values, blocks = zip(*returned)
        out = [
            call(
                functools.partial(keep_kernel, blocks),
                tiled,
                [in_vmem] * len(values) + [in_hbm] * len(out),
                in_hbm,
                [dma((sum(map(len, blocks)),))],
                mib=1,
                input_output_aliases={len(values): 0} if out else {},
            )(*values, *out)
        ]
    return out[0].reshape(2, group_rows, local_len)


def solution(mesh):
    groups = mesh.shape["grp"]
    devices = mesh.devices.reshape(2, groups // 2, mesh.shape["en"])
    finer = Mesh(devices, ("half", "grp", "en"))
    spec = P(None, ("half", "grp"), "en")
    in_specs = (spec, spec, P(("half", "grp")))

    return jax.shard_map(body, mesh=finer, in_specs=in_specs, out_specs=spec, check_vma=False)
```

profile of v0, /device:TPU:0, one launch (start us, length us, event | category | flops | bytes accessed | tf_op | source)
XLA Modules:
  0.0 59.5 jit_solution(1070680957387074561)
XLA Ops:
  0.0 1.7 %shard_map.64 = (f32[15,2,8,512]{3,2,1,0:T(8,128)S(1)}, f32[15,2,8,512]{3,2,1,0:T(8,128)S(1)}, f32[2,8,512]{2,1,0:T(8,128)S(1)}, f32[2,8,512]{2,1,0:T(8,128)S(1)}) custom-call(s32[1,128]{1,0:T(1,128)} %bitcast.6, f32[2,8,2,8,512]{4,3,2,1,0:T(8,128)} %bitcast.4, f32[2,8,2,8,512]{4,3,2,1,0:T(8,128)} %bitcast.5), custom_call_target="tpu_custom_call" | custom-call | tf_op jit(solution)/shard_map/pallas_call | solution.py:312
  1.7 0.6 collective-permute-start
  2.3 1.5 %collective-permute-done.refs_1_ = f32[15,2,8,512]{3,2,1,0:T(8,128)S(1)} collective-permute-done((f32[15,2,8,512]{3,2,1,0:T(8,128)S(1)}, f32[15,2,8,512]{3,2,1,0:T(8,128)S(1)}, u32[]{:S(2)}, u32[]{:S(2)}) %collective-permute-start) | collective-permute-done | bytes 491552 | tf_op jit(solution)/shard_map/ppermute | solution.py:279
  3.8 0.0 copy-start
  3.8 0.0 copy-start.1
  3.8 0.0 copy-start.2
  3.8 0.1 shard_map.65
  3.8 5.0 %collective-permute-start.12 = (f32[2,2,8,512]{3,2,1,0:T(8,128)S(1)}, f32[2,2,8,512]{3,2,1,0:T(8,128)S(1)}, u32[]{:S(2)}, u32[]{:S(2)}) collective-permute-start(f32[2,2,8,512]{3,2,1,0:T(8,128)S(1)} %get-tuple-element.45), channel_id=1, source_target_pairs={{0,6},{1,7},{2,4},{3,5},{4,2},{5,3},{6,0},{7,1},{16,22},{17,23},{1... | collective-permute-start | bytes 196616 | tf_op jit(solution)/shard_map/ppermute | solution.py:293
  8.9 1.2 %collective-permute-start.10 = (f32[2,8,512]{2,1,0:T(8,128)S(1)}, f32[2,8,512]{2,1,0:T(8,128)S(1)}, u32[]{:S(2)}, u32[]{:S(2)}) collective-permute-start(f32[2,8,512]{2,1,0:T(8,128)S(1)} %get-tuple-element.43), channel_id=1, source_target_pairs={{0,22},{1,23},{2,20},{3,21},{4,18},{5,19},{6,16},{7,17},{16,6},{17... | collective-permute-start | bytes 98312 | tf_op jit(solution)/shard_map/ppermute | solution.py:293
  10.0 0.0 collective-permute-start.1
  10.1 1.8 %collective-permute-start.2 = (f32[4,2,8,512]{3,2,1,0:T(8,128)S(1)}, f32[4,2,8,512]{3,2,1,0:T(8,128)S(1)}, u32[]{:S(2)}, u32[]{:S(2)}) collective-permute-start(f32[4,2,8,512]{3,2,1,0:T(8,128)S(1)} %get-tuple-element.34), channel_id=1, source_target_pairs={{0,2},{1,3},{2,0},{3,1},{4,6},{5,7},{6,4},{7,5},{16,18},{17,19},{1... | collective-permute-start | bytes 393224 | tf_op jit(solution)/shard_map/ppermute | solution.py:293
  11.9 3.3 %collective-permute-start.11 = (f32[2,8,512]{2,1,0:T(8,128)S(1)}, f32[2,8,512]{2,1,0:T(8,128)S(1)}, u32[]{:S(2)}, u32[]{:S(2)}) collective-permute-start(f32[2,8,512]{2,1,0:T(8,128)S(1)} %get-tuple-element.44), channel_id=1, source_target_pairs={{0,23},{1,22},{2,21},{3,20},{4,19},{5,18},{6,17},{7,16},{16,7},{17... | collective-permute-start | bytes 98312 | tf_op jit(solution)/shard_map/ppermute | solution.py:293
  15.2 0.6 %collective-permute-done.10.refs_0_ = f32[2,8,512]{2,1,0:T(8,128)S(1)} collective-permute-done((f32[2,8,512]{2,1,0:T(8,128)S(1)}, f32[2,8,512]{2,1,0:T(8,128)S(1)}, u32[]{:S(2)}, u32[]{:S(2)}) %collective-permute-start.10) | collective-permute-done | bytes 32800 | tf_op jit(solution)/shard_map/ppermute | solution.py:293
  15.8 1.5 %collective-permute-start.3 = (f32[4,2,8,512]{3,2,1,0:T(8,128)S(1)}, f32[4,2,8,512]{3,2,1,0:T(8,128)S(1)}, u32[]{:S(2)}, u32[]{:S(2)}) collective-permute-start(f32[4,2,8,512]{3,2,1,0:T(8,128)S(1)} %get-tuple-element.35), channel_id=1, source_target_pairs={{0,16},{1,17},{2,18},{3,19},{4,20},{5,21},{6,22},{7,23},{16,0},{17... | collective-permute-start | bytes 393224 | tf_op jit(solution)/shard_map/ppermute | solution.py:293
  17.4 2.6 %collective-permute-done.11.refs_1_ = f32[2,8,512]{2,1,0:T(8,128)S(1)} collective-permute-done((f32[2,8,512]{2,1,0:T(8,128)S(1)}, f32[2,8,512]{2,1,0:T(8,128)S(1)}, u32[]{:S(2)}, u32[]{:S(2)}) %collective-permute-start.11) | collective-permute-done | bytes 32800 | tf_op jit(solution)/shard_map/ppermute | solution.py:293
  20.0 0.0 collective-permute-start.13
  20.0 0.0 collective-permute-done.12.refs_2_
  20.0 3.8 %collective-permute-start.14 = (f32[2,2,8,512]{3,2,1,0:T(8,128)S(1)}, f32[2,2,8,512]{3,2,1,0:T(8,128)S(1)}, u32[]{:S(2)}, u32[]{:S(2)}) collective-permute-start(f32[2,2,8,512]{3,2,1,0:T(8,128)S(1)} %get-tuple-element.47), channel_id=1, source_target_pairs={{0,4},{1,5},{2,6},{3,7},{4,0},{5,1},{6,2},{7,3},{16,20},{17,21},{1... | collective-permute-start | bytes 196616 | tf_op jit(solution)/shard_map/ppermute | solution.py:293
  23.8 2.9 %collective-permute-done.13.refs_3_ = f32[2,2,8,512]{3,2,1,0:T(8,128)S(1)} collective-permute-done((f32[2,2,8,512]{3,2,1,0:T(8,128)S(1)}, f32[2,2,8,512]{3,2,1,0:T(8,128)S(1)}, u32[]{:S(2)}, u32[]{:S(2)}) %collective-permute-start.13) | collective-permute-done | bytes 65568 | tf_op jit(solution)/shard_map/ppermute | solution.py:293
  26.7 3.0 %collective-permute-start.4 = (f32[2,2,8,512]{3,2,1,0:T(8,128)S(1)}, f32[2,2,8,512]{3,2,1,0:T(8,128)S(1)}, u32[]{:S(2)}, u32[]{:S(2)}) collective-permute-start(f32[2,2,8,512]{3,2,1,0:T(8,128)S(1)} %get-tuple-element.37), channel_id=1, source_target_pairs={{0,22},{1,23},{2,20},{3,21},{4,18},{5,19},{6,16},{7,17},{16,6},{17... | collective-permute-start | bytes 196616 | tf_op jit(solution)/shard_map/ppermute | solution.py:293
  29.7 0.0 collective-permute-done.14.refs_4_
  29.7 2.4 %collective-permute-start.5 = (f32[2,2,8,512]{3,2,1,0:T(8,128)S(1)}, f32[2,2,8,512]{3,2,1,0:T(8,128)S(1)}, u32[]{:S(2)}, u32[]{:S(2)}) collective-permute-start(f32[2,2,8,512]{3,2,1,0:T(8,128)S(1)} %get-tuple-element.38), channel_id=1, source_target_pairs={{0,6},{1,7},{2,4},{3,5},{4,2},{5,3},{6,0},{7,1},{16,22},{17,23},{1... | collective-permute-start | bytes 196616 | tf_op jit(solution)/shard_map/ppermute | solution.py:293
  32.1 0.0 collective-permute-done.1.refs_0_.refs_5_
  32.1 0.0 collective-permute-start.6
  32.1 0.0 collective-permute-done.2.refs_1_.refs_6_
  32.1 2.7 %collective-permute-start.7 = (f32[2,2,8,512]{3,2,1,0:T(8,128)S(1)}, f32[2,2,8,512]{3,2,1,0:T(8,128)S(1)}, u32[]{:S(2)}, u32[]{:S(2)}) collective-permute-start(f32[2,2,8,512]{3,2,1,0:T(8,128)S(1)} %get-tuple-element.40), channel_id=1, source_target_pairs={{0,4},{1,5},{2,6},{3,7},{4,0},{5,1},{6,2},{7,3},{16,20},{17,21},{1... | collective-permute-start | bytes 196616 | tf_op jit(solution)/shard_map/ppermute | solution.py:293
  34.8 0.0 collective-permute-done.3.refs_2_.refs_7_
  34.8 0.0 copy-done
  34.8 0.0 copy-done.1
  34.8 0.0 copy-done.2
  34.8 1.1 %shard_map.67 = (f32[4,2,8,512]{3,2,1,0:T(8,128)S(1)}, f32[4,2,8,512]{3,2,1,0:T(8,128)S(1)}) custom-call(f32[2,8,512]{2,1,0:T(8,128)S(1)} %collective-permute-done.10.refs_0_, f32[2,8,512]{2,1,0:T(8,128)S(1)} %collective-permute-done.11.refs_1_, f32[2,2,8,512]{3,2,1,0:T(8,128)S(1)} %collective-permute-done.12.refs_2_, ...), custom_call_target="tpu_custom_call" | custom-call | flops 301989888 | bytes 4194304 | tf_op jit(solution)/shard_map/pallas_call | solution.py:341
  36.0 0.1 collective-permute-start.15
  36.0 0.0 collective-permute-done.4.refs_4_
  36.0 0.5 collective-permute-done.5.refs_5_
  36.5 4.7 %collective-permute-done.6.refs_6_ = f32[2,2,8,512]{3,2,1,0:T(8,128)S(1)} collective-permute-done((f32[2,2,8,512]{3,2,1,0:T(8,128)S(1)}, f32[2,2,8,512]{3,2,1,0:T(8,128)S(1)}, u32[]{:S(2)}, u32[]{:S(2)}) %collective-permute-start.6) | collective-permute-done | bytes 65568 | tf_op jit(solution)/shard_map/ppermute | solution.py:293
  41.3 0.1 collective-permute-done.7.refs_7_
  41.4 1.1 %shard_map.66 = (f32[3,2,8,512]{3,2,1,0:T(8,128)S(1)}, f32[3,2,8,512]{3,2,1,0:T(8,128)S(1)}, f32[2,8,512]{2,1,0:T(8,128)S(1)}, f32[2,8,512]{2,1,0:T(8,128)S(1)}) custom-call(f32[4,2,8,512]{3,2,1,0:T(8,128)S(1)} %collective-permute-done.1.refs_0_.refs_5_, f32[4,2,8,512]{3,2,1,0:T(8,128)S(1)} %collective-permute-done.2.refs_1_.refs_6_, ...), custom_call_target="tpu_custom_call" | custom-call | flops 301989888 | bytes 4194304 | tf_op jit(solution)/shard_map/pallas_call | solution.py:341
  42.5 0.1 collective-permute-start.16
  42.6 1.3 %collective-permute-done.16.refs_3_ = f32[3,2,8,512]{3,2,1,0:T(8,128)S(1)} collective-permute-done((f32[3,2,8,512]{3,2,1,0:T(8,128)S(1)}, f32[3,2,8,512]{3,2,1,0:T(8,128)S(1)}, u32[]{:S(2)}, u32[]{:S(2)}) %collective-permute-start.16) | collective-permute-done | bytes 98336 | tf_op jit(solution)/shard_map/ppermute | solution.py:279
  43.8 0.0 collective-permute-done.15.refs_1_
  43.9 0.1 collective-permute-start.18
  44.0 2.1 %collective-permute-start.19 = (f32[2,2,8,512]{3,2,1,0:T(8,128)S(1)}, f32[2,2,8,512]{3,2,1,0:T(8,128)S(1)}, u32[]{:S(2)}, u32[]{:S(2)}) collective-permute-start(f32[2,2,8,512]{3,2,1,0:T(8,128)S(1)} %get-tuple-element.55), channel_id=1, source_target_pairs={{0,6},{1,7},{2,4},{3,5},{4,2},{5,3},{6,0},{7,1},{16,22},{17,23},{1... | collective-permute-start | bytes 196616 | tf_op jit(solution)/shard_map/ppermute | solution.py:293
  46.0 1.5 %collective-permute-start.20 = (f32[2,2,8,512]{3,2,1,0:T(8,128)S(1)}, f32[2,2,8,512]{3,2,1,0:T(8,128)S(1)}, u32[]{:S(2)}, u32[]{:S(2)}) collective-permute-start(f32[2,2,8,512]{3,2,1,0:T(8,128)S(1)} %get-tuple-element.56), channel_id=1, source_target_pairs={{0,4},{1,5},{2,6},{3,7},{4,0},{5,1},{6,2},{7,3},{16,20},{17,21},{1... | collective-permute-start | bytes 196616 | tf_op jit(solution)/shard_map/ppermute | solution.py:293
  47.5 1.4 %collective-permute-start.17 = (f32[2,2,8,512]{3,2,1,0:T(8,128)S(1)}, f32[2,2,8,512]{3,2,1,0:T(8,128)S(1)}, u32[]{:S(2)}, u32[]{:S(2)}) collective-permute-start(f32[2,2,8,512]{3,2,1,0:T(8,128)S(1)} %get-tuple-element.52), channel_id=1, source_target_pairs={{0,4},{1,5},{2,6},{3,7},{4,0},{5,1},{6,2},{7,3},{16,20},{17,21},{1... | collective-permute-start | bytes 196616 | tf_op jit(solution)/shard_map/ppermute | solution.py:293
  49.0 1.8 %collective-permute-start.8 = (f32[2,8,512]{2,1,0:T(8,128)S(1)}, f32[2,8,512]{2,1,0:T(8,128)S(1)}, u32[]{:S(2)}, u32[]{:S(2)}) collective-permute-start(f32[2,8,512]{2,1,0:T(8,128)S(1)} %get-tuple-element.41), channel_id=1, source_target_pairs={{0,6},{1,7},{2,4},{3,5},{4,2},{5,3},{6,0},{7,1},{16,22},{17,23},{1... | collective-permute-start | bytes 98312 | tf_op jit(solution)/shard_map/ppermute | solution.py:293
  50.8 1.0 %collective-permute-done.19.refs_0_ = f32[2,2,8,512]{3,2,1,0:T(8,128)S(1)} collective-permute-done((f32[2,2,8,512]{3,2,1,0:T(8,128)S(1)}, f32[2,2,8,512]{3,2,1,0:T(8,128)S(1)}, u32[]{:S(2)}, u32[]{:S(2)}) %collective-permute-start.19) | collective-permute-done | bytes 65568 | tf_op jit(solution)/shard_map/ppermute | solution.py:293
  51.8 0.4 collective-permute-start.9
  52.2 5.0 %collective-permute-done.20.refs_1_ = f32[2,2,8,512]{3,2,1,0:T(8,128)S(1)} collective-permute-done((f32[2,2,8,512]{3,2,1,0:T(8,128)S(1)}, f32[2,2,8,512]{3,2,1,0:T(8,128)S(1)}, u32[]{:S(2)}, u32[]{:S(2)}) %collective-permute-start.20) | collective-permute-done | bytes 65568 | tf_op jit(solution)/shard_map/ppermute | solution.py:293
  57.2 0.7 %shard_map.70.refs_5_ = f32[2,8,2,8,512]{4,3,2,1,0:T(8,128)} custom-call(f32[2,2,8,512]{3,2,1,0:T(8,128)S(1)} %collective-permute-done.19.refs_0_, f32[2,2,8,512]{3,2,1,0:T(8,128)S(1)} %collective-permute-done.20.refs_1_), custom_call_target="tpu_custom_call" | custom-call | tf_op jit(solution)/shard_map/pallas_call | solution.py:385
  57.9 0.0 collective-permute-done.8.refs_0_
  57.9 0.0 collective-permute-done.9.refs_1_
  57.9 0.7 %collective-permute-done.17.refs_2_ = f32[2,2,8,512]{3,2,1,0:T(8,128)S(1)} collective-permute-done((f32[2,2,8,512]{3,2,1,0:T(8,128)S(1)}, f32[2,2,8,512]{3,2,1,0:T(8,128)S(1)}, u32[]{:S(2)}, u32[]{:S(2)}) %collective-permute-start.17) | collective-permute-done | bytes 65568 | tf_op jit(solution)/shard_map/ppermute | solution.py:293
  58.6 0.0 collective-permute-done.18.refs_3_
  58.6 0.8 %shard_map.71 = f32[2,8,2,8,512]{4,3,2,1,0:T(8,128)} custom-call(f32[2,8,512]{2,1,0:T(8,128)S(1)} %collective-permute-done.8.refs_0_, f32[2,8,512]{2,1,0:T(8,128)S(1)} %collective-permute-done.9.refs_1_, f32[2,2,8,512]{3,2,1,0:T(8,128)S(1)} %collective-permute-done.17.refs_2_, ...), custom_call_target="tpu_custom_call", output_to_operand_aliasing={{}: (5, {})} | custom-call | tf_op jit(solution)/shard_map/pallas_call | solution.py:385
  (2 shorter events, 0.0 us)
Async XLA Ops:
  1.7 2.0 %collective-permute-start = (f32[15,2,8,512]{3,2,1,0:T(8,128)S(1)}, f32[15,2,8,512]{3,2,1,0:T(8,128)S(1)}, u32[]{:S(2)}, u32[]{:S(2)}) collective-permute-start(f32[15,2,8,512]{3,2,1,0:T(8,128)S(1)} %get-tuple-element.32), channel_id=1, source_target_pairs={{0,1},{1,0},{2,3},{3,2},{4,5},{5,4},{6,7},{7,6},{8,9},{9,8},{10,11... | collective-permute-start | bytes 1474568 | tf_op jit(solution)/shard_map/ppermute | solution.py:279
  3.8 31.0 %copy-start = (bf16[2,256,256]{2,1,0:T(8,128)(2,1)S(1)}, bf16[2,256,256]{2,1,0:T(8,128)(2,1)}, u32[]{:S(2)}) copy-start(bf16[2,256,256]{2,1,0:T(8,128)(2,1)} %constant.7.clone.refs_9_.refs_10_) | copy-start | bytes 786436
  3.8 31.0 %copy-start.1 = (bf16[2,256,256]{2,1,0:T(8,128)(2,1)S(1)}, bf16[2,256,256]{2,1,0:T(8,128)(2,1)}, u32[]{:S(2)}) copy-start(bf16[2,256,256]{2,1,0:T(8,128)(2,1)} %constant.6.clone.refs_8_.refs_9_) | copy-start | bytes 786436
  3.8 31.0 %copy-start.2 = (f32[2,32,128]{2,1,0:T(8,128)S(1)}, f32[2,32,128]{2,1,0:T(8,128)}, u32[]{:S(2)}) copy-start(f32[2,32,128]{2,1,0:T(8,128)} %constant.8.clone.refs_10_.refs_11_) | copy-start | bytes 98308
  3.8 16.1 %collective-permute-start.12 = (f32[2,2,8,512]{3,2,1,0:T(8,128)S(1)}, f32[2,2,8,512]{3,2,1,0:T(8,128)S(1)}, u32[]{:S(2)}, u32[]{:S(2)}) collective-permute-start(f32[2,2,8,512]{3,2,1,0:T(8,128)S(1)} %get-tuple-element.45), channel_id=1, source_target_pairs={{0,6},{1,7},{2,4},{3,5},{4,2},{5,3},{6,0},{7,1},{16,22},{17,23},{1... | collective-permute-start | bytes 196616 | tf_op jit(solution)/shard_map/ppermute | solution.py:293
  8.9 7.0 %collective-permute-start.10 = (f32[2,8,512]{2,1,0:T(8,128)S(1)}, f32[2,8,512]{2,1,0:T(8,128)S(1)}, u32[]{:S(2)}, u32[]{:S(2)}) collective-permute-start(f32[2,8,512]{2,1,0:T(8,128)S(1)} %get-tuple-element.43), channel_id=1, source_target_pairs={{0,22},{1,23},{2,20},{3,21},{4,18},{5,19},{6,16},{7,17},{16,6},{17... | collective-permute-start | bytes 98312 | tf_op jit(solution)/shard_map/ppermute | solution.py:293
  10.0 22.1 %collective-permute-start.1 = (f32[4,2,8,512]{3,2,1,0:T(8,128)S(1)}, f32[4,2,8,512]{3,2,1,0:T(8,128)S(1)}, u32[]{:S(2)}, u32[]{:S(2)}) collective-permute-start(f32[4,2,8,512]{3,2,1,0:T(8,128)S(1)} %get-tuple-element.33), channel_id=1, source_target_pairs={{0,18},{1,19},{2,16},{3,17},{4,22},{5,23},{6,20},{7,21},{16,2},{17... | collective-permute-start | bytes 393224 | tf_op jit(solution)/shard_map/ppermute | solution.py:293
  10.1 22.1 %collective-permute-start.2 = (f32[4,2,8,512]{3,2,1,0:T(8,128)S(1)}, f32[4,2,8,512]{3,2,1,0:T(8,128)S(1)}, u32[]{:S(2)}, u32[]{:S(2)}) collective-permute-start(f32[4,2,8,512]{3,2,1,0:T(8,128)S(1)} %get-tuple-element.34), channel_id=1, source_target_pairs={{0,2},{1,3},{2,0},{3,1},{4,6},{5,7},{6,4},{7,5},{16,18},{17,19},{1... | collective-permute-start | bytes 393224 | tf_op jit(solution)/shard_map/ppermute | solution.py:293
  11.9 8.1 %collective-permute-start.11 = (f32[2,8,512]{2,1,0:T(8,128)S(1)}, f32[2,8,512]{2,1,0:T(8,128)S(1)}, u32[]{:S(2)}, u32[]{:S(2)}) collective-permute-start(f32[2,8,512]{2,1,0:T(8,128)S(1)} %get-tuple-element.44), channel_id=1, source_target_pairs={{0,23},{1,22},{2,21},{3,20},{4,19},{5,18},{6,17},{7,16},{16,7},{17... | collective-permute-start | bytes 98312 | tf_op jit(solution)/shard_map/ppermute | solution.py:293
  15.8 19.0 %collective-permute-start.3 = (f32[4,2,8,512]{3,2,1,0:T(8,128)S(1)}, f32[4,2,8,512]{3,2,1,0:T(8,128)S(1)}, u32[]{:S(2)}, u32[]{:S(2)}) collective-permute-start(f32[4,2,8,512]{3,2,1,0:T(8,128)S(1)} %get-tuple-element.35), channel_id=1, source_target_pairs={{0,16},{1,17},{2,18},{3,19},{4,20},{5,21},{6,22},{7,23},{16,0},{17... | collective-permute-start | bytes 393224 | tf_op jit(solution)/shard_map/ppermute | solution.py:293
  20.0 6.7 %collective-permute-start.13 = (f32[2,2,8,512]{3,2,1,0:T(8,128)S(1)}, f32[2,2,8,512]{3,2,1,0:T(8,128)S(1)}, u32[]{:S(2)}, u32[]{:S(2)}) collective-permute-start(f32[2,2,8,512]{3,2,1,0:T(8,128)S(1)} %get-tuple-element.46), channel_id=1, source_target_pairs={{0,20},{1,21},{2,22},{3,23},{4,16},{5,17},{6,18},{7,19},{16,4},{17... | collective-permute-start | bytes 196616 | tf_op jit(solution)/shard_map/ppermute | solution.py:293
  20.0 9.8 %collective-permute-start.14 = (f32[2,2,8,512]{3,2,1,0:T(8,128)S(1)}, f32[2,2,8,512]{3,2,1,0:T(8,128)S(1)}, u32[]{:S(2)}, u32[]{:S(2)}) collective-permute-start(f32[2,2,8,512]{3,2,1,0:T(8,128)S(1)} %get-tuple-element.47), channel_id=1, source_target_pairs={{0,4},{1,5},{2,6},{3,7},{4,0},{5,1},{6,2},{7,3},{16,20},{17,21},{1... | collective-permute-start | bytes 196616 | tf_op jit(solution)/shard_map/ppermute | solution.py:293
  26.7 9.4 %collective-permute-start.4 = (f32[2,2,8,512]{3,2,1,0:T(8,128)S(1)}, f32[2,2,8,512]{3,2,1,0:T(8,128)S(1)}, u32[]{:S(2)}, u32[]{:S(2)}) collective-permute-start(f32[2,2,8,512]{3,2,1,0:T(8,128)S(1)} %get-tuple-element.37), channel_id=1, source_target_pairs={{0,22},{1,23},{2,20},{3,21},{4,18},{5,19},{6,16},{7,17},{16,6},{17... | collective-permute-start | bytes 196616 | tf_op jit(solution)/shard_map/ppermute | solution.py:293
  29.7 6.8 %collective-permute-start.5 = (f32[2,2,8,512]{3,2,1,0:T(8,128)S(1)}, f32[2,2,8,512]{3,2,1,0:T(8,128)S(1)}, u32[]{:S(2)}, u32[]{:S(2)}) collective-permute-start(f32[2,2,8,512]{3,2,1,0:T(8,128)S(1)} %get-tuple-element.38), channel_id=1, source_target_pairs={{0,6},{1,7},{2,4},{3,5},{4,2},{5,3},{6,0},{7,1},{16,22},{17,23},{1... | collective-permute-start | bytes 196616 | tf_op jit(solution)/shard_map/ppermute | solution.py:293
  32.1 9.2 %collective-permute-start.6 = (f32[2,2,8,512]{3,2,1,0:T(8,128)S(1)}, f32[2,2,8,512]{3,2,1,0:T(8,128)S(1)}, u32[]{:S(2)}, u32[]{:S(2)}) collective-permute-start(f32[2,2,8,512]{3,2,1,0:T(8,128)S(1)} %get-tuple-element.39), channel_id=1, source_target_pairs={{0,20},{1,21},{2,22},{3,23},{4,16},{5,17},{6,18},{7,19},{16,4},{17... | collective-permute-start | bytes 196616 | tf_op jit(solution)/shard_map/ppermute | solution.py:293
  32.1 9.2 %collective-permute-start.7 = (f32[2,2,8,512]{3,2,1,0:T(8,128)S(1)}, f32[2,2,8,512]{3,2,1,0:T(8,128)S(1)}, u32[]{:S(2)}, u32[]{:S(2)}) collective-permute-start(f32[2,2,8,512]{3,2,1,0:T(8,128)S(1)} %get-tuple-element.40), channel_id=1, source_target_pairs={{0,4},{1,5},{2,6},{3,7},{4,0},{5,1},{6,2},{7,3},{16,20},{17,21},{1... | collective-permute-start | bytes 196616 | tf_op jit(solution)/shard_map/ppermute | solution.py:293
  36.0 7.9 %collective-permute-start.15 = (f32[4,2,8,512]{3,2,1,0:T(8,128)S(1)}, f32[4,2,8,512]{3,2,1,0:T(8,128)S(1)}, u32[]{:S(2)}, u32[]{:S(2)}) collective-permute-start(f32[4,2,8,512]{3,2,1,0:T(8,128)S(1)} %get-tuple-element.49), channel_id=1, source_target_pairs={{0,1},{1,0},{2,3},{3,2},{4,5},{5,4},{6,7},{7,6},{8,9},{9,8},{10,11... | collective-permute-start | bytes 393224 | tf_op jit(solution)/shard_map/ppermute | solution.py:279
  42.5 1.4 %collective-permute-start.16 = (f32[3,2,8,512]{3,2,1,0:T(8,128)S(1)}, f32[3,2,8,512]{3,2,1,0:T(8,128)S(1)}, u32[]{:S(2)}, u32[]{:S(2)}) collective-permute-start(f32[3,2,8,512]{3,2,1,0:T(8,128)S(1)} %get-tuple-element.51), channel_id=1, source_target_pairs={{0,1},{1,0},{2,3},{3,2},{4,5},{5,4},{6,7},{7,6},{8,9},{9,8},{10,11... | collective-permute-start | bytes 294920 | tf_op jit(solution)/shard_map/ppermute | solution.py:279
  43.9 14.7 %collective-permute-start.18 = (f32[4,2,8,512]{3,2,1,0:T(8,128)S(1)}, f32[4,2,8,512]{3,2,1,0:T(8,128)S(1)}, u32[]{:S(2)}, u32[]{:S(2)}) collective-permute-start(f32[4,2,8,512]{3,2,1,0:T(8,128)S(1)} %get-tuple-element.53), channel_id=1, source_target_pairs={{0,2},{1,3},{2,0},{3,1},{4,6},{5,7},{6,4},{7,5},{16,18},{17,19},{1... | collective-permute-start | bytes 393224 | tf_op jit(solution)/shard_map/ppermute | solution.py:293
  44.0 7.8 %collective-permute-start.19 = (f32[2,2,8,512]{3,2,1,0:T(8,128)S(1)}, f32[2,2,8,512]{3,2,1,0:T(8,128)S(1)}, u32[]{:S(2)}, u32[]{:S(2)}) collective-permute-start(f32[2,2,8,512]{3,2,1,0:T(8,128)S(1)} %get-tuple-element.55), channel_id=1, source_target_pairs={{0,6},{1,7},{2,4},{3,5},{4,2},{5,3},{6,0},{7,1},{16,22},{17,23},{1... | collective-permute-start | bytes 196616 | tf_op jit(solution)/shard_map/ppermute | solution.py:293
  46.0 11.2 %collective-permute-start.20 = (f32[2,2,8,512]{3,2,1,0:T(8,128)S(1)}, f32[2,2,8,512]{3,2,1,0:T(8,128)S(1)}, u32[]{:S(2)}, u32[]{:S(2)}) collective-permute-start(f32[2,2,8,512]{3,2,1,0:T(8,128)S(1)} %get-tuple-element.56), channel_id=1, source_target_pairs={{0,4},{1,5},{2,6},{3,7},{4,0},{5,1},{6,2},{7,3},{16,20},{17,21},{1... | collective-permute-start | bytes 196616 | tf_op jit(solution)/shard_map/ppermute | solution.py:293
  47.5 11.1 %collective-permute-start.17 = (f32[2,2,8,512]{3,2,1,0:T(8,128)S(1)}, f32[2,2,8,512]{3,2,1,0:T(8,128)S(1)}, u32[]{:S(2)}, u32[]{:S(2)}) collective-permute-start(f32[2,2,8,512]{3,2,1,0:T(8,128)S(1)} %get-tuple-element.52), channel_id=1, source_target_pairs={{0,4},{1,5},{2,6},{3,7},{4,0},{5,1},{6,2},{7,3},{16,20},{17,21},{1... | collective-permute-start | bytes 196616 | tf_op jit(solution)/shard_map/ppermute | solution.py:293
  49.0 8.9 %collective-permute-start.8 = (f32[2,8,512]{2,1,0:T(8,128)S(1)}, f32[2,8,512]{2,1,0:T(8,128)S(1)}, u32[]{:S(2)}, u32[]{:S(2)}) collective-permute-start(f32[2,8,512]{2,1,0:T(8,128)S(1)} %get-tuple-element.41), channel_id=1, source_target_pairs={{0,6},{1,7},{2,4},{3,5},{4,2},{5,3},{6,0},{7,1},{16,22},{17,23},{1... | collective-permute-start | bytes 98312 | tf_op jit(solution)/shard_map/ppermute | solution.py:293
  51.8 6.1 %collective-permute-start.9 = (f32[2,8,512]{2,1,0:T(8,128)S(1)}, f32[2,8,512]{2,1,0:T(8,128)S(1)}, u32[]{:S(2)}, u32[]{:S(2)}) collective-permute-start(f32[2,8,512]{2,1,0:T(8,128)S(1)} %get-tuple-element.42), channel_id=1, source_target_pairs={{0,7},{1,6},{2,5},{3,4},{4,3},{5,2},{6,1},{7,0},{16,23},{17,22},{1... | collective-permute-start | bytes 98312 | tf_op jit(solution)/shard_map/ppermute | solution.py:293
where the time goes:
time: 59.6 us; the launch traced here: 59.5 us
  starting transfers between devices  32.8 us (55%)
  waiting for transfers between devices  20.9 us (35%)
  Pallas kernels  5.56 us (9%)
    ppermute x18, starting transfers between devices, send(): return lax.ppermute(value, ('half', 'en'), route) if distance else value  32.1 us
    ppermute x18, waiting for transfers between devices, send(): return lax.ppermute(value, ('half', 'en'), route) if distance else value  18.2 us
    ppermute x3, waiting for transfers between devices, swap(): return lax.ppermute(give, 'en', [(e, e ^ 1) for e in range(count)])  2.77 us
    pallas_call x2, Pallas kernels, body(): call(functools.partial(correlate_kernel, chunk, tuple((held[i] for i in u...  2.23 us
    pallas_call x1, Pallas kernels, body(): call(functools.partial(pack_kernel, units, alone), [stack(len(units))] *...  1.71 us
    pallas_call x2, Pallas kernels, body(): call(functools.partial(keep_kernel, blocks), tiled, [in_vmem] * len(value...  1.52 us
  transfers between devices with their start and end apart: 21, of which 11 were waited for; matrix products, arithmetic and copies ran while one was open for 0% of the time, Pallas kernels for 5%

commit v1 on v0

--- a/solution.py
+++ b/solution.py
@@ -102,6 +102,11 @@
     return re * cos - im * sin, re * sin + im * cos
 
 
+def device(me, count, turn, core):
+    chips = count // 2
+    return 2 * lax.rem(lax.div(me, 2) + turn % chips, chips) + (lax.rem(me, 2) ^ core)
+
+
 def pack_kernel(units, alone, mirror, lesser, greater, mine, give, *refs):
     *single, places, held, moved_rows, sems, block_sems = refs
     _, count, tiles, sub, local_len = lesser.shape
@@ -113,8 +118,10 @@
     offers += [(give.at[i], *unit, 1) for i, unit in enumerate(units)]
     offers += [(ref, *one) for ref, one in zip(single, alone)]
     blocks = [
-        pltpu.make_async_copy(lesser.at[:, me ^ (2 * chip + core), chunk], ref, block_sems.at[i])
-        for i, (ref, chunk, (half, chip), core) in enumerate(offers)
+        pltpu.make_async_copy(
+            lesser.at[:, device(me, count, turn, core), chunk], ref, block_sems.at[i]
+        )
+        for i, (ref, chunk, (half, turn), core) in enumerate(offers)
         if not half
     ]
     for copy in loads + blocks:
@@ -142,9 +149,9 @@
                         picked = jnp.take_along_axis(tile, wanted % sub, axis=0)
                         moved = jnp.where(wanted // sub == u, picked, moved)
                     moved_rows[t, to, part, :, span] = moved
-    for ref, chunk, (half, chip), core in offers:
+    for ref, chunk, (half, turn), core in offers:
         if half:
-            ref[...] = moved_rows[chunk, me ^ (2 * chip + core)]
+            ref[...] = moved_rows[chunk, device(me, count, turn, core)]
     for copy in blocks:
         copy.wait()
 
@@ -203,30 +210,31 @@
 
 
 def correlate_kernel(chunk, held, bundled, direct, *refs):
-    count = len(held)
-    pieces, (forward, backward, twist) = refs[:count], refs[count : count + 3]
-    mine, give, *rest = refs[count + 3 :]
+    pieces, (forward, backward, twist) = refs[: len(held)], refs[len(held) : len(held) + 3]
+    mine, give, *rest = refs[len(held) + 3 :]
     far, (got, out, *scratch) = rest[: 2 * len(direct)], rest[2 * len(direct) :]
+    count = out.shape[0]
     own = lax.axis_index("half")
     me = lax.axis_index("en")
-    for ref, of, (half, chip), core in pieces_of(pieces, held):
+    for ref, of, (half, turn), core in pieces_of(pieces, held):
         if of == chunk:
             side = 1 - own if half else own
-            got[side * out.shape[0] + (me ^ (2 * chip + core))] = ref[...]
+            got[side * count + device(me, count, -turn, core)] = ref[...]
     correlate(got, forward, backward, twist, out, *scratch)
-    for i, chip in enumerate(bundled):
-        mine[i] = out[me ^ (2 * chip)]
-        give[i] = out[me ^ (2 * chip + 1)]
+    for i, turn in enumerate(bundled):
+        mine[i] = out[device(me, count, turn, 0)]
+        give[i] = out[device(me, count, turn, 1)]
     for i, ref in enumerate(far):
-        ref[...] = out[me ^ (2 * direct[i // 2] + i % 2)]
+        ref[...] = out[device(me, count, direct[i // 2], i % 2)]
 
 
 def keep_kernel(held, *refs):
     out, sems = refs[-2:]
+    count = out.shape[1]
     me = lax.axis_index("en")
     copies = [
-        pltpu.make_async_copy(ref, out.at[:, me ^ (2 * chip + core), chunk], sems.at[i])
-        for i, (ref, chunk, chip, core) in enumerate(pieces_of(refs, held))
+        pltpu.make_async_copy(ref, out.at[:, device(me, count, -turn, core), chunk], sems.at[i])
+        for i, (ref, chunk, turn, core) in enumerate(pieces_of(refs, held))
     ]
     for copy in copies:
         copy.start()
@@ -247,10 +255,9 @@
 
 
 def plan(chips):
-    arrive = [(half, chip) for chip in range(chips - 1, -1, -1) for half in (1, 0)]
-    back = list(range(chips - 1, -1, -1))
-    cut = chips // 2
-    return arrive[: 2 * cut], arrive[2 * cut :], back[:cut], back[cut:]
+    turns = sorted(range(1, chips), key=lambda turn: (-min(turn, chips - turn), turn))
+    arrive = [(half, turn) for turn in turns for half in (1, 0)]
+    return arrive, [(1, 0), (0, 0)], list(range(1, chips)), [0]
 
 
 def body(lesser, greater, mirror):
@@ -287,10 +294,15 @@
             [in_vmem] * len(groups),
         )(*sum(pairs, ()))
 
-    def send(value, half, chip, core=0):
-        distance = half * count + 2 * chip + core
-        route = [(d, d ^ distance) for d in range(2 * count)]
-        return lax.ppermute(value, ("half", "en"), route) if distance else value
+    def send(value, half, turn, core=0):
+        if not half + turn + core:
+            return value
+        pairs = [(h, z, c) for h in range(2) for z in range(chips) for c in range(2)]
+        route = [
+            (h * count + 2 * z + c, (h ^ half) * count + 2 * ((z + turn) % chips) + (c ^ core))
+            for h, z, c in pairs
+        ]
+        return lax.ppermute(value, ("half", "en"), route)
 
     mirror, lesser, greater = (
         pltpu.with_memory_space_constraint(x, pltpu.HBM)

time: 59.6 us -> 55.3 us (0.928)
  waiting for transfers between devices: 20.9 us -> 16.1 us
    ppermute x3, waiting for transfers between devices: 2.77 us -> 0.01 us  [swap(): return lax.ppermute(give, 'en', [(e, e ^ 1) for e in range(count)])]
    ppermute x18 -> x21, waiting for transfers between devices: 18.2 us -> 16.1 us  [send(): return lax.ppermute(value, ('half', 'en'), route)]
    ppermute x18 -> x21, starting transfers between devices: 32.1 us -> 32.2 us  [send(): return lax.ppermute(value, ('half', 'en'), route)]
  transfers between devices with their start and end apart: 21 -> 24, of which waited for: 11 -> 8; matrix products, arithmetic and copies ran while one was open for 0% -> 0% of each run, Pallas kernels for 5% -> 6%
where the time goes in v1:
time: 55.3 us; the launch traced here: 54.8 us
  starting transfers between devices  32.9 us (59%)
  waiting for transfers between devices  16.1 us (29%)
  Pallas kernels  5.59 us (10%)
    ppermute x21, starting transfers between devices, send(): return lax.ppermute(value, ('half', 'en'), route)  32.2 us
    ppermute x21, waiting for transfers between devices, send(): return lax.ppermute(value, ('half', 'en'), route)  16.1 us
    pallas_call x2, Pallas kernels, body(): call(functools.partial(correlate_kernel, chunk, tuple((held[i] for i in u...  2.24 us
    pallas_call x1, Pallas kernels, body(): call(functools.partial(pack_kernel, units, alone), [stack(len(units))] *...  1.73 us
    pallas_call x2, Pallas kernels, body(): call(functools.partial(keep_kernel, blocks), tiled, [in_vmem] * len(value...  1.52 us
  transfers between devices with their start and end apart: 24, of which 8 were waited for; matrix products, arithmetic and copies ran while one was open for 0% of the time, Pallas kernels for 6%

profile of v1, /device:TPU:0, one launch (start us, length us, event | category | flops | bytes accessed | tf_op | source)
XLA Modules:
  0.0 54.8 jit_solution(4762809222077948271)
XLA Ops:
  0.0 1.7 %shard_map.64 = (f32[15,2,8,512]{3,2,1,0:T(8,128)S(1)}, f32[15,2,8,512]{3,2,1,0:T(8,128)S(1)}, f32[2,8,512]{2,1,0:T(8,128)S(1)}, f32[2,8,512]{2,1,0:T(8,128)S(1)}) custom-call(s32[1,128]{1,0:T(1,128)} %bitcast.6, f32[2,8,2,8,512]{4,3,2,1,0:T(8,128)} %bitcast.4, f32[2,8,2,8,512]{4,3,2,1,0:T(8,128)} %bitcast.5), custom_call_target="tpu_custom_call" | custom-call | tf_op jit(solution)/shard_map/pallas_call | solution.py:324
  1.7 0.6 %collective-permute-start = (f32[15,2,8,512]{3,2,1,0:T(8,128)S(1)}, f32[15,2,8,512]{3,2,1,0:T(8,128)S(1)}, u32[]{:S(2)}, u32[]{:S(2)}) collective-permute-start(f32[15,2,8,512]{3,2,1,0:T(8,128)S(1)} %get-tuple-element.35), channel_id=1, source_target_pairs={{0,1},{1,0},{2,3},{3,2},{4,5},{5,4},{6,7},{7,6},{8,9},{9,8},{10,11... | collective-permute-start | bytes 1474568 | tf_op jit(solution)/shard_map/ppermute | solution.py:286
  2.3 4.6 %collective-permute-start.10 = (f32[2,8,512]{2,1,0:T(8,128)S(1)}, f32[2,8,512]{2,1,0:T(8,128)S(1)}, u32[]{:S(2)}, u32[]{:S(2)}) collective-permute-start(f32[2,8,512]{2,1,0:T(8,128)S(1)} %get-tuple-element.46), channel_id=1, source_target_pairs={{0,20},{1,21},{2,22},{3,23},{4,16},{5,17},{6,18},{7,19},{16,4},{17... | collective-permute-start | bytes 98312 | tf_op jit(solution)/shard_map/ppermute | solution.py:305
  6.9 0.0 collective-permute-done.refs_1_
  6.9 0.0 copy-start
  6.9 0.0 copy-start.1
  6.9 0.0 copy-start.2
  6.9 0.1 shard_map.65
  7.0 1.8 %collective-permute-start.2 = (f32[2,2,8,512]{3,2,1,0:T(8,128)S(1)}, f32[2,2,8,512]{3,2,1,0:T(8,128)S(1)}, u32[]{:S(2)}, u32[]{:S(2)}) collective-permute-start(f32[2,2,8,512]{3,2,1,0:T(8,128)S(1)} %get-tuple-element.38), channel_id=1, source_target_pairs={{0,20},{1,21},{2,22},{3,23},{4,16},{5,17},{6,18},{7,19},{16,4},{17... | collective-permute-start | bytes 196616 | tf_op jit(solution)/shard_map/ppermute | solution.py:305
  8.8 1.1 %collective-permute-start.12 = (f32[2,2,8,512]{3,2,1,0:T(8,128)S(1)}, f32[2,2,8,512]{3,2,1,0:T(8,128)S(1)}, u32[]{:S(2)}, u32[]{:S(2)}) collective-permute-start(f32[2,2,8,512]{3,2,1,0:T(8,128)S(1)} %get-tuple-element.48), channel_id=1, source_target_pairs={{0,4},{1,5},{2,6},{3,7},{4,0},{5,1},{6,2},{7,3},{16,20},{17,21},{1... | collective-permute-start | bytes 196616 | tf_op jit(solution)/shard_map/ppermute | solution.py:305
  9.9 1.5 %collective-permute-start.1 = (f32[4,2,8,512]{3,2,1,0:T(8,128)S(1)}, f32[4,2,8,512]{3,2,1,0:T(8,128)S(1)}, u32[]{:S(2)}, u32[]{:S(2)}) collective-permute-start(f32[4,2,8,512]{3,2,1,0:T(8,128)S(1)} %get-tuple-element.36), channel_id=1, source_target_pairs={{0,16},{1,17},{2,18},{3,19},{4,20},{5,21},{6,22},{7,23},{16,0},{17... | collective-permute-start | bytes 393224 | tf_op jit(solution)/shard_map/ppermute | solution.py:305
  11.5 1.5 %collective-permute-start.13 = (f32[2,2,8,512]{3,2,1,0:T(8,128)S(1)}, f32[2,2,8,512]{3,2,1,0:T(8,128)S(1)}, u32[]{:S(2)}, u32[]{:S(2)}) collective-permute-start(f32[2,2,8,512]{3,2,1,0:T(8,128)S(1)} %get-tuple-element.49), channel_id=1, source_target_pairs={{0,18},{1,19},{2,20},{3,21},{4,22},{5,23},{6,16},{7,17},{16,2},{17... | collective-permute-start | bytes 196616 | tf_op jit(solution)/shard_map/ppermute | solution.py:305
  13.0 0.0 collective-permute-done.10.refs_0_
  13.0 0.4 collective-permute-start.11
  13.4 6.5 %collective-permute-done.11.refs_1_ = f32[2,8,512]{2,1,0:T(8,128)S(1)} collective-permute-done((f32[2,8,512]{2,1,0:T(8,128)S(1)}, f32[2,8,512]{2,1,0:T(8,128)S(1)}, u32[]{:S(2)}, u32[]{:S(2)}) %collective-permute-start.11) | collective-permute-done | bytes 32800 | tf_op jit(solution)/shard_map/ppermute | solution.py:305
  19.9 0.0 collective-permute-start.14
  19.9 0.0 collective-permute-done.2.refs_2_
  19.9 3.8 %collective-permute-start.15 = (f32[2,2,8,512]{3,2,1,0:T(8,128)S(1)}, f32[2,2,8,512]{3,2,1,0:T(8,128)S(1)}, u32[]{:S(2)}, u32[]{:S(2)}) collective-permute-start(f32[2,2,8,512]{3,2,1,0:T(8,128)S(1)} %get-tuple-element.51), channel_id=1, source_target_pairs={{0,22},{1,23},{2,16},{3,17},{4,18},{5,19},{6,20},{7,21},{16,6},{17... | collective-permute-start | bytes 196616 | tf_op jit(solution)/shard_map/ppermute | solution.py:305
  23.7 0.0 collective-permute-done.12.refs_2_
  23.7 1.0 %collective-permute-start.16 = (f32[2,2,8,512]{3,2,1,0:T(8,128)S(1)}, f32[2,2,8,512]{3,2,1,0:T(8,128)S(1)}, u32[]{:S(2)}, u32[]{:S(2)}) collective-permute-start(f32[2,2,8,512]{3,2,1,0:T(8,128)S(1)} %get-tuple-element.52), channel_id=1, source_target_pairs={{0,6},{1,7},{2,0},{3,1},{4,2},{5,3},{6,4},{7,5},{16,22},{17,23},{1... | collective-permute-start | bytes 196616 | tf_op jit(solution)/shard_map/ppermute | solution.py:305
  24.7 0.0 collective-permute-done.13.refs_3_
  24.7 0.0 collective-permute-start.3
  24.7 1.9 %collective-permute-done.14.refs_4_ = f32[2,2,8,512]{3,2,1,0:T(8,128)S(1)} collective-permute-done((f32[2,2,8,512]{3,2,1,0:T(8,128)S(1)}, f32[2,2,8,512]{3,2,1,0:T(8,128)S(1)}, u32[]{:S(2)}, u32[]{:S(2)}) %collective-permute-start.14) | collective-permute-done | bytes 65568 | tf_op jit(solution)/shard_map/ppermute | solution.py:305
  26.6 0.1 collective-permute-start.4
  26.7 0.0 collective-permute-done.15.refs_5_
  26.7 1.5 %collective-permute-start.5 = (f32[2,2,8,512]{3,2,1,0:T(8,128)S(1)}, f32[2,2,8,512]{3,2,1,0:T(8,128)S(1)}, u32[]{:S(2)}, u32[]{:S(2)}) collective-permute-start(f32[2,2,8,512]{3,2,1,0:T(8,128)S(1)} %get-tuple-element.41), channel_id=1, source_target_pairs={{0,2},{1,3},{2,4},{3,5},{4,6},{5,7},{6,0},{7,1},{16,18},{17,19},{1... | collective-permute-start | bytes 196616 | tf_op jit(solution)/shard_map/ppermute | solution.py:305
  28.2 0.5 collective-permute-done.16.refs_6_
  28.7 4.1 %collective-permute-start.6 = (f32[2,2,8,512]{3,2,1,0:T(8,128)S(1)}, f32[2,2,8,512]{3,2,1,0:T(8,128)S(1)}, u32[]{:S(2)}, u32[]{:S(2)}) collective-permute-start(f32[2,2,8,512]{3,2,1,0:T(8,128)S(1)} %get-tuple-element.42), channel_id=1, source_target_pairs={{0,22},{1,23},{2,16},{3,17},{4,18},{5,19},{6,20},{7,21},{16,6},{17... | collective-permute-start | bytes 196616 | tf_op jit(solution)/shard_map/ppermute | solution.py:305
  32.8 0.0 collective-permute-done.1.refs_0_.refs_7_
  32.8 0.7 %collective-permute-start.7 = (f32[2,2,8,512]{3,2,1,0:T(8,128)S(1)}, f32[2,2,8,512]{3,2,1,0:T(8,128)S(1)}, u32[]{:S(2)}, u32[]{:S(2)}) collective-permute-start(f32[2,2,8,512]{3,2,1,0:T(8,128)S(1)} %get-tuple-element.43), channel_id=1, source_target_pairs={{0,6},{1,7},{2,0},{3,1},{4,2},{5,3},{6,4},{7,5},{16,22},{17,23},{1... | collective-permute-start | bytes 196616 | tf_op jit(solution)/shard_map/ppermute | solution.py:305
  33.5 0.0 copy-done
  33.5 0.0 copy-done.1
  33.5 0.0 copy-done.2
  33.5 1.1 %shard_map.67 = (f32[4,2,8,512]{3,2,1,0:T(8,128)S(1)}, f32[4,2,8,512]{3,2,1,0:T(8,128)S(1)}) custom-call(f32[2,8,512]{2,1,0:T(8,128)S(1)} %collective-permute-done.10.refs_0_, f32[2,8,512]{2,1,0:T(8,128)S(1)} %collective-permute-done.11.refs_1_, f32[2,2,8,512]{3,2,1,0:T(8,128)S(1)} %collective-permute-done.12.refs_2_, ...), custom_call_target="tpu_custom_call" | custom-call | flops 301989888 | bytes 4194304 | tf_op jit(solution)/shard_map/pallas_call | solution.py:353
  34.6 0.0 collective-permute-done.3.refs_3_
  34.6 0.1 collective-permute-start.17
  34.7 0.0 collective-permute-done.4.refs_4_
  34.7 0.0 collective-permute-done.5.refs_5_
  34.7 0.8 %collective-permute-done.6.refs_6_ = f32[2,2,8,512]{3,2,1,0:T(8,128)S(1)} collective-permute-done((f32[2,2,8,512]{3,2,1,0:T(8,128)S(1)}, f32[2,2,8,512]{3,2,1,0:T(8,128)S(1)}, u32[]{:S(2)}, u32[]{:S(2)}) %collective-permute-start.6) | collective-permute-done | bytes 65568 | tf_op jit(solution)/shard_map/ppermute | solution.py:305
  35.5 1.5 %collective-permute-done.7.refs_7_ = f32[2,2,8,512]{3,2,1,0:T(8,128)S(1)} collective-permute-done((f32[2,2,8,512]{3,2,1,0:T(8,128)S(1)}, f32[2,2,8,512]{3,2,1,0:T(8,128)S(1)}, u32[]{:S(2)}, u32[]{:S(2)}) %collective-permute-start.7) | collective-permute-done | bytes 65568 | tf_op jit(solution)/shard_map/ppermute | solution.py:305
  37.1 1.1 %shard_map.66 = (f32[3,2,8,512]{3,2,1,0:T(8,128)S(1)}, f32[3,2,8,512]{3,2,1,0:T(8,128)S(1)}, f32[2,8,512]{2,1,0:T(8,128)S(1)}, f32[2,8,512]{2,1,0:T(8,128)S(1)}) custom-call(f32[4,2,8,512]{3,2,1,0:T(8,128)S(1)} %collective-permute-done.1.refs_0_.refs_7_, f32[4,2,8,512]{3,2,1,0:T(8,128)S(1)} %get-tuple-element.37.refs_1_.refs_8_, ...), custom_call_target="tpu_custom_call" | custom-call | flops 301989888 | bytes 4194304 | tf_op jit(solution)/shard_map/pallas_call | solution.py:353
  38.2 0.1 collective-permute-start.18
  38.3 0.0 collective-permute-done.17.refs_1_
  38.3 0.1 collective-permute-start.21
  38.4 3.0 %collective-permute-start.22 = (f32[2,2,8,512]{3,2,1,0:T(8,128)S(1)}, f32[2,2,8,512]{3,2,1,0:T(8,128)S(1)}, u32[]{:S(2)}, u32[]{:S(2)}) collective-permute-start(f32[2,2,8,512]{3,2,1,0:T(8,128)S(1)} %get-tuple-element.61), channel_id=1, source_target_pairs={{0,4},{1,5},{2,6},{3,7},{4,0},{5,1},{6,2},{7,3},{16,20},{17,21},{1... | collective-permute-start | bytes 196616 | tf_op jit(solution)/shard_map/ppermute | solution.py:305
  41.4 0.8 %collective-permute-start.23 = (f32[2,2,8,512]{3,2,1,0:T(8,128)S(1)}, f32[2,2,8,512]{3,2,1,0:T(8,128)S(1)}, u32[]{:S(2)}, u32[]{:S(2)}) collective-permute-start(f32[2,2,8,512]{3,2,1,0:T(8,128)S(1)} %get-tuple-element.62), channel_id=1, source_target_pairs={{0,6},{1,7},{2,0},{3,1},{4,2},{5,3},{6,4},{7,5},{16,22},{17,23},{1... | collective-permute-start | bytes 196616 | tf_op jit(solution)/shard_map/ppermute | solution.py:305
  42.2 0.0 collective-permute-done.18.refs_3_
  42.2 2.1 %collective-permute-start.19 = (f32[2,2,8,512]{3,2,1,0:T(8,128)S(1)}, f32[2,2,8,512]{3,2,1,0:T(8,128)S(1)}, u32[]{:S(2)}, u32[]{:S(2)}) collective-permute-start(f32[2,2,8,512]{3,2,1,0:T(8,128)S(1)} %get-tuple-element.57), channel_id=1, source_target_pairs={{0,4},{1,5},{2,6},{3,7},{4,0},{5,1},{6,2},{7,3},{16,20},{17,21},{1... | collective-permute-start | bytes 196616 | tf_op jit(solution)/shard_map/ppermute | solution.py:305
  44.3 1.6 %collective-permute-start.20 = (f32[2,2,8,512]{3,2,1,0:T(8,128)S(1)}, f32[2,2,8,512]{3,2,1,0:T(8,128)S(1)}, u32[]{:S(2)}, u32[]{:S(2)}) collective-permute-start(f32[2,2,8,512]{3,2,1,0:T(8,128)S(1)} %get-tuple-element.58), channel_id=1, source_target_pairs={{0,6},{1,7},{2,0},{3,1},{4,2},{5,3},{6,4},{7,5},{16,22},{17,23},{1... | collective-permute-start | bytes 196616 | tf_op jit(solution)/shard_map/ppermute | solution.py:305
  45.9 0.0 collective-permute-done.21.refs_0_
  45.9 0.4 collective-permute-start.8
  46.3 1.0 %collective-permute-done.22.refs_1_ = f32[2,2,8,512]{3,2,1,0:T(8,128)S(1)} collective-permute-done((f32[2,2,8,512]{3,2,1,0:T(8,128)S(1)}, f32[2,2,8,512]{3,2,1,0:T(8,128)S(1)}, u32[]{:S(2)}, u32[]{:S(2)}) %collective-permute-start.22) | collective-permute-done | bytes 65568 | tf_op jit(solution)/shard_map/ppermute | solution.py:305
  47.3 2.1 %collective-permute-start.9 = (f32[2,8,512]{2,1,0:T(8,128)S(1)}, f32[2,8,512]{2,1,0:T(8,128)S(1)}, u32[]{:S(2)}, u32[]{:S(2)}) collective-permute-start(f32[2,8,512]{2,1,0:T(8,128)S(1)} %get-tuple-element.45), channel_id=1, source_target_pairs={{0,3},{1,2},{2,5},{3,4},{4,7},{5,6},{6,1},{7,0},{16,19},{17,18},{1... | collective-permute-start | bytes 98312 | tf_op jit(solution)/shard_map/ppermute | solution.py:305
  49.4 0.0 collective-permute-done.23.refs_2_
  49.4 0.7 %shard_map.70.refs_5_ = f32[2,8,2,8,512]{4,3,2,1,0:T(8,128)} custom-call(f32[2,2,8,512]{3,2,1,0:T(8,128)S(1)} %collective-permute-done.21.refs_0_, f32[2,2,8,512]{3,2,1,0:T(8,128)S(1)} %collective-permute-done.22.refs_1_, f32[2,2,8,512]{3,2,1,0:T(8,128)S(1)} %collective-permute-done.23.refs_2_), custom_call_target="tpu_custom_call" | custom-call | tf_op jit(solution)/shard_map/pallas_call | solution.py:397
  50.1 1.6 %collective-permute-done.8.refs_0_ = f32[2,8,512]{2,1,0:T(8,128)S(1)} collective-permute-done((f32[2,8,512]{2,1,0:T(8,128)S(1)}, f32[2,8,512]{2,1,0:T(8,128)S(1)}, u32[]{:S(2)}, u32[]{:S(2)}) %collective-permute-start.8) | collective-permute-done | bytes 32800 | tf_op jit(solution)/shard_map/ppermute | solution.py:305
  51.7 2.3 %collective-permute-done.9.refs_1_ = f32[2,8,512]{2,1,0:T(8,128)S(1)} collective-permute-done((f32[2,8,512]{2,1,0:T(8,128)S(1)}, f32[2,8,512]{2,1,0:T(8,128)S(1)}, u32[]{:S(2)}, u32[]{:S(2)}) %collective-permute-start.9) | collective-permute-done | bytes 32800 | tf_op jit(solution)/shard_map/ppermute | solution.py:305
  54.0 0.0 collective-permute-done.19.refs_2_
  54.0 0.0 collective-permute-done.20.refs_3_
  54.0 0.8 %shard_map.71 = f32[2,8,2,8,512]{4,3,2,1,0:T(8,128)} custom-call(f32[2,8,512]{2,1,0:T(8,128)S(1)} %collective-permute-done.8.refs_0_, f32[2,8,512]{2,1,0:T(8,128)S(1)} %collective-permute-done.9.refs_1_, f32[2,2,8,512]{3,2,1,0:T(8,128)S(1)} %collective-permute-done.19.refs_2_, ...), custom_call_target="tpu_custom_call", output_to_operand_aliasing={{}: (5, {})} | custom-call | tf_op jit(solution)/shard_map/pallas_call | solution.py:397
  (2 shorter events, 0.0 us)
Async XLA Ops:
  1.7 5.2 %collective-permute-start = (f32[15,2,8,512]{3,2,1,0:T(8,128)S(1)}, f32[15,2,8,512]{3,2,1,0:T(8,128)S(1)}, u32[]{:S(2)}, u32[]{:S(2)}) collective-permute-start(f32[15,2,8,512]{3,2,1,0:T(8,128)S(1)} %get-tuple-element.35), channel_id=1, source_target_pairs={{0,1},{1,0},{2,3},{3,2},{4,5},{5,4},{6,7},{7,6},{8,9},{9,8},{10,11... | collective-permute-start | bytes 1474568 | tf_op jit(solution)/shard_map/ppermute | solution.py:286
  2.3 10.7 %collective-permute-start.10 = (f32[2,8,512]{2,1,0:T(8,128)S(1)}, f32[2,8,512]{2,1,0:T(8,128)S(1)}, u32[]{:S(2)}, u32[]{:S(2)}) collective-permute-start(f32[2,8,512]{2,1,0:T(8,128)S(1)} %get-tuple-element.46), channel_id=1, source_target_pairs={{0,20},{1,21},{2,22},{3,23},{4,16},{5,17},{6,18},{7,19},{16,4},{17... | collective-permute-start | bytes 98312 | tf_op jit(solution)/shard_map/ppermute | solution.py:305
  6.9 26.6 %copy-start = (bf16[2,256,256]{2,1,0:T(8,128)(2,1)S(1)}, bf16[2,256,256]{2,1,0:T(8,128)(2,1)}, u32[]{:S(2)}) copy-start(bf16[2,256,256]{2,1,0:T(8,128)(2,1)} %constant.7.clone.refs_9_.refs_10_) | copy-start | bytes 786436
  6.9 26.6 %copy-start.1 = (bf16[2,256,256]{2,1,0:T(8,128)(2,1)S(1)}, bf16[2,256,256]{2,1,0:T(8,128)(2,1)}, u32[]{:S(2)}) copy-start(bf16[2,256,256]{2,1,0:T(8,128)(2,1)} %constant.6.clone.refs_8_.refs_9_) | copy-start | bytes 786436
  6.9 26.6 %copy-start.2 = (f32[2,32,128]{2,1,0:T(8,128)S(1)}, f32[2,32,128]{2,1,0:T(8,128)}, u32[]{:S(2)}) copy-start(f32[2,32,128]{2,1,0:T(8,128)} %constant.8.clone.refs_10_.refs_11_) | copy-start | bytes 98308
  7.0 12.9 %collective-permute-start.2 = (f32[2,2,8,512]{3,2,1,0:T(8,128)S(1)}, f32[2,2,8,512]{3,2,1,0:T(8,128)S(1)}, u32[]{:S(2)}, u32[]{:S(2)}) collective-permute-start(f32[2,2,8,512]{3,2,1,0:T(8,128)S(1)} %get-tuple-element.38), channel_id=1, source_target_pairs={{0,20},{1,21},{2,22},{3,23},{4,16},{5,17},{6,18},{7,19},{16,4},{17... | collective-permute-start | bytes 196616 | tf_op jit(solution)/shard_map/ppermute | solution.py:305
  8.8 14.9 %collective-permute-start.12 = (f32[2,2,8,512]{3,2,1,0:T(8,128)S(1)}, f32[2,2,8,512]{3,2,1,0:T(8,128)S(1)}, u32[]{:S(2)}, u32[]{:S(2)}) collective-permute-start(f32[2,2,8,512]{3,2,1,0:T(8,128)S(1)} %get-tuple-element.48), channel_id=1, source_target_pairs={{0,4},{1,5},{2,6},{3,7},{4,0},{5,1},{6,2},{7,3},{16,20},{17,21},{1... | collective-permute-start | bytes 196616 | tf_op jit(solution)/shard_map/ppermute | solution.py:305
  9.9 22.9 %collective-permute-start.1 = (f32[4,2,8,512]{3,2,1,0:T(8,128)S(1)}, f32[4,2,8,512]{3,2,1,0:T(8,128)S(1)}, u32[]{:S(2)}, u32[]{:S(2)}) collective-permute-start(f32[4,2,8,512]{3,2,1,0:T(8,128)S(1)} %get-tuple-element.36), channel_id=1, source_target_pairs={{0,16},{1,17},{2,18},{3,19},{4,20},{5,21},{6,22},{7,23},{16,0},{17... | collective-permute-start | bytes 393224 | tf_op jit(solution)/shard_map/ppermute | solution.py:305
  11.5 13.2 %collective-permute-start.13 = (f32[2,2,8,512]{3,2,1,0:T(8,128)S(1)}, f32[2,2,8,512]{3,2,1,0:T(8,128)S(1)}, u32[]{:S(2)}, u32[]{:S(2)}) collective-permute-start(f32[2,2,8,512]{3,2,1,0:T(8,128)S(1)} %get-tuple-element.49), channel_id=1, source_target_pairs={{0,18},{1,19},{2,20},{3,21},{4,22},{5,23},{6,16},{7,17},{16,2},{17... | collective-permute-start | bytes 196616 | tf_op jit(solution)/shard_map/ppermute | solution.py:305
  13.0 6.9 %collective-permute-start.11 = (f32[2,8,512]{2,1,0:T(8,128)S(1)}, f32[2,8,512]{2,1,0:T(8,128)S(1)}, u32[]{:S(2)}, u32[]{:S(2)}) collective-permute-start(f32[2,8,512]{2,1,0:T(8,128)S(1)} %get-tuple-element.47), channel_id=1, source_target_pairs={{0,21},{1,20},{2,23},{3,22},{4,17},{5,16},{6,19},{7,18},{16,5},{17... | collective-permute-start | bytes 98312 | tf_op jit(solution)/shard_map/ppermute | solution.py:305
  19.9 6.8 %collective-permute-start.14 = (f32[2,2,8,512]{3,2,1,0:T(8,128)S(1)}, f32[2,2,8,512]{3,2,1,0:T(8,128)S(1)}, u32[]{:S(2)}, u32[]{:S(2)}) collective-permute-start(f32[2,2,8,512]{3,2,1,0:T(8,128)S(1)} %get-tuple-element.50), channel_id=1, source_target_pairs={{0,2},{1,3},{2,4},{3,5},{4,6},{5,7},{6,0},{7,1},{16,18},{17,19},{1... | collective-permute-start | bytes 196616 | tf_op jit(solution)/shard_map/ppermute | solution.py:305
  19.9 6.8 %collective-permute-start.15 = (f32[2,2,8,512]{3,2,1,0:T(8,128)S(1)}, f32[2,2,8,512]{3,2,1,0:T(8,128)S(1)}, u32[]{:S(2)}, u32[]{:S(2)}) collective-permute-start(f32[2,2,8,512]{3,2,1,0:T(8,128)S(1)} %get-tuple-element.51), channel_id=1, source_target_pairs={{0,22},{1,23},{2,16},{3,17},{4,18},{5,19},{6,20},{7,21},{16,6},{17... | collective-permute-start | bytes 196616 | tf_op jit(solution)/shard_map/ppermute | solution.py:305
  23.7 5.0 %collective-permute-start.16 = (f32[2,2,8,512]{3,2,1,0:T(8,128)S(1)}, f32[2,2,8,512]{3,2,1,0:T(8,128)S(1)}, u32[]{:S(2)}, u32[]{:S(2)}) collective-permute-start(f32[2,2,8,512]{3,2,1,0:T(8,128)S(1)} %get-tuple-element.52), channel_id=1, source_target_pairs={{0,6},{1,7},{2,0},{3,1},{4,2},{5,3},{6,4},{7,5},{16,22},{17,23},{1... | collective-permute-start | bytes 196616 | tf_op jit(solution)/shard_map/ppermute | solution.py:305
  24.7 9.9 %collective-permute-start.3 = (f32[2,2,8,512]{3,2,1,0:T(8,128)S(1)}, f32[2,2,8,512]{3,2,1,0:T(8,128)S(1)}, u32[]{:S(2)}, u32[]{:S(2)}) collective-permute-start(f32[2,2,8,512]{3,2,1,0:T(8,128)S(1)} %get-tuple-element.39), channel_id=1, source_target_pairs={{0,4},{1,5},{2,6},{3,7},{4,0},{5,1},{6,2},{7,3},{16,20},{17,21},{1... | collective-permute-start | bytes 196616 | tf_op jit(solution)/shard_map/ppermute | solution.py:305
  26.6 8.1 %collective-permute-start.4 = (f32[2,2,8,512]{3,2,1,0:T(8,128)S(1)}, f32[2,2,8,512]{3,2,1,0:T(8,128)S(1)}, u32[]{:S(2)}, u32[]{:S(2)}) collective-permute-start(f32[2,2,8,512]{3,2,1,0:T(8,128)S(1)} %get-tuple-element.40), channel_id=1, source_target_pairs={{0,18},{1,19},{2,20},{3,21},{4,22},{5,23},{6,16},{7,17},{16,2},{17... | collective-permute-start | bytes 196616 | tf_op jit(solution)/shard_map/ppermute | solution.py:305
  26.7 8.0 %collective-permute-start.5 = (f32[2,2,8,512]{3,2,1,0:T(8,128)S(1)}, f32[2,2,8,512]{3,2,1,0:T(8,128)S(1)}, u32[]{:S(2)}, u32[]{:S(2)}) collective-permute-start(f32[2,2,8,512]{3,2,1,0:T(8,128)S(1)} %get-tuple-element.41), channel_id=1, source_target_pairs={{0,2},{1,3},{2,4},{3,5},{4,6},{5,7},{6,0},{7,1},{16,18},{17,19},{1... | collective-permute-start | bytes 196616 | tf_op jit(solution)/shard_map/ppermute | solution.py:305
  28.7 6.9 %collective-permute-start.6 = (f32[2,2,8,512]{3,2,1,0:T(8,128)S(1)}, f32[2,2,8,512]{3,2,1,0:T(8,128)S(1)}, u32[]{:S(2)}, u32[]{:S(2)}) collective-permute-start(f32[2,2,8,512]{3,2,1,0:T(8,128)S(1)} %get-tuple-element.42), channel_id=1, source_target_pairs={{0,22},{1,23},{2,16},{3,17},{4,18},{5,19},{6,20},{7,21},{16,6},{17... | collective-permute-start | bytes 196616 | tf_op jit(solution)/shard_map/ppermute | solution.py:305
  32.8 4.3 %collective-permute-start.7 = (f32[2,2,8,512]{3,2,1,0:T(8,128)S(1)}, f32[2,2,8,512]{3,2,1,0:T(8,128)S(1)}, u32[]{:S(2)}, u32[]{:S(2)}) collective-permute-start(f32[2,2,8,512]{3,2,1,0:T(8,128)S(1)} %get-tuple-element.43), channel_id=1, source_target_pairs={{0,6},{1,7},{2,0},{3,1},{4,2},{5,3},{6,4},{7,5},{16,22},{17,23},{1... | collective-permute-start | bytes 196616 | tf_op jit(solution)/shard_map/ppermute | solution.py:305
  34.6 3.7 %collective-permute-start.17 = (f32[4,2,8,512]{3,2,1,0:T(8,128)S(1)}, f32[4,2,8,512]{3,2,1,0:T(8,128)S(1)}, u32[]{:S(2)}, u32[]{:S(2)}) collective-permute-start(f32[4,2,8,512]{3,2,1,0:T(8,128)S(1)} %get-tuple-element.54), channel_id=1, source_target_pairs={{0,1},{1,0},{2,3},{3,2},{4,5},{5,4},{6,7},{7,6},{8,9},{9,8},{10,11... | collective-permute-start | bytes 393224 | tf_op jit(solution)/shard_map/ppermute | solution.py:286
  38.2 4.0 %collective-permute-start.18 = (f32[3,2,8,512]{3,2,1,0:T(8,128)S(1)}, f32[3,2,8,512]{3,2,1,0:T(8,128)S(1)}, u32[]{:S(2)}, u32[]{:S(2)}) collective-permute-start(f32[3,2,8,512]{3,2,1,0:T(8,128)S(1)} %get-tuple-element.56), channel_id=1, source_target_pairs={{0,1},{1,0},{2,3},{3,2},{4,5},{5,4},{6,7},{7,6},{8,9},{9,8},{10,11... | collective-permute-start | bytes 294920 | tf_op jit(solution)/shard_map/ppermute | solution.py:286
  38.3 7.6 %collective-permute-start.21 = (f32[2,2,8,512]{3,2,1,0:T(8,128)S(1)}, f32[2,2,8,512]{3,2,1,0:T(8,128)S(1)}, u32[]{:S(2)}, u32[]{:S(2)}) collective-permute-start(f32[2,2,8,512]{3,2,1,0:T(8,128)S(1)} %get-tuple-element.60), channel_id=1, source_target_pairs={{0,2},{1,3},{2,4},{3,5},{4,6},{5,7},{6,0},{7,1},{16,18},{17,19},{1... | collective-permute-start | bytes 196616 | tf_op jit(solution)/shard_map/ppermute | solution.py:305
  38.4 9.0 %collective-permute-start.22 = (f32[2,2,8,512]{3,2,1,0:T(8,128)S(1)}, f32[2,2,8,512]{3,2,1,0:T(8,128)S(1)}, u32[]{:S(2)}, u32[]{:S(2)}) collective-permute-start(f32[2,2,8,512]{3,2,1,0:T(8,128)S(1)} %get-tuple-element.61), channel_id=1, source_target_pairs={{0,4},{1,5},{2,6},{3,7},{4,0},{5,1},{6,2},{7,3},{16,20},{17,21},{1... | collective-permute-start | bytes 196616 | tf_op jit(solution)/shard_map/ppermute | solution.py:305
  41.4 8.0 %collective-permute-start.23 = (f32[2,2,8,512]{3,2,1,0:T(8,128)S(1)}, f32[2,2,8,512]{3,2,1,0:T(8,128)S(1)}, u32[]{:S(2)}, u32[]{:S(2)}) collective-permute-start(f32[2,2,8,512]{3,2,1,0:T(8,128)S(1)} %get-tuple-element.62), channel_id=1, source_target_pairs={{0,6},{1,7},{2,0},{3,1},{4,2},{5,3},{6,4},{7,5},{16,22},{17,23},{1... | collective-permute-start | bytes 196616 | tf_op jit(solution)/shard_map/ppermute | solution.py:305
  42.2 11.8 %collective-permute-start.19 = (f32[2,2,8,512]{3,2,1,0:T(8,128)S(1)}, f32[2,2,8,512]{3,2,1,0:T(8,128)S(1)}, u32[]{:S(2)}, u32[]{:S(2)}) collective-permute-start(f32[2,2,8,512]{3,2,1,0:T(8,128)S(1)} %get-tuple-element.57), channel_id=1, source_target_pairs={{0,4},{1,5},{2,6},{3,7},{4,0},{5,1},{6,2},{7,3},{16,20},{17,21},{1... | collective-permute-start | bytes 196616 | tf_op jit(solution)/shard_map/ppermute | solution.py:305
  44.3 9.7 %collective-permute-start.20 = (f32[2,2,8,512]{3,2,1,0:T(8,128)S(1)}, f32[2,2,8,512]{3,2,1,0:T(8,128)S(1)}, u32[]{:S(2)}, u32[]{:S(2)}) collective-permute-start(f32[2,2,8,512]{3,2,1,0:T(8,128)S(1)} %get-tuple-element.58), channel_id=1, source_target_pairs={{0,6},{1,7},{2,0},{3,1},{4,2},{5,3},{6,4},{7,5},{16,22},{17,23},{1... | collective-permute-start | bytes 196616 | tf_op jit(solution)/shard_map/ppermute | solution.py:305
  45.9 5.8 %collective-permute-start.8 = (f32[2,8,512]{2,1,0:T(8,128)S(1)}, f32[2,8,512]{2,1,0:T(8,128)S(1)}, u32[]{:S(2)}, u32[]{:S(2)}) collective-permute-start(f32[2,8,512]{2,1,0:T(8,128)S(1)} %get-tuple-element.44), channel_id=1, source_target_pairs={{0,2},{1,3},{2,4},{3,5},{4,6},{5,7},{6,0},{7,1},{16,18},{17,19},{1... | collective-permute-start | bytes 98312 | tf_op jit(solution)/shard_map/ppermute | solution.py:305
  47.3 6.6 %collective-permute-start.9 = (f32[2,8,512]{2,1,0:T(8,128)S(1)}, f32[2,8,512]{2,1,0:T(8,128)S(1)}, u32[]{:S(2)}, u32[]{:S(2)}) collective-permute-start(f32[2,8,512]{2,1,0:T(8,128)S(1)} %get-tuple-element.45), channel_id=1, source_target_pairs={{0,3},{1,2},{2,5},{3,4},{4,7},{5,6},{6,1},{7,0},{16,19},{17,18},{1... | collective-permute-start | bytes 98312 | tf_op jit(solution)/shard_map/ppermute | solution.py:305

commit v2 on v1

--- a/solution.py
+++ b/solution.py
@@ -108,7 +108,7 @@
 
 
 def pack_kernel(units, alone, mirror, lesser, greater, mine, give, *refs):
-    *single, places, held, moved_rows, sems, block_sems = refs
+    *single, places, held, wanted, sems, block_sems = refs
     _, count, tiles, sub, local_len = lesser.shape
     rows = tiles * sub
     me = lax.axis_index("en")
@@ -131,27 +131,29 @@
     line = lax.broadcasted_iota(jnp.int32, (rows, count * rows), 0)
     goal = jnp.broadcast_to(places[...], (rows, count * rows)) % rows
     source = jnp.where(goal == line, (lane % rows).astype(jnp.float32), 0.0)
-    orders = [
-        jnp.sum(jnp.where(lane // rows == to, source, 0.0), axis=1, keepdims=True).astype(jnp.int32)
-        for to in range(count)
-    ]
+    for to in range(count):
+        share = jnp.where(lane // rows == to, source, 0.0)
+        order = jnp.sum(share, axis=1, keepdims=True).astype(jnp.int32)
+        wanted[to] = jnp.broadcast_to(order, (rows, LANES))
+    targets = {}
+    for ref, chunk, (half, turn), core in offers:
+        if half:
+            targets.setdefault((turn, core), {})[chunk] = ref
     for part in range(2):
         loads[1 + part].wait()
-        for to in range(count):
-            order = jnp.broadcast_to(orders[to], (rows, LANES))
+        for (turn, core), refs_of in targets.items():
+            to = device(me, count, turn, core)
+            order = wanted[to]
             for start in range(0, local_len, LANES):
                 span = slice(start, start + LANES)
                 tiles_in = [held[part, to, u, :, span] for u in range(tiles)]
-                for t in range(tiles):
-                    wanted = order[t * sub : (t + 1) * sub]
+                for t, ref in refs_of.items():
+                    want = order[t * sub : (t + 1) * sub]
                     moved = jnp.zeros((sub, LANES), jnp.float32)
                     for u, tile in enumerate(tiles_in):
-                        picked = jnp.take_along_axis(tile, wanted % sub, axis=0)
-                        moved = jnp.where(wanted // sub == u, picked, moved)
-                    moved_rows[t, to, part, :, span] = moved
-    for ref, chunk, (half, turn), core in offers:
-        if half:
-            ref[...] = moved_rows[chunk, device(me, count, turn, core)]
+                        picked = jnp.take_along_axis(tile, want % sub, axis=0)
+                        moved = jnp.where(want // sub == u, picked, moved)
+                    ref[part, :, span] = moved
     for copy in blocks:
         copy.wait()
 
@@ -254,10 +256,17 @@
     )
 
 
+FIRST_ORDER = ((0, 2), (1, 2), (0, 3), (0, 1), (1, 3), (1, 1))
+
+
+def ordered(values, order):
+    return [v for v in order if v in values] + [v for v in values if v not in order]
+
+
 def plan(chips):
     turns = sorted(range(1, chips), key=lambda turn: (-min(turn, chips - turn), turn))
     arrive = [(half, turn) for turn in turns for half in (1, 0)]
-    return arrive, [(1, 0), (0, 0)], list(range(1, chips)), [0]
+    return ordered(arrive, FIRST_ORDER), [(1, 0), (0, 0)], list(range(1, chips)), [0]
 
 
 def body(lesser, greater, mirror):
@@ -329,7 +338,7 @@
         [
             pltpu.VMEM((1, group_rows), jnp.int32),
             vmem(tiled),
-            pltpu.VMEM((tiles, count, *block.shape), f32),
+            pltpu.VMEM((count, rows, LANES), jnp.int32),
             dma((3,)),
             dma((2 * len(units) + len(alone),)),
         ],

time: 55.3 us -> 55.6 us (level)
  the two profiles are of different devices: /device:TPU:0 before, /device:TPU:1 now
where the time goes in v2:
time: 55.6 us; the launch traced here: 55.5 us
  starting transfers between devices  39.3 us (71%)
  waiting for transfers between devices  10.5 us (19%)
  Pallas kernels  5.62 us (10%)
    ppermute x21, starting transfers between devices, send(): return lax.ppermute(value, ('half', 'en'), route)  32.9 us
    ppermute x21, waiting for transfers between devices, send(): return lax.ppermute(value, ('half', 'en'), route)  10.5 us
    ppermute x3, starting transfers between devices, swap(): return lax.ppermute(give, 'en', [(e, e ^ 1) for e in range(count)])  6.39 us
    pallas_call x2, Pallas kernels, body(): call(functools.partial(correlate_kernel, chunk, tuple((held[i] for i in u...  2.24 us
    pallas_call x1, Pallas kernels, body(): call(functools.partial(pack_kernel, units, alone), [stack(len(units))] *...  1.76 us
    pallas_call x2, Pallas kernels, body(): call(functools.partial(keep_kernel, blocks), tiled, [in_vmem] * len(value...  1.52 us
  transfers between devices with their start and end apart: 24, of which 5 were waited for; matrix products, arithmetic and copies ran while one was open for 0% of the time, Pallas kernels for 6%

profile of v2, /device:TPU:1, one launch (start us, length us, event | category | flops | bytes accessed | tf_op | source)
XLA Modules:
  0.0 55.5 jit_solution(3478219480306093676)
XLA Ops:
  0.0 1.8 %shard_map.64 = (f32[15,2,8,512]{3,2,1,0:T(8,128)S(1)}, f32[15,2,8,512]{3,2,1,0:T(8,128)S(1)}, f32[2,8,512]{2,1,0:T(8,128)S(1)}, f32[2,8,512]{2,1,0:T(8,128)S(1)}) custom-call(s32[1,128]{1,0:T(1,128)} %bitcast.6, f32[2,8,2,8,512]{4,3,2,1,0:T(8,128)} %bitcast.4, f32[2,8,2,8,512]{4,3,2,1,0:T(8,128)} %bitcast.5), custom_call_target="tpu_custom_call" | custom-call | tf_op jit(solution)/shard_map/pallas_call | solution.py:333
  1.8 0.1 collective-permute-start
  1.8 3.8 %collective-permute-start.10 = (f32[2,8,512]{2,1,0:T(8,128)S(1)}, f32[2,8,512]{2,1,0:T(8,128)S(1)}, u32[]{:S(2)}, u32[]{:S(2)}) collective-permute-start(f32[2,8,512]{2,1,0:T(8,128)S(1)} %get-tuple-element.46), channel_id=1, source_target_pairs={{0,4},{1,5},{2,6},{3,7},{4,0},{5,1},{6,2},{7,3},{16,20},{17,21},{1... | collective-permute-start | bytes 98312 | tf_op jit(solution)/shard_map/ppermute | solution.py:314
  5.6 0.0 collective-permute-done.refs_1_
  5.6 0.0 copy-start
  5.6 0.0 copy-start.1
  5.6 0.0 copy-start.2
  5.6 0.1 shard_map.65
  5.7 1.5 %collective-permute-start.2 = (f32[2,2,8,512]{3,2,1,0:T(8,128)S(1)}, f32[2,2,8,512]{3,2,1,0:T(8,128)S(1)}, u32[]{:S(2)}, u32[]{:S(2)}) collective-permute-start(f32[2,2,8,512]{3,2,1,0:T(8,128)S(1)} %get-tuple-element.38), channel_id=1, source_target_pairs={{0,4},{1,5},{2,6},{3,7},{4,0},{5,1},{6,2},{7,3},{16,20},{17,21},{1... | collective-permute-start | bytes 196616 | tf_op jit(solution)/shard_map/ppermute | solution.py:314
  7.3 1.8 %collective-permute-start.12 = (f32[2,2,8,512]{3,2,1,0:T(8,128)S(1)}, f32[2,2,8,512]{3,2,1,0:T(8,128)S(1)}, u32[]{:S(2)}, u32[]{:S(2)}) collective-permute-start(f32[2,2,8,512]{3,2,1,0:T(8,128)S(1)} %get-tuple-element.48), channel_id=1, source_target_pairs={{0,20},{1,21},{2,22},{3,23},{4,16},{5,17},{6,18},{7,19},{16,4},{17... | collective-permute-start | bytes 196616 | tf_op jit(solution)/shard_map/ppermute | solution.py:314
  9.1 0.2 collective-permute-start.1
  9.3 2.5 %collective-permute-start.13 = (f32[2,2,8,512]{3,2,1,0:T(8,128)S(1)}, f32[2,2,8,512]{3,2,1,0:T(8,128)S(1)}, u32[]{:S(2)}, u32[]{:S(2)}) collective-permute-start(f32[2,2,8,512]{3,2,1,0:T(8,128)S(1)} %get-tuple-element.49), channel_id=1, source_target_pairs={{0,6},{1,7},{2,0},{3,1},{4,2},{5,3},{6,4},{7,5},{16,22},{17,23},{1... | collective-permute-start | bytes 196616 | tf_op jit(solution)/shard_map/ppermute | solution.py:314
  11.8 0.0 collective-permute-done.10.refs_0_
  11.8 1.4 %collective-permute-start.11 = (f32[2,8,512]{2,1,0:T(8,128)S(1)}, f32[2,8,512]{2,1,0:T(8,128)S(1)}, u32[]{:S(2)}, u32[]{:S(2)}) collective-permute-start(f32[2,8,512]{2,1,0:T(8,128)S(1)} %get-tuple-element.47), channel_id=1, source_target_pairs={{0,5},{1,4},{2,7},{3,6},{4,1},{5,0},{6,3},{7,2},{16,21},{17,20},{1... | collective-permute-start | bytes 98312 | tf_op jit(solution)/shard_map/ppermute | solution.py:314
  13.2 4.5 %collective-permute-done.11.refs_1_ = f32[2,8,512]{2,1,0:T(8,128)S(1)} collective-permute-done((f32[2,8,512]{2,1,0:T(8,128)S(1)}, f32[2,8,512]{2,1,0:T(8,128)S(1)}, u32[]{:S(2)}, u32[]{:S(2)}) %collective-permute-start.11) | collective-permute-done | bytes 32800 | tf_op jit(solution)/shard_map/ppermute | solution.py:314
  17.6 0.0 collective-permute-start.14
  17.6 0.0 collective-permute-done.2.refs_2_
  17.7 4.2 %collective-permute-start.15 = (f32[2,2,8,512]{3,2,1,0:T(8,128)S(1)}, f32[2,2,8,512]{3,2,1,0:T(8,128)S(1)}, u32[]{:S(2)}, u32[]{:S(2)}) collective-permute-start(f32[2,2,8,512]{3,2,1,0:T(8,128)S(1)} %get-tuple-element.51), channel_id=1, source_target_pairs={{0,22},{1,23},{2,16},{3,17},{4,18},{5,19},{6,20},{7,21},{16,6},{17... | collective-permute-start | bytes 196616 | tf_op jit(solution)/shard_map/ppermute | solution.py:314
  21.9 0.0 collective-permute-done.12.refs_2_
  21.9 0.0 collective-permute-start.16
  21.9 0.0 collective-permute-done.13.refs_3_
  21.9 1.8 %collective-permute-start.3 = (f32[2,2,8,512]{3,2,1,0:T(8,128)S(1)}, f32[2,2,8,512]{3,2,1,0:T(8,128)S(1)}, u32[]{:S(2)}, u32[]{:S(2)}) collective-permute-start(f32[2,2,8,512]{3,2,1,0:T(8,128)S(1)} %get-tuple-element.39), channel_id=1, source_target_pairs={{0,20},{1,21},{2,22},{3,23},{4,16},{5,17},{6,18},{7,19},{16,4},{17... | collective-permute-start | bytes 196616 | tf_op jit(solution)/shard_map/ppermute | solution.py:314
  23.7 0.0 collective-permute-done.14.refs_4_
  23.7 1.5 %collective-permute-start.4 = (f32[2,2,8,512]{3,2,1,0:T(8,128)S(1)}, f32[2,2,8,512]{3,2,1,0:T(8,128)S(1)}, u32[]{:S(2)}, u32[]{:S(2)}) collective-permute-start(f32[2,2,8,512]{3,2,1,0:T(8,128)S(1)} %get-tuple-element.40), channel_id=1, source_target_pairs={{0,6},{1,7},{2,0},{3,1},{4,2},{5,3},{6,4},{7,5},{16,22},{17,23},{1... | collective-permute-start | bytes 196616 | tf_op jit(solution)/shard_map/ppermute | solution.py:314
  25.1 0.0 collective-permute-done.15.refs_5_
  25.1 1.2 %collective-permute-start.5 = (f32[2,2,8,512]{3,2,1,0:T(8,128)S(1)}, f32[2,2,8,512]{3,2,1,0:T(8,128)S(1)}, u32[]{:S(2)}, u32[]{:S(2)}) collective-permute-start(f32[2,2,8,512]{3,2,1,0:T(8,128)S(1)} %get-tuple-element.41), channel_id=1, source_target_pairs={{0,2},{1,3},{2,4},{3,5},{4,6},{5,7},{6,0},{7,1},{16,18},{17,19},{1... | collective-permute-start | bytes 196616 | tf_op jit(solution)/shard_map/ppermute | solution.py:314
  26.4 1.4 %collective-permute-done.16.refs_6_ = f32[2,2,8,512]{3,2,1,0:T(8,128)S(1)} collective-permute-done((f32[2,2,8,512]{3,2,1,0:T(8,128)S(1)}, f32[2,2,8,512]{3,2,1,0:T(8,128)S(1)}, u32[]{:S(2)}, u32[]{:S(2)}) %collective-permute-start.16) | collective-permute-done | bytes 65568 | tf_op jit(solution)/shard_map/ppermute | solution.py:314
  27.8 1.6 %collective-permute-start.6 = (f32[2,2,8,512]{3,2,1,0:T(8,128)S(1)}, f32[2,2,8,512]{3,2,1,0:T(8,128)S(1)}, u32[]{:S(2)}, u32[]{:S(2)}) collective-permute-start(f32[2,2,8,512]{3,2,1,0:T(8,128)S(1)} %get-tuple-element.42), channel_id=1, source_target_pairs={{0,22},{1,23},{2,16},{3,17},{4,18},{5,19},{6,20},{7,21},{16,6},{17... | collective-permute-start | bytes 196616 | tf_op jit(solution)/shard_map/ppermute | solution.py:314
  29.4 0.0 collective-permute-done.1.refs_0_.refs_7_
  29.4 0.8 %collective-permute-start.7 = (f32[2,2,8,512]{3,2,1,0:T(8,128)S(1)}, f32[2,2,8,512]{3,2,1,0:T(8,128)S(1)}, u32[]{:S(2)}, u32[]{:S(2)}) collective-permute-start(f32[2,2,8,512]{3,2,1,0:T(8,128)S(1)} %get-tuple-element.43), channel_id=1, source_target_pairs={{0,18},{1,19},{2,20},{3,21},{4,22},{5,23},{6,16},{7,17},{16,2},{17... | collective-permute-start | bytes 196616 | tf_op jit(solution)/shard_map/ppermute | solution.py:314
  30.1 0.0 copy-done
  30.1 0.0 copy-done.1
  30.1 0.0 copy-done.2
  30.1 1.1 %shard_map.67 = (f32[4,2,8,512]{3,2,1,0:T(8,128)S(1)}, f32[4,2,8,512]{3,2,1,0:T(8,128)S(1)}) custom-call(f32[2,8,512]{2,1,0:T(8,128)S(1)} %collective-permute-done.10.refs_0_, f32[2,8,512]{2,1,0:T(8,128)S(1)} %collective-permute-done.11.refs_1_, f32[2,2,8,512]{3,2,1,0:T(8,128)S(1)} %collective-permute-done.12.refs_2_, ...), custom_call_target="tpu_custom_call" | custom-call | flops 301989888 | bytes 4194304 | tf_op jit(solution)/shard_map/pallas_call | solution.py:362
  31.3 0.0 collective-permute-done.3.refs_3_
  31.3 3.2 %collective-permute-start.17 = (f32[4,2,8,512]{3,2,1,0:T(8,128)S(1)}, f32[4,2,8,512]{3,2,1,0:T(8,128)S(1)}, u32[]{:S(2)}, u32[]{:S(2)}) collective-permute-start(f32[4,2,8,512]{3,2,1,0:T(8,128)S(1)} %get-tuple-element.54), channel_id=1, source_target_pairs={{0,1},{1,0},{2,3},{3,2},{4,5},{5,4},{6,7},{7,6},{8,9},{9,8},{10,11... | collective-permute-start | bytes 393224 | tf_op jit(solution)/shard_map/ppermute | solution.py:295
  34.5 0.0 collective-permute-done.4.refs_4_
  34.5 0.0 collective-permute-done.5.refs_5_
  34.5 0.0 collective-permute-done.6.refs_6_
  34.5 0.8 %collective-permute-done.7.refs_7_ = f32[2,2,8,512]{3,2,1,0:T(8,128)S(1)} collective-permute-done((f32[2,2,8,512]{3,2,1,0:T(8,128)S(1)}, f32[2,2,8,512]{3,2,1,0:T(8,128)S(1)}, u32[]{:S(2)}, u32[]{:S(2)}) %collective-permute-start.7) | collective-permute-done | bytes 65568 | tf_op jit(solution)/shard_map/ppermute | solution.py:314
  35.3 1.1 %shard_map.66 = (f32[3,2,8,512]{3,2,1,0:T(8,128)S(1)}, f32[3,2,8,512]{3,2,1,0:T(8,128)S(1)}, f32[2,8,512]{2,1,0:T(8,128)S(1)}, f32[2,8,512]{2,1,0:T(8,128)S(1)}) custom-call(f32[4,2,8,512]{3,2,1,0:T(8,128)S(1)} %collective-permute-done.1.refs_0_.refs_7_, f32[4,2,8,512]{3,2,1,0:T(8,128)S(1)} %get-tuple-element.37.refs_1_.refs_8_, ...), custom_call_target="tpu_custom_call" | custom-call | flops 301989888 | bytes 4194304 | tf_op jit(solution)/shard_map/pallas_call | solution.py:362
  36.4 3.1 %collective-permute-start.18 = (f32[3,2,8,512]{3,2,1,0:T(8,128)S(1)}, f32[3,2,8,512]{3,2,1,0:T(8,128)S(1)}, u32[]{:S(2)}, u32[]{:S(2)}) collective-permute-start(f32[3,2,8,512]{3,2,1,0:T(8,128)S(1)} %get-tuple-element.56), channel_id=1, source_target_pairs={{0,1},{1,0},{2,3},{3,2},{4,5},{5,4},{6,7},{7,6},{8,9},{9,8},{10,11... | collective-permute-start | bytes 294920 | tf_op jit(solution)/shard_map/ppermute | solution.py:295
  39.5 0.0 collective-permute-done.17.refs_1_
  39.5 0.1 collective-permute-start.21
  39.6 0.1 collective-permute-start.22
  39.7 3.2 %collective-permute-start.23 = (f32[2,2,8,512]{3,2,1,0:T(8,128)S(1)}, f32[2,2,8,512]{3,2,1,0:T(8,128)S(1)}, u32[]{:S(2)}, u32[]{:S(2)}) collective-permute-start(f32[2,2,8,512]{3,2,1,0:T(8,128)S(1)} %get-tuple-element.62), channel_id=1, source_target_pairs={{0,6},{1,7},{2,0},{3,1},{4,2},{5,3},{6,4},{7,5},{16,22},{17,23},{1... | collective-permute-start | bytes 196616 | tf_op jit(solution)/shard_map/ppermute | solution.py:314
  42.8 0.0 collective-permute-done.18.refs_3_
  42.9 1.5 %collective-permute-start.19 = (f32[2,2,8,512]{3,2,1,0:T(8,128)S(1)}, f32[2,2,8,512]{3,2,1,0:T(8,128)S(1)}, u32[]{:S(2)}, u32[]{:S(2)}) collective-permute-start(f32[2,2,8,512]{3,2,1,0:T(8,128)S(1)} %get-tuple-element.57), channel_id=1, source_target_pairs={{0,4},{1,5},{2,6},{3,7},{4,0},{5,1},{6,2},{7,3},{16,20},{17,21},{1... | collective-permute-start | bytes 196616 | tf_op jit(solution)/shard_map/ppermute | solution.py:314
  44.4 0.9 %collective-permute-start.20 = (f32[2,2,8,512]{3,2,1,0:T(8,128)S(1)}, f32[2,2,8,512]{3,2,1,0:T(8,128)S(1)}, u32[]{:S(2)}, u32[]{:S(2)}) collective-permute-start(f32[2,2,8,512]{3,2,1,0:T(8,128)S(1)} %get-tuple-element.58), channel_id=1, source_target_pairs={{0,6},{1,7},{2,0},{3,1},{4,2},{5,3},{6,4},{7,5},{16,22},{17,23},{1... | collective-permute-start | bytes 196616 | tf_op jit(solution)/shard_map/ppermute | solution.py:314
  45.3 0.0 collective-permute-done.21.refs_0_
  45.3 0.6 %collective-permute-start.8 = (f32[2,8,512]{2,1,0:T(8,128)S(1)}, f32[2,8,512]{2,1,0:T(8,128)S(1)}, u32[]{:S(2)}, u32[]{:S(2)}) collective-permute-start(f32[2,8,512]{2,1,0:T(8,128)S(1)} %get-tuple-element.44), channel_id=1, source_target_pairs={{0,2},{1,3},{2,4},{3,5},{4,6},{5,7},{6,0},{7,1},{16,18},{17,19},{1... | collective-permute-start | bytes 98312 | tf_op jit(solution)/shard_map/ppermute | solution.py:314
  45.9 0.0 collective-permute-done.22.refs_1_
  45.9 4.3 %collective-permute-start.9 = (f32[2,8,512]{2,1,0:T(8,128)S(1)}, f32[2,8,512]{2,1,0:T(8,128)S(1)}, u32[]{:S(2)}, u32[]{:S(2)}) collective-permute-start(f32[2,8,512]{2,1,0:T(8,128)S(1)} %get-tuple-element.45), channel_id=1, source_target_pairs={{0,3},{1,2},{2,5},{3,4},{4,7},{5,6},{6,1},{7,0},{16,19},{17,18},{1... | collective-permute-start | bytes 98312 | tf_op jit(solution)/shard_map/ppermute | solution.py:314
  50.1 0.0 collective-permute-done.23.refs_2_
  50.1 0.7 %shard_map.70.refs_5_ = f32[2,8,2,8,512]{4,3,2,1,0:T(8,128)} custom-call(f32[2,2,8,512]{3,2,1,0:T(8,128)S(1)} %collective-permute-done.21.refs_0_, f32[2,2,8,512]{3,2,1,0:T(8,128)S(1)} %collective-permute-done.22.refs_1_, f32[2,2,8,512]{3,2,1,0:T(8,128)S(1)} %collective-permute-done.23.refs_2_), custom_call_target="tpu_custom_call" | custom-call | tf_op jit(solution)/shard_map/pallas_call | solution.py:406
  50.9 0.2 collective-permute-done.8.refs_0_
  51.1 3.6 %collective-permute-done.9.refs_1_ = f32[2,8,512]{2,1,0:T(8,128)S(1)} collective-permute-done((f32[2,8,512]{2,1,0:T(8,128)S(1)}, f32[2,8,512]{2,1,0:T(8,128)S(1)}, u32[]{:S(2)}, u32[]{:S(2)}) %collective-permute-start.9) | collective-permute-done | bytes 32800 | tf_op jit(solution)/shard_map/ppermute | solution.py:314
  54.7 0.0 collective-permute-done.19.refs_2_
  54.7 0.0 collective-permute-done.20.refs_3_
  54.7 0.8 %shard_map.71 = f32[2,8,2,8,512]{4,3,2,1,0:T(8,128)} custom-call(f32[2,8,512]{2,1,0:T(8,128)S(1)} %collective-permute-done.8.refs_0_, f32[2,8,512]{2,1,0:T(8,128)S(1)} %collective-permute-done.9.refs_1_, f32[2,2,8,512]{3,2,1,0:T(8,128)S(1)} %collective-permute-done.19.refs_2_, ...), custom_call_target="tpu_custom_call", output_to_operand_aliasing={{}: (5, {})} | custom-call | tf_op jit(solution)/shard_map/pallas_call | solution.py:406
  (2 shorter events, 0.0 us)
Async XLA Ops:
  1.8 3.9 %collective-permute-start = (f32[15,2,8,512]{3,2,1,0:T(8,128)S(1)}, f32[15,2,8,512]{3,2,1,0:T(8,128)S(1)}, u32[]{:S(2)}, u32[]{:S(2)}) collective-permute-start(f32[15,2,8,512]{3,2,1,0:T(8,128)S(1)} %get-tuple-element.35), channel_id=1, source_target_pairs={{0,1},{1,0},{2,3},{3,2},{4,5},{5,4},{6,7},{7,6},{8,9},{9,8},{10,11... | collective-permute-start | bytes 1474568 | tf_op jit(solution)/shard_map/ppermute | solution.py:295
  1.8 10.0 %collective-permute-start.10 = (f32[2,8,512]{2,1,0:T(8,128)S(1)}, f32[2,8,512]{2,1,0:T(8,128)S(1)}, u32[]{:S(2)}, u32[]{:S(2)}) collective-permute-start(f32[2,8,512]{2,1,0:T(8,128)S(1)} %get-tuple-element.46), channel_id=1, source_target_pairs={{0,4},{1,5},{2,6},{3,7},{4,0},{5,1},{6,2},{7,3},{16,20},{17,21},{1... | collective-permute-start | bytes 98312 | tf_op jit(solution)/shard_map/ppermute | solution.py:314
  5.6 24.5 %copy-start = (bf16[2,256,256]{2,1,0:T(8,128)(2,1)S(1)}, bf16[2,256,256]{2,1,0:T(8,128)(2,1)}, u32[]{:S(2)}) copy-start(bf16[2,256,256]{2,1,0:T(8,128)(2,1)} %constant.7.clone.refs_9_.refs_10_) | copy-start | bytes 786436
  5.6 24.5 %copy-start.1 = (bf16[2,256,256]{2,1,0:T(8,128)(2,1)S(1)}, bf16[2,256,256]{2,1,0:T(8,128)(2,1)}, u32[]{:S(2)}) copy-start(bf16[2,256,256]{2,1,0:T(8,128)(2,1)} %constant.6.clone.refs_8_.refs_9_) | copy-start | bytes 786436
  5.6 24.5 %copy-start.2 = (f32[2,32,128]{2,1,0:T(8,128)S(1)}, f32[2,32,128]{2,1,0:T(8,128)}, u32[]{:S(2)}) copy-start(f32[2,32,128]{2,1,0:T(8,128)} %constant.8.clone.refs_10_.refs_11_) | copy-start | bytes 98308
  5.7 11.9 %collective-permute-start.2 = (f32[2,2,8,512]{3,2,1,0:T(8,128)S(1)}, f32[2,2,8,512]{3,2,1,0:T(8,128)S(1)}, u32[]{:S(2)}, u32[]{:S(2)}) collective-permute-start(f32[2,2,8,512]{3,2,1,0:T(8,128)S(1)} %get-tuple-element.38), channel_id=1, source_target_pairs={{0,4},{1,5},{2,6},{3,7},{4,0},{5,1},{6,2},{7,3},{16,20},{17,21},{1... | collective-permute-start | bytes 196616 | tf_op jit(solution)/shard_map/ppermute | solution.py:314
  7.3 14.6 %collective-permute-start.12 = (f32[2,2,8,512]{3,2,1,0:T(8,128)S(1)}, f32[2,2,8,512]{3,2,1,0:T(8,128)S(1)}, u32[]{:S(2)}, u32[]{:S(2)}) collective-permute-start(f32[2,2,8,512]{3,2,1,0:T(8,128)S(1)} %get-tuple-element.48), channel_id=1, source_target_pairs={{0,20},{1,21},{2,22},{3,23},{4,16},{5,17},{6,18},{7,19},{16,4},{17... | collective-permute-start | bytes 196616 | tf_op jit(solution)/shard_map/ppermute | solution.py:314
  9.1 20.3 %collective-permute-start.1 = (f32[4,2,8,512]{3,2,1,0:T(8,128)S(1)}, f32[4,2,8,512]{3,2,1,0:T(8,128)S(1)}, u32[]{:S(2)}, u32[]{:S(2)}) collective-permute-start(f32[4,2,8,512]{3,2,1,0:T(8,128)S(1)} %get-tuple-element.36), channel_id=1, source_target_pairs={{0,16},{1,17},{2,18},{3,19},{4,20},{5,21},{6,22},{7,23},{16,0},{17... | collective-permute-start | bytes 393224 | tf_op jit(solution)/shard_map/ppermute | solution.py:314
  9.3 12.5 %collective-permute-start.13 = (f32[2,2,8,512]{3,2,1,0:T(8,128)S(1)}, f32[2,2,8,512]{3,2,1,0:T(8,128)S(1)}, u32[]{:S(2)}, u32[]{:S(2)}) collective-permute-start(f32[2,2,8,512]{3,2,1,0:T(8,128)S(1)} %get-tuple-element.49), channel_id=1, source_target_pairs={{0,6},{1,7},{2,0},{3,1},{4,2},{5,3},{6,4},{7,5},{16,22},{17,23},{1... | collective-permute-start | bytes 196616 | tf_op jit(solution)/shard_map/ppermute | solution.py:314
  11.8 5.8 %collective-permute-start.11 = (f32[2,8,512]{2,1,0:T(8,128)S(1)}, f32[2,8,512]{2,1,0:T(8,128)S(1)}, u32[]{:S(2)}, u32[]{:S(2)}) collective-permute-start(f32[2,8,512]{2,1,0:T(8,128)S(1)} %get-tuple-element.47), channel_id=1, source_target_pairs={{0,5},{1,4},{2,7},{3,6},{4,1},{5,0},{6,3},{7,2},{16,21},{17,20},{1... | collective-permute-start | bytes 98312 | tf_op jit(solution)/shard_map/ppermute | solution.py:314
  17.6 6.0 %collective-permute-start.14 = (f32[2,2,8,512]{3,2,1,0:T(8,128)S(1)}, f32[2,2,8,512]{3,2,1,0:T(8,128)S(1)}, u32[]{:S(2)}, u32[]{:S(2)}) collective-permute-start(f32[2,2,8,512]{3,2,1,0:T(8,128)S(1)} %get-tuple-element.50), channel_id=1, source_target_pairs={{0,2},{1,3},{2,4},{3,5},{4,6},{5,7},{6,0},{7,1},{16,18},{17,19},{1... | collective-permute-start | bytes 196616 | tf_op jit(solution)/shard_map/ppermute | solution.py:314
  17.7 7.5 %collective-permute-start.15 = (f32[2,2,8,512]{3,2,1,0:T(8,128)S(1)}, f32[2,2,8,512]{3,2,1,0:T(8,128)S(1)}, u32[]{:S(2)}, u32[]{:S(2)}) collective-permute-start(f32[2,2,8,512]{3,2,1,0:T(8,128)S(1)} %get-tuple-element.51), channel_id=1, source_target_pairs={{0,22},{1,23},{2,16},{3,17},{4,18},{5,19},{6,20},{7,21},{16,6},{17... | collective-permute-start | bytes 196616 | tf_op jit(solution)/shard_map/ppermute | solution.py:314
  21.9 5.9 %collective-permute-start.16 = (f32[2,2,8,512]{3,2,1,0:T(8,128)S(1)}, f32[2,2,8,512]{3,2,1,0:T(8,128)S(1)}, u32[]{:S(2)}, u32[]{:S(2)}) collective-permute-start(f32[2,2,8,512]{3,2,1,0:T(8,128)S(1)} %get-tuple-element.52), channel_id=1, source_target_pairs={{0,18},{1,19},{2,20},{3,21},{4,22},{5,23},{6,16},{7,17},{16,2},{17... | collective-permute-start | bytes 196616 | tf_op jit(solution)/shard_map/ppermute | solution.py:314
  21.9 9.4 %collective-permute-start.3 = (f32[2,2,8,512]{3,2,1,0:T(8,128)S(1)}, f32[2,2,8,512]{3,2,1,0:T(8,128)S(1)}, u32[]{:S(2)}, u32[]{:S(2)}) collective-permute-start(f32[2,2,8,512]{3,2,1,0:T(8,128)S(1)} %get-tuple-element.39), channel_id=1, source_target_pairs={{0,20},{1,21},{2,22},{3,23},{4,16},{5,17},{6,18},{7,19},{16,4},{17... | collective-permute-start | bytes 196616 | tf_op jit(solution)/shard_map/ppermute | solution.py:314
  23.7 10.8 %collective-permute-start.4 = (f32[2,2,8,512]{3,2,1,0:T(8,128)S(1)}, f32[2,2,8,512]{3,2,1,0:T(8,128)S(1)}, u32[]{:S(2)}, u32[]{:S(2)}) collective-permute-start(f32[2,2,8,512]{3,2,1,0:T(8,128)S(1)} %get-tuple-element.40), channel_id=1, source_target_pairs={{0,6},{1,7},{2,0},{3,1},{4,2},{5,3},{6,4},{7,5},{16,22},{17,23},{1... | collective-permute-start | bytes 196616 | tf_op jit(solution)/shard_map/ppermute | solution.py:314
  25.1 9.4 %collective-permute-start.5 = (f32[2,2,8,512]{3,2,1,0:T(8,128)S(1)}, f32[2,2,8,512]{3,2,1,0:T(8,128)S(1)}, u32[]{:S(2)}, u32[]{:S(2)}) collective-permute-start(f32[2,2,8,512]{3,2,1,0:T(8,128)S(1)} %get-tuple-element.41), channel_id=1, source_target_pairs={{0,2},{1,3},{2,4},{3,5},{4,6},{5,7},{6,0},{7,1},{16,18},{17,19},{1... | collective-permute-start | bytes 196616 | tf_op jit(solution)/shard_map/ppermute | solution.py:314
  27.8 6.8 %collective-permute-start.6 = (f32[2,2,8,512]{3,2,1,0:T(8,128)S(1)}, f32[2,2,8,512]{3,2,1,0:T(8,128)S(1)}, u32[]{:S(2)}, u32[]{:S(2)}) collective-permute-start(f32[2,2,8,512]{3,2,1,0:T(8,128)S(1)} %get-tuple-element.42), channel_id=1, source_target_pairs={{0,22},{1,23},{2,16},{3,17},{4,18},{5,19},{6,20},{7,21},{16,6},{17... | collective-permute-start | bytes 196616 | tf_op jit(solution)/shard_map/ppermute | solution.py:314
  29.4 5.9 %collective-permute-start.7 = (f32[2,2,8,512]{3,2,1,0:T(8,128)S(1)}, f32[2,2,8,512]{3,2,1,0:T(8,128)S(1)}, u32[]{:S(2)}, u32[]{:S(2)}) collective-permute-start(f32[2,2,8,512]{3,2,1,0:T(8,128)S(1)} %get-tuple-element.43), channel_id=1, source_target_pairs={{0,18},{1,19},{2,20},{3,21},{4,22},{5,23},{6,16},{7,17},{16,2},{17... | collective-permute-start | bytes 196616 | tf_op jit(solution)/shard_map/ppermute | solution.py:314
  31.3 8.2 %collective-permute-start.17 = (f32[4,2,8,512]{3,2,1,0:T(8,128)S(1)}, f32[4,2,8,512]{3,2,1,0:T(8,128)S(1)}, u32[]{:S(2)}, u32[]{:S(2)}) collective-permute-start(f32[4,2,8,512]{3,2,1,0:T(8,128)S(1)} %get-tuple-element.54), channel_id=1, source_target_pairs={{0,1},{1,0},{2,3},{3,2},{4,5},{5,4},{6,7},{7,6},{8,9},{9,8},{10,11... | collective-permute-start | bytes 393224 | tf_op jit(solution)/shard_map/ppermute | solution.py:295
  36.4 6.4 %collective-permute-start.18 = (f32[3,2,8,512]{3,2,1,0:T(8,128)S(1)}, f32[3,2,8,512]{3,2,1,0:T(8,128)S(1)}, u32[]{:S(2)}, u32[]{:S(2)}) collective-permute-start(f32[3,2,8,512]{3,2,1,0:T(8,128)S(1)} %get-tuple-element.56), channel_id=1, source_target_pairs={{0,1},{1,0},{2,3},{3,2},{4,5},{5,4},{6,7},{7,6},{8,9},{9,8},{10,11... | collective-permute-start | bytes 294920 | tf_op jit(solution)/shard_map/ppermute | solution.py:295
  39.5 5.8 %collective-permute-start.21 = (f32[2,2,8,512]{3,2,1,0:T(8,128)S(1)}, f32[2,2,8,512]{3,2,1,0:T(8,128)S(1)}, u32[]{:S(2)}, u32[]{:S(2)}) collective-permute-start(f32[2,2,8,512]{3,2,1,0:T(8,128)S(1)} %get-tuple-element.60), channel_id=1, source_target_pairs={{0,2},{1,3},{2,4},{3,5},{4,6},{5,7},{6,0},{7,1},{16,18},{17,19},{1... | collective-permute-start | bytes 196616 | tf_op jit(solution)/shard_map/ppermute | solution.py:314
  39.6 6.3 %collective-permute-start.22 = (f32[2,2,8,512]{3,2,1,0:T(8,128)S(1)}, f32[2,2,8,512]{3,2,1,0:T(8,128)S(1)}, u32[]{:S(2)}, u32[]{:S(2)}) collective-permute-start(f32[2,2,8,512]{3,2,1,0:T(8,128)S(1)} %get-tuple-element.61), channel_id=1, source_target_pairs={{0,4},{1,5},{2,6},{3,7},{4,0},{5,1},{6,2},{7,3},{16,20},{17,21},{1... | collective-permute-start | bytes 196616 | tf_op jit(solution)/shard_map/ppermute | solution.py:314
  39.7 10.5 %collective-permute-start.23 = (f32[2,2,8,512]{3,2,1,0:T(8,128)S(1)}, f32[2,2,8,512]{3,2,1,0:T(8,128)S(1)}, u32[]{:S(2)}, u32[]{:S(2)}) collective-permute-start(f32[2,2,8,512]{3,2,1,0:T(8,128)S(1)} %get-tuple-element.62), channel_id=1, source_target_pairs={{0,6},{1,7},{2,0},{3,1},{4,2},{5,3},{6,4},{7,5},{16,22},{17,23},{1... | collective-permute-start | bytes 196616 | tf_op jit(solution)/shard_map/ppermute | solution.py:314
  42.9 11.8 %collective-permute-start.19 = (f32[2,2,8,512]{3,2,1,0:T(8,128)S(1)}, f32[2,2,8,512]{3,2,1,0:T(8,128)S(1)}, u32[]{:S(2)}, u32[]{:S(2)}) collective-permute-start(f32[2,2,8,512]{3,2,1,0:T(8,128)S(1)} %get-tuple-element.57), channel_id=1, source_target_pairs={{0,4},{1,5},{2,6},{3,7},{4,0},{5,1},{6,2},{7,3},{16,20},{17,21},{1... | collective-permute-start | bytes 196616 | tf_op jit(solution)/shard_map/ppermute | solution.py:314
  44.4 10.3 %collective-permute-start.20 = (f32[2,2,8,512]{3,2,1,0:T(8,128)S(1)}, f32[2,2,8,512]{3,2,1,0:T(8,128)S(1)}, u32[]{:S(2)}, u32[]{:S(2)}) collective-permute-start(f32[2,2,8,512]{3,2,1,0:T(8,128)S(1)} %get-tuple-element.58), channel_id=1, source_target_pairs={{0,6},{1,7},{2,0},{3,1},{4,2},{5,3},{6,4},{7,5},{16,22},{17,23},{1... | collective-permute-start | bytes 196616 | tf_op jit(solution)/shard_map/ppermute | solution.py:314
  45.3 5.8 %collective-permute-start.8 = (f32[2,8,512]{2,1,0:T(8,128)S(1)}, f32[2,8,512]{2,1,0:T(8,128)S(1)}, u32[]{:S(2)}, u32[]{:S(2)}) collective-permute-start(f32[2,8,512]{2,1,0:T(8,128)S(1)} %get-tuple-element.44), channel_id=1, source_target_pairs={{0,2},{1,3},{2,4},{3,5},{4,6},{5,7},{6,0},{7,1},{16,18},{17,19},{1... | collective-permute-start | bytes 98312 | tf_op jit(solution)/shard_map/ppermute | solution.py:314
  45.9 8.8 %collective-permute-start.9 = (f32[2,8,512]{2,1,0:T(8,128)S(1)}, f32[2,8,512]{2,1,0:T(8,128)S(1)}, u32[]{:S(2)}, u32[]{:S(2)}) collective-permute-start(f32[2,8,512]{2,1,0:T(8,128)S(1)} %get-tuple-element.45), channel_id=1, source_target_pairs={{0,3},{1,2},{2,5},{3,4},{4,7},{5,6},{6,1},{7,0},{16,19},{17,18},{1... | collective-permute-start | bytes 98312 | tf_op jit(solution)/shard_map/ppermute | solution.py:314

commit v3 on v2

--- a/solution.py
+++ b/solution.py
@@ -354,7 +354,7 @@
         arrived.append(send(value, *t))
         held.append(tuple((*unit, core) for unit in group for core in range(2)))
 
-    kept, pairs, out = [], [], []
+    kept, pairs, keeps, out = [], [], [], []
     for chunk in chunks:
         direct = far_back[:1] if chunk == last else []
         bundled = far_back[len(direct) :] + near_back
@@ -401,6 +401,11 @@
             z = group[0][1]
             blocks = tuple((*unit, core) for unit in group for core in range(2))
             returned.append((send(value, 0, z), blocks))
+        stays = [one for one in returned if one[1][0][1] == 0]
+        leaves = [one for one in returned if one[1][0][1] != 0]
+        keeps.append(leaves)
+        keeps[0] += stays
+    for chunk, returned in enumerate(keeps):
         values, blocks = zip(*returned)
         out = [
             call(

time: 55.6 us -> 55.6 us (level)
  no operation moved by 1% of the time
where the time goes in v3:
time: 55.6 us; the launch traced here: 55.4 us
  starting transfers between devices  39.3 us (71%)
  waiting for transfers between devices  10.4 us (19%)
  Pallas kernels  5.62 us (10%)
    ppermute x21, starting transfers between devices, send(): return lax.ppermute(value, ('half', 'en'), route)  32.9 us
    ppermute x21, waiting for transfers between devices, send(): return lax.ppermute(value, ('half', 'en'), route)  10.4 us
    ppermute x3, starting transfers between devices, swap(): return lax.ppermute(give, 'en', [(e, e ^ 1) for e in range(count)])  6.39 us
    pallas_call x2, Pallas kernels, body(): call(functools.partial(correlate_kernel, chunk, tuple((held[i] for i in u...  2.24 us
    pallas_call x1, Pallas kernels, body(): call(functools.partial(pack_kernel, units, alone), [stack(len(units))] *...  1.76 us
    pallas_call x2, Pallas kernels, body(): call(functools.partial(keep_kernel, blocks), tiled, [in_vmem] * len(value...  1.52 us
  transfers between devices with their start and end apart: 24, of which 5 were waited for; matrix products, arithmetic and copies ran while one was open for 0% of the time, Pallas kernels for 6%

profile of v3, /device:TPU:1, one launch (start us, length us, event | category | flops | bytes accessed | tf_op | source)
XLA Modules:
  0.0 55.4 jit_solution(9307781977497841342)
XLA Ops:
  0.0 1.8 %shard_map.64 = (f32[15,2,8,512]{3,2,1,0:T(8,128)S(1)}, f32[15,2,8,512]{3,2,1,0:T(8,128)S(1)}, f32[2,8,512]{2,1,0:T(8,128)S(1)}, f32[2,8,512]{2,1,0:T(8,128)S(1)}) custom-call(s32[1,128]{1,0:T(1,128)} %bitcast.6, f32[2,8,2,8,512]{4,3,2,1,0:T(8,128)} %bitcast.4, f32[2,8,2,8,512]{4,3,2,1,0:T(8,128)} %bitcast.5), custom_call_target="tpu_custom_call" | custom-call | tf_op jit(solution)/shard_map/pallas_call | solution.py:333
  1.8 0.1 collective-permute-start
  1.8 3.8 %collective-permute-start.10 = (f32[2,8,512]{2,1,0:T(8,128)S(1)}, f32[2,8,512]{2,1,0:T(8,128)S(1)}, u32[]{:S(2)}, u32[]{:S(2)}) collective-permute-start(f32[2,8,512]{2,1,0:T(8,128)S(1)} %get-tuple-element.46), channel_id=1, source_target_pairs={{0,4},{1,5},{2,6},{3,7},{4,0},{5,1},{6,2},{7,3},{16,20},{17,21},{1... | collective-permute-start | bytes 98312 | tf_op jit(solution)/shard_map/ppermute | solution.py:314
  5.6 0.0 collective-permute-done.refs_1_
  5.6 0.0 copy-start
  5.6 0.0 copy-start.1
  5.6 0.0 copy-start.2
  5.6 0.1 shard_map.65
  5.7 1.5 %collective-permute-start.2 = (f32[2,2,8,512]{3,2,1,0:T(8,128)S(1)}, f32[2,2,8,512]{3,2,1,0:T(8,128)S(1)}, u32[]{:S(2)}, u32[]{:S(2)}) collective-permute-start(f32[2,2,8,512]{3,2,1,0:T(8,128)S(1)} %get-tuple-element.38), channel_id=1, source_target_pairs={{0,4},{1,5},{2,6},{3,7},{4,0},{5,1},{6,2},{7,3},{16,20},{17,21},{1... | collective-permute-start | bytes 196616 | tf_op jit(solution)/shard_map/ppermute | solution.py:314
  7.3 1.8 %collective-permute-start.12 = (f32[2,2,8,512]{3,2,1,0:T(8,128)S(1)}, f32[2,2,8,512]{3,2,1,0:T(8,128)S(1)}, u32[]{:S(2)}, u32[]{:S(2)}) collective-permute-start(f32[2,2,8,512]{3,2,1,0:T(8,128)S(1)} %get-tuple-element.48), channel_id=1, source_target_pairs={{0,20},{1,21},{2,22},{3,23},{4,16},{5,17},{6,18},{7,19},{16,4},{17... | collective-permute-start | bytes 196616 | tf_op jit(solution)/shard_map/ppermute | solution.py:314
  9.1 0.2 collective-permute-start.1
  9.3 2.5 %collective-permute-start.13 = (f32[2,2,8,512]{3,2,1,0:T(8,128)S(1)}, f32[2,2,8,512]{3,2,1,0:T(8,128)S(1)}, u32[]{:S(2)}, u32[]{:S(2)}) collective-permute-start(f32[2,2,8,512]{3,2,1,0:T(8,128)S(1)} %get-tuple-element.49), channel_id=1, source_target_pairs={{0,6},{1,7},{2,0},{3,1},{4,2},{5,3},{6,4},{7,5},{16,22},{17,23},{1... | collective-permute-start | bytes 196616 | tf_op jit(solution)/shard_map/ppermute | solution.py:314
  11.8 0.0 collective-permute-done.10.refs_0_
  11.8 1.4 %collective-permute-start.11 = (f32[2,8,512]{2,1,0:T(8,128)S(1)}, f32[2,8,512]{2,1,0:T(8,128)S(1)}, u32[]{:S(2)}, u32[]{:S(2)}) collective-permute-start(f32[2,8,512]{2,1,0:T(8,128)S(1)} %get-tuple-element.47), channel_id=1, source_target_pairs={{0,5},{1,4},{2,7},{3,6},{4,1},{5,0},{6,3},{7,2},{16,21},{17,20},{1... | collective-permute-start | bytes 98312 | tf_op jit(solution)/shard_map/ppermute | solution.py:314
  13.2 4.5 %collective-permute-done.11.refs_1_ = f32[2,8,512]{2,1,0:T(8,128)S(1)} collective-permute-done((f32[2,8,512]{2,1,0:T(8,128)S(1)}, f32[2,8,512]{2,1,0:T(8,128)S(1)}, u32[]{:S(2)}, u32[]{:S(2)}) %collective-permute-start.11) | collective-permute-done | bytes 32800 | tf_op jit(solution)/shard_map/ppermute | solution.py:314
  17.6 0.0 collective-permute-start.14
  17.6 0.0 collective-permute-done.2.refs_2_
  17.7 4.2 %collective-permute-start.15 = (f32[2,2,8,512]{3,2,1,0:T(8,128)S(1)}, f32[2,2,8,512]{3,2,1,0:T(8,128)S(1)}, u32[]{:S(2)}, u32[]{:S(2)}) collective-permute-start(f32[2,2,8,512]{3,2,1,0:T(8,128)S(1)} %get-tuple-element.51), channel_id=1, source_target_pairs={{0,22},{1,23},{2,16},{3,17},{4,18},{5,19},{6,20},{7,21},{16,6},{17... | collective-permute-start | bytes 196616 | tf_op jit(solution)/shard_map/ppermute | solution.py:314
  21.9 0.0 collective-permute-done.12.refs_2_
  21.9 0.0 collective-permute-start.16
  21.9 0.0 collective-permute-done.13.refs_3_
  21.9 1.8 %collective-permute-start.3 = (f32[2,2,8,512]{3,2,1,0:T(8,128)S(1)}, f32[2,2,8,512]{3,2,1,0:T(8,128)S(1)}, u32[]{:S(2)}, u32[]{:S(2)}) collective-permute-start(f32[2,2,8,512]{3,2,1,0:T(8,128)S(1)} %get-tuple-element.39), channel_id=1, source_target_pairs={{0,20},{1,21},{2,22},{3,23},{4,16},{5,17},{6,18},{7,19},{16,4},{17... | collective-permute-start | bytes 196616 | tf_op jit(solution)/shard_map/ppermute | solution.py:314
  23.7 0.0 collective-permute-done.14.refs_4_
  23.7 1.5 %collective-permute-start.4 = (f32[2,2,8,512]{3,2,1,0:T(8,128)S(1)}, f32[2,2,8,512]{3,2,1,0:T(8,128)S(1)}, u32[]{:S(2)}, u32[]{:S(2)}) collective-permute-start(f32[2,2,8,512]{3,2,1,0:T(8,128)S(1)} %get-tuple-element.40), channel_id=1, source_target_pairs={{0,6},{1,7},{2,0},{3,1},{4,2},{5,3},{6,4},{7,5},{16,22},{17,23},{1... | collective-permute-start | bytes 196616 | tf_op jit(solution)/shard_map/ppermute | solution.py:314
  25.1 0.0 collective-permute-done.15.refs_5_
  25.1 1.2 %collective-permute-start.5 = (f32[2,2,8,512]{3,2,1,0:T(8,128)S(1)}, f32[2,2,8,512]{3,2,1,0:T(8,128)S(1)}, u32[]{:S(2)}, u32[]{:S(2)}) collective-permute-start(f32[2,2,8,512]{3,2,1,0:T(8,128)S(1)} %get-tuple-element.41), channel_id=1, source_target_pairs={{0,2},{1,3},{2,4},{3,5},{4,6},{5,7},{6,0},{7,1},{16,18},{17,19},{1... | collective-permute-start | bytes 196616 | tf_op jit(solution)/shard_map/ppermute | solution.py:314
  26.4 1.4 %collective-permute-done.16.refs_6_ = f32[2,2,8,512]{3,2,1,0:T(8,128)S(1)} collective-permute-done((f32[2,2,8,512]{3,2,1,0:T(8,128)S(1)}, f32[2,2,8,512]{3,2,1,0:T(8,128)S(1)}, u32[]{:S(2)}, u32[]{:S(2)}) %collective-permute-start.16) | collective-permute-done | bytes 65568 | tf_op jit(solution)/shard_map/ppermute | solution.py:314
  27.8 1.6 %collective-permute-start.6 = (f32[2,2,8,512]{3,2,1,0:T(8,128)S(1)}, f32[2,2,8,512]{3,2,1,0:T(8,128)S(1)}, u32[]{:S(2)}, u32[]{:S(2)}) collective-permute-start(f32[2,2,8,512]{3,2,1,0:T(8,128)S(1)} %get-tuple-element.42), channel_id=1, source_target_pairs={{0,22},{1,23},{2,16},{3,17},{4,18},{5,19},{6,20},{7,21},{16,6},{17... | collective-permute-start | bytes 196616 | tf_op jit(solution)/shard_map/ppermute | solution.py:314
  29.4 0.0 collective-permute-done.1.refs_0_.refs_7_
  29.4 0.8 %collective-permute-start.7 = (f32[2,2,8,512]{3,2,1,0:T(8,128)S(1)}, f32[2,2,8,512]{3,2,1,0:T(8,128)S(1)}, u32[]{:S(2)}, u32[]{:S(2)}) collective-permute-start(f32[2,2,8,512]{3,2,1,0:T(8,128)S(1)} %get-tuple-element.43), channel_id=1, source_target_pairs={{0,18},{1,19},{2,20},{3,21},{4,22},{5,23},{6,16},{7,17},{16,2},{17... | collective-permute-start | bytes 196616 | tf_op jit(solution)/shard_map/ppermute | solution.py:314
  30.1 0.0 copy-done
  30.1 0.0 copy-done.1
  30.1 0.0 copy-done.2
  30.1 1.1 %shard_map.67 = (f32[4,2,8,512]{3,2,1,0:T(8,128)S(1)}, f32[4,2,8,512]{3,2,1,0:T(8,128)S(1)}) custom-call(f32[2,8,512]{2,1,0:T(8,128)S(1)} %collective-permute-done.10.refs_0_, f32[2,8,512]{2,1,0:T(8,128)S(1)} %collective-permute-done.11.refs_1_, f32[2,2,8,512]{3,2,1,0:T(8,128)S(1)} %collective-permute-done.12.refs_2_, ...), custom_call_target="tpu_custom_call" | custom-call | flops 301989888 | bytes 4194304 | tf_op jit(solution)/shard_map/pallas_call | solution.py:362
  31.3 0.0 collective-permute-done.3.refs_3_
  31.3 3.2 %collective-permute-start.17 = (f32[4,2,8,512]{3,2,1,0:T(8,128)S(1)}, f32[4,2,8,512]{3,2,1,0:T(8,128)S(1)}, u32[]{:S(2)}, u32[]{:S(2)}) collective-permute-start(f32[4,2,8,512]{3,2,1,0:T(8,128)S(1)} %get-tuple-element.54), channel_id=1, source_target_pairs={{0,1},{1,0},{2,3},{3,2},{4,5},{5,4},{6,7},{7,6},{8,9},{9,8},{10,11... | collective-permute-start | bytes 393224 | tf_op jit(solution)/shard_map/ppermute | solution.py:295
  34.5 0.0 collective-permute-done.4.refs_4_
  34.5 0.0 collective-permute-done.5.refs_5_
  34.5 0.0 collective-permute-done.6.refs_6_
  34.5 0.8 %collective-permute-done.7.refs_7_ = f32[2,2,8,512]{3,2,1,0:T(8,128)S(1)} collective-permute-done((f32[2,2,8,512]{3,2,1,0:T(8,128)S(1)}, f32[2,2,8,512]{3,2,1,0:T(8,128)S(1)}, u32[]{:S(2)}, u32[]{:S(2)}) %collective-permute-start.7) | collective-permute-done | bytes 65568 | tf_op jit(solution)/shard_map/ppermute | solution.py:314
  35.3 1.1 %shard_map.66 = (f32[3,2,8,512]{3,2,1,0:T(8,128)S(1)}, f32[3,2,8,512]{3,2,1,0:T(8,128)S(1)}, f32[2,8,512]{2,1,0:T(8,128)S(1)}, f32[2,8,512]{2,1,0:T(8,128)S(1)}) custom-call(f32[4,2,8,512]{3,2,1,0:T(8,128)S(1)} %collective-permute-done.1.refs_0_.refs_7_, f32[4,2,8,512]{3,2,1,0:T(8,128)S(1)} %get-tuple-element.37.refs_1_.refs_8_, ...), custom_call_target="tpu_custom_call" | custom-call | flops 301989888 | bytes 4194304 | tf_op jit(solution)/shard_map/pallas_call | solution.py:362
  36.4 3.1 %collective-permute-start.18 = (f32[3,2,8,512]{3,2,1,0:T(8,128)S(1)}, f32[3,2,8,512]{3,2,1,0:T(8,128)S(1)}, u32[]{:S(2)}, u32[]{:S(2)}) collective-permute-start(f32[3,2,8,512]{3,2,1,0:T(8,128)S(1)} %get-tuple-element.56), channel_id=1, source_target_pairs={{0,1},{1,0},{2,3},{3,2},{4,5},{5,4},{6,7},{7,6},{8,9},{9,8},{10,11... | collective-permute-start | bytes 294920 | tf_op jit(solution)/shard_map/ppermute | solution.py:295
  39.5 0.0 collective-permute-done.17.refs_1_
  39.5 0.1 collective-permute-start.21
  39.6 0.1 collective-permute-start.22
  39.7 3.2 %collective-permute-start.23 = (f32[2,2,8,512]{3,2,1,0:T(8,128)S(1)}, f32[2,2,8,512]{3,2,1,0:T(8,128)S(1)}, u32[]{:S(2)}, u32[]{:S(2)}) collective-permute-start(f32[2,2,8,512]{3,2,1,0:T(8,128)S(1)} %get-tuple-element.61), channel_id=1, source_target_pairs={{0,6},{1,7},{2,0},{3,1},{4,2},{5,3},{6,4},{7,5},{16,22},{17,23},{1... | collective-permute-start | bytes 196616 | tf_op jit(solution)/shard_map/ppermute | solution.py:314
  42.8 0.0 collective-permute-done.18.refs_3_
  42.9 1.5 %collective-permute-start.19 = (f32[2,2,8,512]{3,2,1,0:T(8,128)S(1)}, f32[2,2,8,512]{3,2,1,0:T(8,128)S(1)}, u32[]{:S(2)}, u32[]{:S(2)}) collective-permute-start(f32[2,2,8,512]{3,2,1,0:T(8,128)S(1)} %get-tuple-element.57), channel_id=1, source_target_pairs={{0,4},{1,5},{2,6},{3,7},{4,0},{5,1},{6,2},{7,3},{16,20},{17,21},{1... | collective-permute-start | bytes 196616 | tf_op jit(solution)/shard_map/ppermute | solution.py:314
  44.4 0.9 %collective-permute-start.20 = (f32[2,2,8,512]{3,2,1,0:T(8,128)S(1)}, f32[2,2,8,512]{3,2,1,0:T(8,128)S(1)}, u32[]{:S(2)}, u32[]{:S(2)}) collective-permute-start(f32[2,2,8,512]{3,2,1,0:T(8,128)S(1)} %get-tuple-element.58), channel_id=1, source_target_pairs={{0,6},{1,7},{2,0},{3,1},{4,2},{5,3},{6,4},{7,5},{16,22},{17,23},{1... | collective-permute-start | bytes 196616 | tf_op jit(solution)/shard_map/ppermute | solution.py:314
  45.3 0.0 collective-permute-done.21.refs_0_
  45.3 0.6 %collective-permute-start.8 = (f32[2,8,512]{2,1,0:T(8,128)S(1)}, f32[2,8,512]{2,1,0:T(8,128)S(1)}, u32[]{:S(2)}, u32[]{:S(2)}) collective-permute-start(f32[2,8,512]{2,1,0:T(8,128)S(1)} %get-tuple-element.44), channel_id=1, source_target_pairs={{0,2},{1,3},{2,4},{3,5},{4,6},{5,7},{6,0},{7,1},{16,18},{17,19},{1... | collective-permute-start | bytes 98312 | tf_op jit(solution)/shard_map/ppermute | solution.py:314
  45.9 0.0 collective-permute-done.22.refs_1_
  45.9 4.3 %collective-permute-start.9 = (f32[2,8,512]{2,1,0:T(8,128)S(1)}, f32[2,8,512]{2,1,0:T(8,128)S(1)}, u32[]{:S(2)}, u32[]{:S(2)}) collective-permute-start(f32[2,8,512]{2,1,0:T(8,128)S(1)} %get-tuple-element.45), channel_id=1, source_target_pairs={{0,3},{1,2},{2,5},{3,4},{4,7},{5,6},{6,1},{7,0},{16,19},{17,18},{1... | collective-permute-start | bytes 98312 | tf_op jit(solution)/shard_map/ppermute | solution.py:314
  50.1 0.0 collective-permute-done.23.refs_2_
  50.1 0.8 %shard_map.70.refs_4_ = f32[2,8,2,8,512]{4,3,2,1,0:T(8,128)} custom-call(f32[2,2,8,512]{3,2,1,0:T(8,128)S(1)} %collective-permute-done.21.refs_0_, f32[2,2,8,512]{3,2,1,0:T(8,128)S(1)} %collective-permute-done.22.refs_1_, f32[2,2,8,512]{3,2,1,0:T(8,128)S(1)} %collective-permute-done.23.refs_2_, f32[4,2,8,512]{3,2,1,0:T(8,128)S(1)} %get-tuple-element.62.refs_3_), custom_call_target="tpu_custom_call" | custom-call | tf_op jit(solution)/shard_map/pallas_call | solution.py:411
  50.9 0.1 collective-permute-done.8.refs_0_
  51.1 3.6 %collective-permute-done.9.refs_1_ = f32[2,8,512]{2,1,0:T(8,128)S(1)} collective-permute-done((f32[2,8,512]{2,1,0:T(8,128)S(1)}, f32[2,8,512]{2,1,0:T(8,128)S(1)}, u32[]{:S(2)}, u32[]{:S(2)}) %collective-permute-start.9) | collective-permute-done | bytes 32800 | tf_op jit(solution)/shard_map/ppermute | solution.py:314
  54.7 0.0 collective-permute-done.19.refs_2_
  54.7 0.0 collective-permute-done.20.refs_3_
  54.7 0.7 %shard_map.71 = f32[2,8,2,8,512]{4,3,2,1,0:T(8,128)} custom-call(f32[2,8,512]{2,1,0:T(8,128)S(1)} %collective-permute-done.8.refs_0_, f32[2,8,512]{2,1,0:T(8,128)S(1)} %collective-permute-done.9.refs_1_, f32[2,2,8,512]{3,2,1,0:T(8,128)S(1)} %collective-permute-done.19.refs_2_, ...), custom_call_target="tpu_custom_call", output_to_operand_aliasing={{}: (4, {})} | custom-call | tf_op jit(solution)/shard_map/pallas_call | solution.py:411
  (2 shorter events, 0.0 us)
Async XLA Ops:
  1.8 3.9 %collective-permute-start = (f32[15,2,8,512]{3,2,1,0:T(8,128)S(1)}, f32[15,2,8,512]{3,2,1,0:T(8,128)S(1)}, u32[]{:S(2)}, u32[]{:S(2)}) collective-permute-start(f32[15,2,8,512]{3,2,1,0:T(8,128)S(1)} %get-tuple-element.35), channel_id=1, source_target_pairs={{0,1},{1,0},{2,3},{3,2},{4,5},{5,4},{6,7},{7,6},{8,9},{9,8},{10,11... | collective-permute-start | bytes 1474568 | tf_op jit(solution)/shard_map/ppermute | solution.py:295
  1.8 10.0 %collective-permute-start.10 = (f32[2,8,512]{2,1,0:T(8,128)S(1)}, f32[2,8,512]{2,1,0:T(8,128)S(1)}, u32[]{:S(2)}, u32[]{:S(2)}) collective-permute-start(f32[2,8,512]{2,1,0:T(8,128)S(1)} %get-tuple-element.46), channel_id=1, source_target_pairs={{0,4},{1,5},{2,6},{3,7},{4,0},{5,1},{6,2},{7,3},{16,20},{17,21},{1... | collective-permute-start | bytes 98312 | tf_op jit(solution)/shard_map/ppermute | solution.py:314
  5.6 24.5 %copy-start = (bf16[2,256,256]{2,1,0:T(8,128)(2,1)S(1)}, bf16[2,256,256]{2,1,0:T(8,128)(2,1)}, u32[]{:S(2)}) copy-start(bf16[2,256,256]{2,1,0:T(8,128)(2,1)} %constant.7.clone.refs_9_.refs_10_) | copy-start | bytes 786436
  5.6 24.5 %copy-start.1 = (bf16[2,256,256]{2,1,0:T(8,128)(2,1)S(1)}, bf16[2,256,256]{2,1,0:T(8,128)(2,1)}, u32[]{:S(2)}) copy-start(bf16[2,256,256]{2,1,0:T(8,128)(2,1)} %constant.6.clone.refs_8_.refs_9_) | copy-start | bytes 786436
  5.6 24.5 %copy-start.2 = (f32[2,32,128]{2,1,0:T(8,128)S(1)}, f32[2,32,128]{2,1,0:T(8,128)}, u32[]{:S(2)}) copy-start(f32[2,32,128]{2,1,0:T(8,128)} %constant.8.clone.refs_10_.refs_11_) | copy-start | bytes 98308
  5.7 11.9 %collective-permute-start.2 = (f32[2,2,8,512]{3,2,1,0:T(8,128)S(1)}, f32[2,2,8,512]{3,2,1,0:T(8,128)S(1)}, u32[]{:S(2)}, u32[]{:S(2)}) collective-permute-start(f32[2,2,8,512]{3,2,1,0:T(8,128)S(1)} %get-tuple-element.38), channel_id=1, source_target_pairs={{0,4},{1,5},{2,6},{3,7},{4,0},{5,1},{6,2},{7,3},{16,20},{17,21},{1... | collective-permute-start | bytes 196616 | tf_op jit(solution)/shard_map/ppermute | solution.py:314
  7.3 14.6 %collective-permute-start.12 = (f32[2,2,8,512]{3,2,1,0:T(8,128)S(1)}, f32[2,2,8,512]{3,2,1,0:T(8,128)S(1)}, u32[]{:S(2)}, u32[]{:S(2)}) collective-permute-start(f32[2,2,8,512]{3,2,1,0:T(8,128)S(1)} %get-tuple-element.48), channel_id=1, source_target_pairs={{0,20},{1,21},{2,22},{3,23},{4,16},{5,17},{6,18},{7,19},{16,4},{17... | collective-permute-start | bytes 196616 | tf_op jit(solution)/shard_map/ppermute | solution.py:314
  9.1 20.3 %collective-permute-start.1 = (f32[4,2,8,512]{3,2,1,0:T(8,128)S(1)}, f32[4,2,8,512]{3,2,1,0:T(8,128)S(1)}, u32[]{:S(2)}, u32[]{:S(2)}) collective-permute-start(f32[4,2,8,512]{3,2,1,0:T(8,128)S(1)} %get-tuple-element.36), channel_id=1, source_target_pairs={{0,16},{1,17},{2,18},{3,19},{4,20},{5,21},{6,22},{7,23},{16,0},{17... | collective-permute-start | bytes 393224 | tf_op jit(solution)/shard_map/ppermute | solution.py:314
  9.3 12.5 %collective-permute-start.13 = (f32[2,2,8,512]{3,2,1,0:T(8,128)S(1)}, f32[2,2,8,512]{3,2,1,0:T(8,128)S(1)}, u32[]{:S(2)}, u32[]{:S(2)}) collective-permute-start(f32[2,2,8,512]{3,2,1,0:T(8,128)S(1)} %get-tuple-element.49), channel_id=1, source_target_pairs={{0,6},{1,7},{2,0},{3,1},{4,2},{5,3},{6,4},{7,5},{16,22},{17,23},{1... | collective-permute-start | bytes 196616 | tf_op jit(solution)/shard_map/ppermute | solution.py:314
  11.8 5.8 %collective-permute-start.11 = (f32[2,8,512]{2,1,0:T(8,128)S(1)}, f32[2,8,512]{2,1,0:T(8,128)S(1)}, u32[]{:S(2)}, u32[]{:S(2)}) collective-permute-start(f32[2,8,512]{2,1,0:T(8,128)S(1)} %get-tuple-element.47), channel_id=1, source_target_pairs={{0,5},{1,4},{2,7},{3,6},{4,1},{5,0},{6,3},{7,2},{16,21},{17,20},{1... | collective-permute-start | bytes 98312 | tf_op jit(solution)/shard_map/ppermute | solution.py:314
  17.6 6.0 %collective-permute-start.14 = (f32[2,2,8,512]{3,2,1,0:T(8,128)S(1)}, f32[2,2,8,512]{3,2,1,0:T(8,128)S(1)}, u32[]{:S(2)}, u32[]{:S(2)}) collective-permute-start(f32[2,2,8,512]{3,2,1,0:T(8,128)S(1)} %get-tuple-element.50), channel_id=1, source_target_pairs={{0,2},{1,3},{2,4},{3,5},{4,6},{5,7},{6,0},{7,1},{16,18},{17,19},{1... | collective-permute-start | bytes 196616 | tf_op jit(solution)/shard_map/ppermute | solution.py:314
  17.7 7.5 %collective-permute-start.15 = (f32[2,2,8,512]{3,2,1,0:T(8,128)S(1)}, f32[2,2,8,512]{3,2,1,0:T(8,128)S(1)}, u32[]{:S(2)}, u32[]{:S(2)}) collective-permute-start(f32[2,2,8,512]{3,2,1,0:T(8,128)S(1)} %get-tuple-element.51), channel_id=1, source_target_pairs={{0,22},{1,23},{2,16},{3,17},{4,18},{5,19},{6,20},{7,21},{16,6},{17... | collective-permute-start | bytes 196616 | tf_op jit(solution)/shard_map/ppermute | solution.py:314
  21.9 5.9 %collective-permute-start.16 = (f32[2,2,8,512]{3,2,1,0:T(8,128)S(1)}, f32[2,2,8,512]{3,2,1,0:T(8,128)S(1)}, u32[]{:S(2)}, u32[]{:S(2)}) collective-permute-start(f32[2,2,8,512]{3,2,1,0:T(8,128)S(1)} %get-tuple-element.52), channel_id=1, source_target_pairs={{0,18},{1,19},{2,20},{3,21},{4,22},{5,23},{6,16},{7,17},{16,2},{17... | collective-permute-start | bytes 196616 | tf_op jit(solution)/shard_map/ppermute | solution.py:314
  21.9 9.4 %collective-permute-start.3 = (f32[2,2,8,512]{3,2,1,0:T(8,128)S(1)}, f32[2,2,8,512]{3,2,1,0:T(8,128)S(1)}, u32[]{:S(2)}, u32[]{:S(2)}) collective-permute-start(f32[2,2,8,512]{3,2,1,0:T(8,128)S(1)} %get-tuple-element.39), channel_id=1, source_target_pairs={{0,20},{1,21},{2,22},{3,23},{4,16},{5,17},{6,18},{7,19},{16,4},{17... | collective-permute-start | bytes 196616 | tf_op jit(solution)/shard_map/ppermute | solution.py:314
  23.7 10.8 %collective-permute-start.4 = (f32[2,2,8,512]{3,2,1,0:T(8,128)S(1)}, f32[2,2,8,512]{3,2,1,0:T(8,128)S(1)}, u32[]{:S(2)}, u32[]{:S(2)}) collective-permute-start(f32[2,2,8,512]{3,2,1,0:T(8,128)S(1)} %get-tuple-element.40), channel_id=1, source_target_pairs={{0,6},{1,7},{2,0},{3,1},{4,2},{5,3},{6,4},{7,5},{16,22},{17,23},{1... | collective-permute-start | bytes 196616 | tf_op jit(solution)/shard_map/ppermute | solution.py:314
  25.1 9.4 %collective-permute-start.5 = (f32[2,2,8,512]{3,2,1,0:T(8,128)S(1)}, f32[2,2,8,512]{3,2,1,0:T(8,128)S(1)}, u32[]{:S(2)}, u32[]{:S(2)}) collective-permute-start(f32[2,2,8,512]{3,2,1,0:T(8,128)S(1)} %get-tuple-element.41), channel_id=1, source_target_pairs={{0,2},{1,3},{2,4},{3,5},{4,6},{5,7},{6,0},{7,1},{16,18},{17,19},{1... | collective-permute-start | bytes 196616 | tf_op jit(solution)/shard_map/ppermute | solution.py:314
  27.8 6.8 %collective-permute-start.6 = (f32[2,2,8,512]{3,2,1,0:T(8,128)S(1)}, f32[2,2,8,512]{3,2,1,0:T(8,128)S(1)}, u32[]{:S(2)}, u32[]{:S(2)}) collective-permute-start(f32[2,2,8,512]{3,2,1,0:T(8,128)S(1)} %get-tuple-element.42), channel_id=1, source_target_pairs={{0,22},{1,23},{2,16},{3,17},{4,18},{5,19},{6,20},{7,21},{16,6},{17... | collective-permute-start | bytes 196616 | tf_op jit(solution)/shard_map/ppermute | solution.py:314
  29.4 5.9 %collective-permute-start.7 = (f32[2,2,8,512]{3,2,1,0:T(8,128)S(1)}, f32[2,2,8,512]{3,2,1,0:T(8,128)S(1)}, u32[]{:S(2)}, u32[]{:S(2)}) collective-permute-start(f32[2,2,8,512]{3,2,1,0:T(8,128)S(1)} %get-tuple-element.43), channel_id=1, source_target_pairs={{0,18},{1,19},{2,20},{3,21},{4,22},{5,23},{6,16},{7,17},{16,2},{17... | collective-permute-start | bytes 196616 | tf_op jit(solution)/shard_map/ppermute | solution.py:314
  31.3 8.2 %collective-permute-start.17 = (f32[4,2,8,512]{3,2,1,0:T(8,128)S(1)}, f32[4,2,8,512]{3,2,1,0:T(8,128)S(1)}, u32[]{:S(2)}, u32[]{:S(2)}) collective-permute-start(f32[4,2,8,512]{3,2,1,0:T(8,128)S(1)} %get-tuple-element.54), channel_id=1, source_target_pairs={{0,1},{1,0},{2,3},{3,2},{4,5},{5,4},{6,7},{7,6},{8,9},{9,8},{10,11... | collective-permute-start | bytes 393224 | tf_op jit(solution)/shard_map/ppermute | solution.py:295
  36.4 6.4 %collective-permute-start.18 = (f32[3,2,8,512]{3,2,1,0:T(8,128)S(1)}, f32[3,2,8,512]{3,2,1,0:T(8,128)S(1)}, u32[]{:S(2)}, u32[]{:S(2)}) collective-permute-start(f32[3,2,8,512]{3,2,1,0:T(8,128)S(1)} %get-tuple-element.56), channel_id=1, source_target_pairs={{0,1},{1,0},{2,3},{3,2},{4,5},{5,4},{6,7},{7,6},{8,9},{9,8},{10,11... | collective-permute-start | bytes 294920 | tf_op jit(solution)/shard_map/ppermute | solution.py:295
  39.5 5.8 %collective-permute-start.21 = (f32[2,2,8,512]{3,2,1,0:T(8,128)S(1)}, f32[2,2,8,512]{3,2,1,0:T(8,128)S(1)}, u32[]{:S(2)}, u32[]{:S(2)}) collective-permute-start(f32[2,2,8,512]{3,2,1,0:T(8,128)S(1)} %get-tuple-element.59), channel_id=1, source_target_pairs={{0,2},{1,3},{2,4},{3,5},{4,6},{5,7},{6,0},{7,1},{16,18},{17,19},{1... | collective-permute-start | bytes 196616 | tf_op jit(solution)/shard_map/ppermute | solution.py:314
  39.6 6.3 %collective-permute-start.22 = (f32[2,2,8,512]{3,2,1,0:T(8,128)S(1)}, f32[2,2,8,512]{3,2,1,0:T(8,128)S(1)}, u32[]{:S(2)}, u32[]{:S(2)}) collective-permute-start(f32[2,2,8,512]{3,2,1,0:T(8,128)S(1)} %get-tuple-element.60), channel_id=1, source_target_pairs={{0,4},{1,5},{2,6},{3,7},{4,0},{5,1},{6,2},{7,3},{16,20},{17,21},{1... | collective-permute-start | bytes 196616 | tf_op jit(solution)/shard_map/ppermute | solution.py:314
  39.7 10.5 %collective-permute-start.23 = (f32[2,2,8,512]{3,2,1,0:T(8,128)S(1)}, f32[2,2,8,512]{3,2,1,0:T(8,128)S(1)}, u32[]{:S(2)}, u32[]{:S(2)}) collective-permute-start(f32[2,2,8,512]{3,2,1,0:T(8,128)S(1)} %get-tuple-element.61), channel_id=1, source_target_pairs={{0,6},{1,7},{2,0},{3,1},{4,2},{5,3},{6,4},{7,5},{16,22},{17,23},{1... | collective-permute-start | bytes 196616 | tf_op jit(solution)/shard_map/ppermute | solution.py:314
  42.9 11.8 %collective-permute-start.19 = (f32[2,2,8,512]{3,2,1,0:T(8,128)S(1)}, f32[2,2,8,512]{3,2,1,0:T(8,128)S(1)}, u32[]{:S(2)}, u32[]{:S(2)}) collective-permute-start(f32[2,2,8,512]{3,2,1,0:T(8,128)S(1)} %get-tuple-element.57), channel_id=1, source_target_pairs={{0,4},{1,5},{2,6},{3,7},{4,0},{5,1},{6,2},{7,3},{16,20},{17,21},{1... | collective-permute-start | bytes 196616 | tf_op jit(solution)/shard_map/ppermute | solution.py:314
  44.4 10.3 %collective-permute-start.20 = (f32[2,2,8,512]{3,2,1,0:T(8,128)S(1)}, f32[2,2,8,512]{3,2,1,0:T(8,128)S(1)}, u32[]{:S(2)}, u32[]{:S(2)}) collective-permute-start(f32[2,2,8,512]{3,2,1,0:T(8,128)S(1)} %get-tuple-element.58), channel_id=1, source_target_pairs={{0,6},{1,7},{2,0},{3,1},{4,2},{5,3},{6,4},{7,5},{16,22},{17,23},{1... | collective-permute-start | bytes 196616 | tf_op jit(solution)/shard_map/ppermute | solution.py:314
  45.3 5.8 %collective-permute-start.8 = (f32[2,8,512]{2,1,0:T(8,128)S(1)}, f32[2,8,512]{2,1,0:T(8,128)S(1)}, u32[]{:S(2)}, u32[]{:S(2)}) collective-permute-start(f32[2,8,512]{2,1,0:T(8,128)S(1)} %get-tuple-element.44), channel_id=1, source_target_pairs={{0,2},{1,3},{2,4},{3,5},{4,6},{5,7},{6,0},{7,1},{16,18},{17,19},{1... | collective-permute-start | bytes 98312 | tf_op jit(solution)/shard_map/ppermute | solution.py:314
  45.9 8.8 %collective-permute-start.9 = (f32[2,8,512]{2,1,0:T(8,128)S(1)}, f32[2,8,512]{2,1,0:T(8,128)S(1)}, u32[]{:S(2)}, u32[]{:S(2)}) collective-permute-start(f32[2,8,512]{2,1,0:T(8,128)S(1)} %get-tuple-element.45), channel_id=1, source_target_pairs={{0,3},{1,2},{2,5},{3,4},{4,7},{5,6},{6,1},{7,0},{16,19},{17,18},{1... | collective-permute-start | bytes 98312 | tf_op jit(solution)/shard_map/ppermute | solution.py:314

commit v4 on v2

--- a/solution.py
+++ b/solution.py
@@ -354,7 +354,7 @@
         arrived.append(send(value, *t))
         held.append(tuple((*unit, core) for unit in group for core in range(2)))
 
-    kept, pairs, out = [], [], []
+    kept, pairs, keeps, out = [], [], [], []
     for chunk in chunks:
         direct = far_back[:1] if chunk == last else []
         bundled = far_back[len(direct) :] + near_back
@@ -401,6 +401,10 @@
             z = group[0][1]
             blocks = tuple((*unit, core) for unit in group for core in range(2))
             returned.append((send(value, 0, z), blocks))
+        soon = [len(held_by) == 1 or held_by[0][1] == 0 for _, held_by in returned]
+        keeps.append([one for one, early in zip(returned, soon) if not early])
+        keeps[0] += [one for one, early in zip(returned, soon) if early]
+    for chunk, returned in enumerate(keeps):
         values, blocks = zip(*returned)
         out = [
             call(

time: 55.6 us -> 57.2 us (1.029)
  the two profiles are of different devices: /device:TPU:1 before, /device:TPU:0 now
where the time goes in v4:
time: 57.2 us; the launch traced here: 57.1 us
  starting transfers between devices  33.9 us (59%)
  waiting for transfers between devices  17.4 us (30%)
  Pallas kernels  5.61 us (10%)
    ppermute x21, starting transfers between devices, send(): return lax.ppermute(value, ('half', 'en'), route)  33.2 us
    ppermute x21, waiting for transfers between devices, send(): return lax.ppermute(value, ('half', 'en'), route)  15.9 us
    pallas_call x2, Pallas kernels, body(): call(functools.partial(correlate_kernel, chunk, tuple((held[i] for i in u...  2.24 us
    pallas_call x1, Pallas kernels, body(): call(functools.partial(pack_kernel, units, alone), [stack(len(units))] *...  1.76 us
    pallas_call x2, Pallas kernels, body(): call(functools.partial(keep_kernel, blocks), tiled, [in_vmem] * len(value...  1.52 us
    ppermute x3, waiting for transfers between devices, swap(): return lax.ppermute(give, 'en', [(e, e ^ 1) for e in range(count)])  1.5 us
  transfers between devices with their start and end apart: 24, of which 8 were waited for; matrix products, arithmetic and copies ran while one was open for 0% of the time, Pallas kernels for 5%

profile of v4, /device:TPU:0, one launch (start us, length us, event | category | flops | bytes accessed | tf_op | source)
XLA Modules:
  0.0 57.1 jit_solution(2330902477619674648)
XLA Ops:
  0.0 1.8 %shard_map.64 = (f32[15,2,8,512]{3,2,1,0:T(8,128)S(1)}, f32[15,2,8,512]{3,2,1,0:T(8,128)S(1)}, f32[2,8,512]{2,1,0:T(8,128)S(1)}, f32[2,8,512]{2,1,0:T(8,128)S(1)}) custom-call(s32[1,128]{1,0:T(1,128)} %bitcast.6, f32[2,8,2,8,512]{4,3,2,1,0:T(8,128)} %bitcast.4, f32[2,8,2,8,512]{4,3,2,1,0:T(8,128)} %bitcast.5), custom_call_target="tpu_custom_call" | custom-call | tf_op jit(solution)/shard_map/pallas_call | solution.py:333
  1.8 0.6 collective-permute-start.2
  2.3 1.5 %collective-permute-done.2.refs_1_ = f32[15,2,8,512]{3,2,1,0:T(8,128)S(1)} collective-permute-done((f32[15,2,8,512]{3,2,1,0:T(8,128)S(1)}, f32[15,2,8,512]{3,2,1,0:T(8,128)S(1)}, u32[]{:S(2)}, u32[]{:S(2)}) %collective-permute-start.2) | collective-permute-done | bytes 491552 | tf_op jit(solution)/shard_map/ppermute | solution.py:295
  3.8 0.0 copy-start
  3.8 0.0 copy-start.1
  3.8 0.0 copy-start.2
  3.8 0.1 shard_map.65
  3.9 5.0 %collective-permute-start.3 = (f32[2,2,8,512]{3,2,1,0:T(8,128)S(1)}, f32[2,2,8,512]{3,2,1,0:T(8,128)S(1)}, u32[]{:S(2)}, u32[]{:S(2)}) collective-permute-start(f32[2,2,8,512]{3,2,1,0:T(8,128)S(1)} %get-tuple-element.38), channel_id=1, source_target_pairs={{0,20},{1,21},{2,22},{3,23},{4,16},{5,17},{6,18},{7,19},{16,4},{17... | collective-permute-start | bytes 196616 | tf_op jit(solution)/shard_map/ppermute | solution.py:314
  8.9 1.3 %collective-permute-start.4 = (f32[2,2,8,512]{3,2,1,0:T(8,128)S(1)}, f32[2,2,8,512]{3,2,1,0:T(8,128)S(1)}, u32[]{:S(2)}, u32[]{:S(2)}) collective-permute-start(f32[2,2,8,512]{3,2,1,0:T(8,128)S(1)} %get-tuple-element.39), channel_id=1, source_target_pairs={{0,6},{1,7},{2,0},{3,1},{4,2},{5,3},{6,4},{7,5},{16,22},{17,23},{1... | collective-permute-start | bytes 196616 | tf_op jit(solution)/shard_map/ppermute | solution.py:314
  10.2 0.5 collective-permute-start.8
  10.7 1.7 %collective-permute-start = (f32[2,8,512]{2,1,0:T(8,128)S(1)}, f32[2,8,512]{2,1,0:T(8,128)S(1)}, u32[]{:S(2)}, u32[]{:S(2)}) collective-permute-start(f32[2,8,512]{2,1,0:T(8,128)S(1)} %get-tuple-element.34), channel_id=1, source_target_pairs={{0,4},{1,5},{2,6},{3,7},{4,0},{5,1},{6,2},{7,3},{16,20},{17,21},{1... | collective-permute-start | bytes 98312 | tf_op jit(solution)/shard_map/ppermute | solution.py:314
  12.4 0.0 collective-permute-start.1
  12.4 4.0 %collective-permute-done.refs_0_ = f32[2,8,512]{2,1,0:T(8,128)S(1)} collective-permute-done((f32[2,8,512]{2,1,0:T(8,128)S(1)}, f32[2,8,512]{2,1,0:T(8,128)S(1)}, u32[]{:S(2)}, u32[]{:S(2)}) %collective-permute-start) | collective-permute-done | bytes 32800 | tf_op jit(solution)/shard_map/ppermute | solution.py:314
  16.4 0.6 %collective-permute-start.5 = (f32[2,2,8,512]{3,2,1,0:T(8,128)S(1)}, f32[2,2,8,512]{3,2,1,0:T(8,128)S(1)}, u32[]{:S(2)}, u32[]{:S(2)}) collective-permute-start(f32[2,2,8,512]{3,2,1,0:T(8,128)S(1)} %get-tuple-element.40), channel_id=1, source_target_pairs={{0,2},{1,3},{2,4},{3,5},{4,6},{5,7},{6,0},{7,1},{16,18},{17,19},{1... | collective-permute-start | bytes 196616 | tf_op jit(solution)/shard_map/ppermute | solution.py:314
  17.0 0.0 collective-permute-done.1.refs_1_
  17.0 4.4 %collective-permute-start.6 = (f32[2,2,8,512]{3,2,1,0:T(8,128)S(1)}, f32[2,2,8,512]{3,2,1,0:T(8,128)S(1)}, u32[]{:S(2)}, u32[]{:S(2)}) collective-permute-start(f32[2,2,8,512]{3,2,1,0:T(8,128)S(1)} %get-tuple-element.41), channel_id=1, source_target_pairs={{0,22},{1,23},{2,16},{3,17},{4,18},{5,19},{6,20},{7,21},{16,6},{17... | collective-permute-start | bytes 196616 | tf_op jit(solution)/shard_map/ppermute | solution.py:314
  21.4 0.0 collective-permute-done.3.refs_2_
  21.4 0.0 collective-permute-start.7
  21.4 0.0 collective-permute-done.4.refs_3_
  21.4 1.9 %collective-permute-start.10 = (f32[2,2,8,512]{3,2,1,0:T(8,128)S(1)}, f32[2,2,8,512]{3,2,1,0:T(8,128)S(1)}, u32[]{:S(2)}, u32[]{:S(2)}) collective-permute-start(f32[2,2,8,512]{3,2,1,0:T(8,128)S(1)} %get-tuple-element.47), channel_id=1, source_target_pairs={{0,4},{1,5},{2,6},{3,7},{4,0},{5,1},{6,2},{7,3},{16,20},{17,21},{1... | collective-permute-start | bytes 196616 | tf_op jit(solution)/shard_map/ppermute | solution.py:314
  23.3 0.0 collective-permute-done.5.refs_4_
  23.3 0.8 %collective-permute-start.11 = (f32[2,2,8,512]{3,2,1,0:T(8,128)S(1)}, f32[2,2,8,512]{3,2,1,0:T(8,128)S(1)}, u32[]{:S(2)}, u32[]{:S(2)}) collective-permute-start(f32[2,2,8,512]{3,2,1,0:T(8,128)S(1)} %get-tuple-element.48), channel_id=1, source_target_pairs={{0,20},{1,21},{2,22},{3,23},{4,16},{5,17},{6,18},{7,19},{16,4},{17... | collective-permute-start | bytes 196616 | tf_op jit(solution)/shard_map/ppermute | solution.py:314
  24.2 0.0 collective-permute-done.6.refs_5_
  24.2 4.9 %collective-permute-start.12 = (f32[2,2,8,512]{3,2,1,0:T(8,128)S(1)}, f32[2,2,8,512]{3,2,1,0:T(8,128)S(1)}, u32[]{:S(2)}, u32[]{:S(2)}) collective-permute-start(f32[2,2,8,512]{3,2,1,0:T(8,128)S(1)} %get-tuple-element.49), channel_id=1, source_target_pairs={{0,6},{1,7},{2,0},{3,1},{4,2},{5,3},{6,4},{7,5},{16,22},{17,23},{1... | collective-permute-start | bytes 196616 | tf_op jit(solution)/shard_map/ppermute | solution.py:314
  29.1 0.0 collective-permute-done.7.refs_6_
  29.1 0.0 collective-permute-start.13
  29.1 1.3 %collective-permute-done.10.refs_2_ = f32[2,2,8,512]{3,2,1,0:T(8,128)S(1)} collective-permute-done((f32[2,2,8,512]{3,2,1,0:T(8,128)S(1)}, f32[2,2,8,512]{3,2,1,0:T(8,128)S(1)}, u32[]{:S(2)}, u32[]{:S(2)}) %collective-permute-start.10) | collective-permute-done | bytes 65568 | tf_op jit(solution)/shard_map/ppermute | solution.py:314
  30.4 3.1 %collective-permute-start.14 = (f32[2,2,8,512]{3,2,1,0:T(8,128)S(1)}, f32[2,2,8,512]{3,2,1,0:T(8,128)S(1)}, u32[]{:S(2)}, u32[]{:S(2)}) collective-permute-start(f32[2,2,8,512]{3,2,1,0:T(8,128)S(1)} %get-tuple-element.51), channel_id=1, source_target_pairs={{0,22},{1,23},{2,16},{3,17},{4,18},{5,19},{6,20},{7,21},{16,6},{17... | collective-permute-start | bytes 196616 | tf_op jit(solution)/shard_map/ppermute | solution.py:314
  33.5 0.0 collective-permute-done.8.refs_7_.refs_0_
  33.5 0.0 collective-permute-start.15
  33.5 0.0 copy-done
  33.5 0.0 copy-done.1
  33.5 0.0 copy-done.2
  33.5 1.1 %shard_map.66 = (f32[4,2,8,512]{3,2,1,0:T(8,128)S(1)}, f32[4,2,8,512]{3,2,1,0:T(8,128)S(1)}) custom-call(f32[2,8,512]{2,1,0:T(8,128)S(1)} %collective-permute-done.refs_0_, f32[2,8,512]{2,1,0:T(8,128)S(1)} %collective-permute-done.1.refs_1_, f32[2,2,8,512]{3,2,1,0:T(8,128)S(1)} %collective-permute-done.3.refs_2_, ...), custom_call_target="tpu_custom_call" | custom-call | flops 301989888 | bytes 4194304 | tf_op jit(solution)/shard_map/pallas_call | solution.py:362
  34.6 0.0 collective-permute-done.11.refs_3_
  34.7 0.1 collective-permute-start.9
  34.7 0.0 collective-permute-done.12.refs_4_
  34.7 0.5 collective-permute-done.13.refs_5_
  35.2 0.7 %collective-permute-done.14.refs_6_ = f32[2,2,8,512]{3,2,1,0:T(8,128)S(1)} collective-permute-done((f32[2,2,8,512]{3,2,1,0:T(8,128)S(1)}, f32[2,2,8,512]{3,2,1,0:T(8,128)S(1)}, u32[]{:S(2)}, u32[]{:S(2)}) %collective-permute-start.14) | collective-permute-done | bytes 65568 | tf_op jit(solution)/shard_map/ppermute | solution.py:314
  35.9 4.5 %collective-permute-done.15.refs_7_ = f32[2,2,8,512]{3,2,1,0:T(8,128)S(1)} collective-permute-done((f32[2,2,8,512]{3,2,1,0:T(8,128)S(1)}, f32[2,2,8,512]{3,2,1,0:T(8,128)S(1)}, u32[]{:S(2)}, u32[]{:S(2)}) %collective-permute-start.15) | collective-permute-done | bytes 65568 | tf_op jit(solution)/shard_map/ppermute | solution.py:314
  40.4 1.1 %shard_map.67 = (f32[3,2,8,512]{3,2,1,0:T(8,128)S(1)}, f32[3,2,8,512]{3,2,1,0:T(8,128)S(1)}, f32[2,8,512]{2,1,0:T(8,128)S(1)}, f32[2,8,512]{2,1,0:T(8,128)S(1)}) custom-call(f32[4,2,8,512]{3,2,1,0:T(8,128)S(1)} %collective-permute-done.8.refs_7_.refs_0_, f32[4,2,8,512]{3,2,1,0:T(8,128)S(1)} %get-tuple-element.44.refs_8_.refs_1_, ...), custom_call_target="tpu_custom_call" | custom-call | flops 301989888 | bytes 4194304 | tf_op jit(solution)/shard_map/pallas_call | solution.py:362
  41.6 0.1 collective-permute-start.16
  41.7 0.1 collective-permute-start.22
  41.7 0.1 collective-permute-start.23
  41.8 0.0 collective-permute-done.9.refs_1_
  41.8 0.4 collective-permute-start.19
  42.2 4.0 %collective-permute-start.20 = (f32[2,2,8,512]{3,2,1,0:T(8,128)S(1)}, f32[2,2,8,512]{3,2,1,0:T(8,128)S(1)}, u32[]{:S(2)}, u32[]{:S(2)}) collective-permute-start(f32[2,2,8,512]{3,2,1,0:T(8,128)S(1)} %get-tuple-element.58), channel_id=1, source_target_pairs={{0,4},{1,5},{2,6},{3,7},{4,0},{5,1},{6,2},{7,3},{16,20},{17,21},{1... | collective-permute-start | bytes 196616 | tf_op jit(solution)/shard_map/ppermute | solution.py:314
  46.2 0.0 collective-permute-done.16.refs_3_
  46.2 2.6 %collective-permute-start.21 = (f32[2,2,8,512]{3,2,1,0:T(8,128)S(1)}, f32[2,2,8,512]{3,2,1,0:T(8,128)S(1)}, u32[]{:S(2)}, u32[]{:S(2)}) collective-permute-start(f32[2,2,8,512]{3,2,1,0:T(8,128)S(1)} %get-tuple-element.59), channel_id=1, source_target_pairs={{0,6},{1,7},{2,0},{3,1},{4,2},{5,3},{6,4},{7,5},{16,22},{17,23},{1... | collective-permute-start | bytes 196616 | tf_op jit(solution)/shard_map/ppermute | solution.py:314
  48.9 0.0 collective-permute-done.22.refs_3_
  48.9 0.1 collective-permute-start.17
  49.0 0.0 collective-permute-done.23.refs_4_
  49.0 1.7 %collective-permute-start.18 = (f32[2,2,8,512]{3,2,1,0:T(8,128)S(1)}, f32[2,2,8,512]{3,2,1,0:T(8,128)S(1)}, u32[]{:S(2)}, u32[]{:S(2)}) collective-permute-start(f32[2,2,8,512]{3,2,1,0:T(8,128)S(1)} %get-tuple-element.56), channel_id=1, source_target_pairs={{0,6},{1,7},{2,0},{3,1},{4,2},{5,3},{6,4},{7,5},{16,22},{17,23},{1... | collective-permute-start | bytes 196616 | tf_op jit(solution)/shard_map/ppermute | solution.py:314
  50.7 0.0 collective-permute-done.19.refs_0_
  50.7 2.2 %collective-permute-done.20.refs_1_ = f32[2,2,8,512]{3,2,1,0:T(8,128)S(1)} collective-permute-done((f32[2,2,8,512]{3,2,1,0:T(8,128)S(1)}, f32[2,2,8,512]{3,2,1,0:T(8,128)S(1)}, u32[]{:S(2)}, u32[]{:S(2)}) %collective-permute-start.20) | collective-permute-done | bytes 65568 | tf_op jit(solution)/shard_map/ppermute | solution.py:314
  52.9 0.0 collective-permute-done.21.refs_2_
  52.9 0.8 %shard_map.70.refs_2_ = f32[2,8,2,8,512]{4,3,2,1,0:T(8,128)} custom-call(f32[2,2,8,512]{3,2,1,0:T(8,128)S(1)} %collective-permute-done.19.refs_0_, f32[2,2,8,512]{3,2,1,0:T(8,128)S(1)} %collective-permute-done.20.refs_1_, f32[2,2,8,512]{3,2,1,0:T(8,128)S(1)} %collective-permute-done.21.refs_2_, f32[2,8,512]{2,1,0:T(8,128)S(1)} %collective-permute-done.22.refs_3_, ...), custom_call_target="tpu_custom_call" | custom-call | tf_op jit(solution)/shard_map/pallas_call | solution.py:410
  53.8 2.7 %collective-permute-done.17.refs_0_ = f32[2,2,8,512]{3,2,1,0:T(8,128)S(1)} collective-permute-done((f32[2,2,8,512]{3,2,1,0:T(8,128)S(1)}, f32[2,2,8,512]{3,2,1,0:T(8,128)S(1)}, u32[]{:S(2)}, u32[]{:S(2)}) %collective-permute-start.17) | collective-permute-done | bytes 65568 | tf_op jit(solution)/shard_map/ppermute | solution.py:314
  56.4 0.0 collective-permute-done.18.refs_1_
  56.4 0.7 %shard_map.71 = f32[2,8,2,8,512]{4,3,2,1,0:T(8,128)} custom-call(f32[2,2,8,512]{3,2,1,0:T(8,128)S(1)} %collective-permute-done.17.refs_0_, f32[2,2,8,512]{3,2,1,0:T(8,128)S(1)} %collective-permute-done.18.refs_1_, f32[2,8,2,8,512]{4,3,2,1,0:T(8,128)} %shard_map.70.refs_2_), custom_call_target="tpu_custom_call", output_to_operand_aliasing={{}: (2, {})} | custom-call | tf_op jit(solution)/shard_map/pallas_call | solution.py:410
  (2 shorter events, 0.0 us)
Async XLA Ops:
  1.8 2.0 %collective-permute-start.2 = (f32[15,2,8,512]{3,2,1,0:T(8,128)S(1)}, f32[15,2,8,512]{3,2,1,0:T(8,128)S(1)}, u32[]{:S(2)}, u32[]{:S(2)}) collective-permute-start(f32[15,2,8,512]{3,2,1,0:T(8,128)S(1)} %get-tuple-element.37), channel_id=1, source_target_pairs={{0,1},{1,0},{2,3},{3,2},{4,5},{5,4},{6,7},{7,6},{8,9},{9,8},{10,11... | collective-permute-start | bytes 1474568 | tf_op jit(solution)/shard_map/ppermute | solution.py:295
  3.8 29.7 %copy-start = (bf16[2,256,256]{2,1,0:T(8,128)(2,1)S(1)}, bf16[2,256,256]{2,1,0:T(8,128)(2,1)}, u32[]{:S(2)}) copy-start(bf16[2,256,256]{2,1,0:T(8,128)(2,1)} %constant.7.clone.refs_10_.refs_9_) | copy-start | bytes 786436
  3.8 29.7 %copy-start.1 = (bf16[2,256,256]{2,1,0:T(8,128)(2,1)S(1)}, bf16[2,256,256]{2,1,0:T(8,128)(2,1)}, u32[]{:S(2)}) copy-start(bf16[2,256,256]{2,1,0:T(8,128)(2,1)} %constant.6.clone.refs_9_.refs_8_) | copy-start | bytes 786436
  3.8 29.7 %copy-start.2 = (f32[2,32,128]{2,1,0:T(8,128)S(1)}, f32[2,32,128]{2,1,0:T(8,128)}, u32[]{:S(2)}) copy-start(f32[2,32,128]{2,1,0:T(8,128)} %constant.8.clone.refs_11_.refs_10_) | copy-start | bytes 98308
  3.9 17.5 %collective-permute-start.3 = (f32[2,2,8,512]{3,2,1,0:T(8,128)S(1)}, f32[2,2,8,512]{3,2,1,0:T(8,128)S(1)}, u32[]{:S(2)}, u32[]{:S(2)}) collective-permute-start(f32[2,2,8,512]{3,2,1,0:T(8,128)S(1)} %get-tuple-element.38), channel_id=1, source_target_pairs={{0,20},{1,21},{2,22},{3,23},{4,16},{5,17},{6,18},{7,19},{16,4},{17... | collective-permute-start | bytes 196616 | tf_op jit(solution)/shard_map/ppermute | solution.py:314
  8.9 12.6 %collective-permute-start.4 = (f32[2,2,8,512]{3,2,1,0:T(8,128)S(1)}, f32[2,2,8,512]{3,2,1,0:T(8,128)S(1)}, u32[]{:S(2)}, u32[]{:S(2)}) collective-permute-start(f32[2,2,8,512]{3,2,1,0:T(8,128)S(1)} %get-tuple-element.39), channel_id=1, source_target_pairs={{0,6},{1,7},{2,0},{3,1},{4,2},{5,3},{6,4},{7,5},{16,22},{17,23},{1... | collective-permute-start | bytes 196616 | tf_op jit(solution)/shard_map/ppermute | solution.py:314
  10.2 23.3 %collective-permute-start.8 = (f32[4,2,8,512]{3,2,1,0:T(8,128)S(1)}, f32[4,2,8,512]{3,2,1,0:T(8,128)S(1)}, u32[]{:S(2)}, u32[]{:S(2)}) collective-permute-start(f32[4,2,8,512]{3,2,1,0:T(8,128)S(1)} %get-tuple-element.43), channel_id=1, source_target_pairs={{0,16},{1,17},{2,18},{3,19},{4,20},{5,21},{6,22},{7,23},{16,0},{17... | collective-permute-start | bytes 393224 | tf_op jit(solution)/shard_map/ppermute | solution.py:314
  10.7 5.7 %collective-permute-start = (f32[2,8,512]{2,1,0:T(8,128)S(1)}, f32[2,8,512]{2,1,0:T(8,128)S(1)}, u32[]{:S(2)}, u32[]{:S(2)}) collective-permute-start(f32[2,8,512]{2,1,0:T(8,128)S(1)} %get-tuple-element.34), channel_id=1, source_target_pairs={{0,4},{1,5},{2,6},{3,7},{4,0},{5,1},{6,2},{7,3},{16,20},{17,21},{1... | collective-permute-start | bytes 98312 | tf_op jit(solution)/shard_map/ppermute | solution.py:314
  12.4 4.6 %collective-permute-start.1 = (f32[2,8,512]{2,1,0:T(8,128)S(1)}, f32[2,8,512]{2,1,0:T(8,128)S(1)}, u32[]{:S(2)}, u32[]{:S(2)}) collective-permute-start(f32[2,8,512]{2,1,0:T(8,128)S(1)} %get-tuple-element.35), channel_id=1, source_target_pairs={{0,5},{1,4},{2,7},{3,6},{4,1},{5,0},{6,3},{7,2},{16,21},{17,20},{1... | collective-permute-start | bytes 98312 | tf_op jit(solution)/shard_map/ppermute | solution.py:314
  16.4 6.9 %collective-permute-start.5 = (f32[2,2,8,512]{3,2,1,0:T(8,128)S(1)}, f32[2,2,8,512]{3,2,1,0:T(8,128)S(1)}, u32[]{:S(2)}, u32[]{:S(2)}) collective-permute-start(f32[2,2,8,512]{3,2,1,0:T(8,128)S(1)} %get-tuple-element.40), channel_id=1, source_target_pairs={{0,2},{1,3},{2,4},{3,5},{4,6},{5,7},{6,0},{7,1},{16,18},{17,19},{1... | collective-permute-start | bytes 196616 | tf_op jit(solution)/shard_map/ppermute | solution.py:314
  17.0 7.2 %collective-permute-start.6 = (f32[2,2,8,512]{3,2,1,0:T(8,128)S(1)}, f32[2,2,8,512]{3,2,1,0:T(8,128)S(1)}, u32[]{:S(2)}, u32[]{:S(2)}) collective-permute-start(f32[2,2,8,512]{3,2,1,0:T(8,128)S(1)} %get-tuple-element.41), channel_id=1, source_target_pairs={{0,22},{1,23},{2,16},{3,17},{4,18},{5,19},{6,20},{7,21},{16,6},{17... | collective-permute-start | bytes 196616 | tf_op jit(solution)/shard_map/ppermute | solution.py:314
  21.4 7.7 %collective-permute-start.7 = (f32[2,2,8,512]{3,2,1,0:T(8,128)S(1)}, f32[2,2,8,512]{3,2,1,0:T(8,128)S(1)}, u32[]{:S(2)}, u32[]{:S(2)}) collective-permute-start(f32[2,2,8,512]{3,2,1,0:T(8,128)S(1)} %get-tuple-element.42), channel_id=1, source_target_pairs={{0,18},{1,19},{2,20},{3,21},{4,22},{5,23},{6,16},{7,17},{16,2},{17... | collective-permute-start | bytes 196616 | tf_op jit(solution)/shard_map/ppermute | solution.py:314
  21.4 9.0 %collective-permute-start.10 = (f32[2,2,8,512]{3,2,1,0:T(8,128)S(1)}, f32[2,2,8,512]{3,2,1,0:T(8,128)S(1)}, u32[]{:S(2)}, u32[]{:S(2)}) collective-permute-start(f32[2,2,8,512]{3,2,1,0:T(8,128)S(1)} %get-tuple-element.47), channel_id=1, source_target_pairs={{0,4},{1,5},{2,6},{3,7},{4,0},{5,1},{6,2},{7,3},{16,20},{17,21},{1... | collective-permute-start | bytes 196616 | tf_op jit(solution)/shard_map/ppermute | solution.py:314
  23.3 11.3 %collective-permute-start.11 = (f32[2,2,8,512]{3,2,1,0:T(8,128)S(1)}, f32[2,2,8,512]{3,2,1,0:T(8,128)S(1)}, u32[]{:S(2)}, u32[]{:S(2)}) collective-permute-start(f32[2,2,8,512]{3,2,1,0:T(8,128)S(1)} %get-tuple-element.48), channel_id=1, source_target_pairs={{0,20},{1,21},{2,22},{3,23},{4,16},{5,17},{6,18},{7,19},{16,4},{17... | collective-permute-start | bytes 196616 | tf_op jit(solution)/shard_map/ppermute | solution.py:314
  24.2 10.6 %collective-permute-start.12 = (f32[2,2,8,512]{3,2,1,0:T(8,128)S(1)}, f32[2,2,8,512]{3,2,1,0:T(8,128)S(1)}, u32[]{:S(2)}, u32[]{:S(2)}) collective-permute-start(f32[2,2,8,512]{3,2,1,0:T(8,128)S(1)} %get-tuple-element.49), channel_id=1, source_target_pairs={{0,6},{1,7},{2,0},{3,1},{4,2},{5,3},{6,4},{7,5},{16,22},{17,23},{1... | collective-permute-start | bytes 196616 | tf_op jit(solution)/shard_map/ppermute | solution.py:314
  29.1 6.2 %collective-permute-start.13 = (f32[2,2,8,512]{3,2,1,0:T(8,128)S(1)}, f32[2,2,8,512]{3,2,1,0:T(8,128)S(1)}, u32[]{:S(2)}, u32[]{:S(2)}) collective-permute-start(f32[2,2,8,512]{3,2,1,0:T(8,128)S(1)} %get-tuple-element.50), channel_id=1, source_target_pairs={{0,2},{1,3},{2,4},{3,5},{4,6},{5,7},{6,0},{7,1},{16,18},{17,19},{1... | collective-permute-start | bytes 196616 | tf_op jit(solution)/shard_map/ppermute | solution.py:314
  30.4 5.5 %collective-permute-start.14 = (f32[2,2,8,512]{3,2,1,0:T(8,128)S(1)}, f32[2,2,8,512]{3,2,1,0:T(8,128)S(1)}, u32[]{:S(2)}, u32[]{:S(2)}) collective-permute-start(f32[2,2,8,512]{3,2,1,0:T(8,128)S(1)} %get-tuple-element.51), channel_id=1, source_target_pairs={{0,22},{1,23},{2,16},{3,17},{4,18},{5,19},{6,20},{7,21},{16,6},{17... | collective-permute-start | bytes 196616 | tf_op jit(solution)/shard_map/ppermute | solution.py:314
  33.5 7.0 %collective-permute-start.15 = (f32[2,2,8,512]{3,2,1,0:T(8,128)S(1)}, f32[2,2,8,512]{3,2,1,0:T(8,128)S(1)}, u32[]{:S(2)}, u32[]{:S(2)}) collective-permute-start(f32[2,2,8,512]{3,2,1,0:T(8,128)S(1)} %get-tuple-element.52), channel_id=1, source_target_pairs={{0,18},{1,19},{2,20},{3,21},{4,22},{5,23},{6,16},{7,17},{16,2},{17... | collective-permute-start | bytes 196616 | tf_op jit(solution)/shard_map/ppermute | solution.py:314
  34.7 7.1 %collective-permute-start.9 = (f32[4,2,8,512]{3,2,1,0:T(8,128)S(1)}, f32[4,2,8,512]{3,2,1,0:T(8,128)S(1)}, u32[]{:S(2)}, u32[]{:S(2)}) collective-permute-start(f32[4,2,8,512]{3,2,1,0:T(8,128)S(1)} %get-tuple-element.46), channel_id=1, source_target_pairs={{0,1},{1,0},{2,3},{3,2},{4,5},{5,4},{6,7},{7,6},{8,9},{9,8},{10,11... | collective-permute-start | bytes 393224 | tf_op jit(solution)/shard_map/ppermute | solution.py:295
  41.6 4.6 %collective-permute-start.16 = (f32[3,2,8,512]{3,2,1,0:T(8,128)S(1)}, f32[3,2,8,512]{3,2,1,0:T(8,128)S(1)}, u32[]{:S(2)}, u32[]{:S(2)}) collective-permute-start(f32[3,2,8,512]{3,2,1,0:T(8,128)S(1)} %get-tuple-element.54), channel_id=1, source_target_pairs={{0,1},{1,0},{2,3},{3,2},{4,5},{5,4},{6,7},{7,6},{8,9},{9,8},{10,11... | collective-permute-start | bytes 294920 | tf_op jit(solution)/shard_map/ppermute | solution.py:295
  41.7 7.2 %collective-permute-start.22 = (f32[2,8,512]{2,1,0:T(8,128)S(1)}, f32[2,8,512]{2,1,0:T(8,128)S(1)}, u32[]{:S(2)}, u32[]{:S(2)}) collective-permute-start(f32[2,8,512]{2,1,0:T(8,128)S(1)} %get-tuple-element.60), channel_id=1, source_target_pairs={{0,2},{1,3},{2,4},{3,5},{4,6},{5,7},{6,0},{7,1},{16,18},{17,19},{1... | collective-permute-start | bytes 98312 | tf_op jit(solution)/shard_map/ppermute | solution.py:314
  41.7 7.3 %collective-permute-start.23 = (f32[2,8,512]{2,1,0:T(8,128)S(1)}, f32[2,8,512]{2,1,0:T(8,128)S(1)}, u32[]{:S(2)}, u32[]{:S(2)}) collective-permute-start(f32[2,8,512]{2,1,0:T(8,128)S(1)} %get-tuple-element.61), channel_id=1, source_target_pairs={{0,3},{1,2},{2,5},{3,4},{4,7},{5,6},{6,1},{7,0},{16,19},{17,18},{1... | collective-permute-start | bytes 98312 | tf_op jit(solution)/shard_map/ppermute | solution.py:314
  41.8 8.9 %collective-permute-start.19 = (f32[2,2,8,512]{3,2,1,0:T(8,128)S(1)}, f32[2,2,8,512]{3,2,1,0:T(8,128)S(1)}, u32[]{:S(2)}, u32[]{:S(2)}) collective-permute-start(f32[2,2,8,512]{3,2,1,0:T(8,128)S(1)} %get-tuple-element.57), channel_id=1, source_target_pairs={{0,2},{1,3},{2,4},{3,5},{4,6},{5,7},{6,0},{7,1},{16,18},{17,19},{1... | collective-permute-start | bytes 196616 | tf_op jit(solution)/shard_map/ppermute | solution.py:314
  42.2 10.7 %collective-permute-start.20 = (f32[2,2,8,512]{3,2,1,0:T(8,128)S(1)}, f32[2,2,8,512]{3,2,1,0:T(8,128)S(1)}, u32[]{:S(2)}, u32[]{:S(2)}) collective-permute-start(f32[2,2,8,512]{3,2,1,0:T(8,128)S(1)} %get-tuple-element.58), channel_id=1, source_target_pairs={{0,4},{1,5},{2,6},{3,7},{4,0},{5,1},{6,2},{7,3},{16,20},{17,21},{1... | collective-permute-start | bytes 196616 | tf_op jit(solution)/shard_map/ppermute | solution.py:314
  46.2 6.7 %collective-permute-start.21 = (f32[2,2,8,512]{3,2,1,0:T(8,128)S(1)}, f32[2,2,8,512]{3,2,1,0:T(8,128)S(1)}, u32[]{:S(2)}, u32[]{:S(2)}) collective-permute-start(f32[2,2,8,512]{3,2,1,0:T(8,128)S(1)} %get-tuple-element.59), channel_id=1, source_target_pairs={{0,6},{1,7},{2,0},{3,1},{4,2},{5,3},{6,4},{7,5},{16,22},{17,23},{1... | collective-permute-start | bytes 196616 | tf_op jit(solution)/shard_map/ppermute | solution.py:314
  48.9 7.5 %collective-permute-start.17 = (f32[2,2,8,512]{3,2,1,0:T(8,128)S(1)}, f32[2,2,8,512]{3,2,1,0:T(8,128)S(1)}, u32[]{:S(2)}, u32[]{:S(2)}) collective-permute-start(f32[2,2,8,512]{3,2,1,0:T(8,128)S(1)} %get-tuple-element.55), channel_id=1, source_target_pairs={{0,4},{1,5},{2,6},{3,7},{4,0},{5,1},{6,2},{7,3},{16,20},{17,21},{1... | collective-permute-start | bytes 196616 | tf_op jit(solution)/shard_map/ppermute | solution.py:314
  49.0 7.4 %collective-permute-start.18 = (f32[2,2,8,512]{3,2,1,0:T(8,128)S(1)}, f32[2,2,8,512]{3,2,1,0:T(8,128)S(1)}, u32[]{:S(2)}, u32[]{:S(2)}) collective-permute-start(f32[2,2,8,512]{3,2,1,0:T(8,128)S(1)} %get-tuple-element.56), channel_id=1, source_target_pairs={{0,6},{1,7},{2,0},{3,1},{4,2},{5,3},{6,4},{7,5},{16,22},{17,23},{1... | collective-permute-start | bytes 196616 | tf_op jit(solution)/shard_map/ppermute | solution.py:314
